TPU v7x, 32 devices: a whole 2x2x4 slice. The times are simulated.
32 devices in a mesh: head: 4 (over z), blk: 8 (over y, x, core).
Axes of the slice: x: 2, y: 2, z: 4, core: 2. Of those that a mesh axis runs over, the one named last changes fastest.
Arguments:
- tokens: bfloat16 [4096, 1024], P(('blk', 'head')), may hold values from -6 to 6
- segments: int32 [4096], replicated, may hold values from 0 to 8, as said below
- routes: int32 [4096, 8], P(('blk', 'head')), may hold values from 0 to 31, all different within a row; in each aligned block of 128 rows (0 to 127, 128 to 255, ...) at most 40 rows name the same one
- w_query: bfloat16 [2, 1024, 1024], P(None, ('head', 'blk')), may hold values from -0.1875 to 0.1875
- w_key: bfloat16 [2, 1024, 512], P(None, ('head', 'blk')), may hold values from -0.25 to 0.25
- w_value: bfloat16 [2, 1024, 512], P(None, ('head', 'blk')), may hold values from -0.1875 to 0.1875
- w_out: bfloat16 [2, 1024, 1024], P(None, ('head', 'blk')), may hold values from -0.375 to 0.375
- w_router: bfloat16 [2, 1024, 32], P(None, ('head', 'blk')), may hold values from -0.25 to 0.25
- gain_attn: bfloat16 [2, 1024], P(None, ('head', 'blk')), may hold values from 0.5 to 1.5
- gain_ffn: bfloat16 [2, 1024], P(None, ('head', 'blk')), may hold values from 0.5 to 1.5
- w_gate: bfloat16 [2, 32, 1024, 512], P(None, 'head', 'blk'), may hold values from -0.1875 to 0.1875
- w_up: bfloat16 [2, 32, 1024, 512], P(None, 'head', 'blk'), may hold values from -0.1875 to 0.1875
- w_down: bfloat16 [2, 32, 1024, 512], P(None, 'head', 'blk'), may hold values from -0.5 to 0.5
- cotangent: bfloat16 [4096, 1024], P(('blk', 'head')), may hold values from -6 to 6
Outputs:
- layers_out: float32 [4096, 1024], P(('blk', 'head'))
- grad_tokens: float32 [4096, 1024], P(('blk', 'head'))
- grad_query: float32 [2, 1024, 1024], P(None, ('head', 'blk'))
- grad_key: float32 [2, 1024, 512], P(None, ('head', 'blk'))
- grad_value: float32 [2, 1024, 512], P(None, ('head', 'blk'))
- grad_out: float32 [2, 1024, 1024], P(None, ('head', 'blk'))
- grad_router: float32 [2, 1024, 32], P(None, ('head', 'blk'))
- grad_gain_attn: float32 [2, 1024], P(None, ('head', 'blk'))
- grad_gain_ffn: float32 [2, 1024], P(None, ('head', 'blk'))
- grad_gate: float32 [2, 32, 1024, 512], P(None, 'head', 'blk')
- grad_up: float32 [2, 32, 1024, 512], P(None, 'head', 'blk')
- grad_down: float32 [2, 32, 1024, 512], P(None, 'head', 'blk')
Inputs may be any that keep to these rules, and one draw needn't show every extreme that they name: `segments`: documents are contiguous and lie inside the sequences of 4096 tokens: segment numbers never fall along the stream and no document crosses a multiple of 4096. In every sequence the longest document has exactly 2560 tokens. `routes`: each token names 8 different experts. Within the rows of one device no expert is named more than 40 times, and that many is reached.
All inputs are finite; a program needn't handle non-finite values.
Results may differ from a plain program's by a relative error of at most 0.04.
Values may be sent and summed in bfloat16 or wider, within the bound.
No kernel may reach another device: no remote copies, remote signals or barrier semaphores. Data moves between devices by JAX's collectives and lax.ppermute only.
A program may use at most 256 MiB of HBM per device.

v0:
```python
import jax
import jax.numpy as jnp
from jax import lax
from jax.sharding import PartitionSpec as P

D = 1024
H = 16
KVH = 8
HD = 64
E = 32
TOPK = 8
LAYERS = 2
CAP = 40


EPSILON = 1e-06
MASKED = -1e30
ROPE_BASE = 10000.0
PRECISE = lax.Precision.HIGHEST


def from_behind(value, axis, by):
    count = lax.axis_size(axis)
    return lax.ppermute(value, axis, [(i, (i + by) % count) for i in range(count)])


def rms_scale(values):
    return lax.rsqrt(jnp.mean(values * values, axis=-1, keepdims=True) + EPSILON)


def rotate(values, cosine_table, sine_table):
    half_dim = values.shape[-1] // 2
    first = values[..., :half_dim]
    second = values[..., half_dim:]
    return jnp.concatenate(
        [first * cosine_table - second * sine_table, second * cosine_table + first * sine_table],
        axis=-1,
    )


def rotary_tables(start, count, head_dim):
    half_dim = head_dim // 2
    frequency = jnp.power(ROPE_BASE, -(jnp.arange(half_dim, dtype=jnp.float32) * 2.0 / head_dim))
    places = start + jnp.arange(count, dtype=jnp.int32)
    angles = places.astype(jnp.float32)[:, None] * frequency[None, :]
    return (jnp.cos(angles)[:, None, :], jnp.sin(angles)[:, None, :])


def contract_rows(left, right):
    return lax.dot_general(
        left, right, (((0,), (0,)), ((), ())), preferred_element_type=jnp.float32
    )


def contract_cols(left, right):
    return lax.dot_general(
        left, right, (((1,), (1,)), ((), ())), preferred_element_type=jnp.float32
    )


def norm_back(stream, scale, gain, grad_normed):
    inner = grad_normed * gain
    grad_gain = jnp.sum(grad_normed * stream * scale, axis=0)
    grad_stream = scale * inner - stream * scale * scale * scale * jnp.mean(
        stream * inner, axis=-1, keepdims=True
    )
    return (grad_stream, grad_gain)


def per_device(
    tokens,
    segments,
    routes,
    w_query,
    w_key,
    w_value,
    w_out,
    w_router,
    gain_attn,
    gain_ffn,
    w_gate,
    w_up,
    w_down,
    cotangent,
):
    head_count = lax.axis_size("head")
    cycle_count = lax.axis_size("blk")
    cycle_index = lax.axis_index("blk")
    head_index = lax.axis_index("head")
    local_tokens = tokens.shape[0]
    block_rows = local_tokens * head_count
    token_start = (cycle_index * head_count + head_index) * local_tokens
    query_start = cycle_index * block_rows
    groups = H // KVH
    key_heads = KVH // head_count
    local_experts = E // head_count
    score_scale = HD ** (-0.5)
    cosine_table, sine_table = rotary_tables(token_start, local_tokens, HD)
    flat_route = routes.reshape(-1)
    route_hot = (flat_route[:, None] == jnp.arange(E, dtype=jnp.int32)[None, :]).astype(jnp.int32)
    slot_index = jnp.sum(route_hot * (jnp.cumsum(route_hot, axis=0) - 1), axis=1)
    buffer_row = flat_route * CAP + slot_index
    onehot = route_hot.reshape(local_tokens, TOPK, E).astype(jnp.float32)
    query_segs = lax.dynamic_slice_in_dim(segments, query_start, block_rows)
    query_pos = query_start + jnp.arange(block_rows, dtype=jnp.int32)

    def gather_attn(layer_index):
        return (
            lax.all_gather(w_query[layer_index], ("head", "blk"), axis=0, tiled=True),
            lax.all_gather(w_key[layer_index], ("head", "blk"), axis=0, tiled=True),
            lax.all_gather(w_value[layer_index], ("head", "blk"), axis=0, tiled=True),
            lax.all_gather(w_out[layer_index], ("head", "blk"), axis=0, tiled=True),
            lax.all_gather(w_router[layer_index], ("head", "blk"), axis=0, tiled=True),
            lax.all_gather(gain_attn[layer_index], ("head", "blk"), axis=0, tiled=True),
            lax.all_gather(gain_ffn[layer_index], ("head", "blk"), axis=0, tiled=True),
        )

    def gather_experts(layer_index):
        return (
            lax.all_gather(w_gate[layer_index], "blk", axis=1, tiled=True),
            lax.all_gather(w_up[layer_index], "blk", axis=1, tiled=True),
            lax.all_gather(w_down[layer_index], "blk", axis=1, tiled=True),
        )

    def block_mask(key_owner):
        key_start = key_owner * block_rows
        key_segs = lax.dynamic_slice_in_dim(segments, key_start, block_rows)
        key_pos = key_start + jnp.arange(block_rows, dtype=jnp.int32)
        allowed = (query_segs[:, None] == key_segs[None, :]) & (
            query_pos[:, None] >= key_pos[None, :]
        )
        active = (key_owner <= cycle_index) & (key_segs[block_rows - 1] >= query_segs[0])
        return (allowed, active)

    def key_block(keys_all, key_owner):
        chosen_rows = lax.dynamic_slice_in_dim(
            keys_all, key_owner * block_rows, block_rows
        ).reshape(block_rows, key_heads, 2, HD)
        return (chosen_rows[:, :, 0], chosen_rows[:, :, 1])

    def block_scores(query_four, key_part, allowed):
        scores = (
            jnp.einsum("qcgd,kcd->cgqk", query_four, key_part, preferred_element_type=jnp.float32)
            * score_scale
        )
        return jnp.where(allowed, scores, MASKED)

    def attend_back(queries, keys_all, attended, log_total, grad_attended):
        query_four = queries.reshape(block_rows, key_heads, groups, HD)
        grad_four = grad_attended.reshape(block_rows, key_heads, groups, HD)
        row_delta = jnp.transpose(
            jnp.sum(
                grad_four.astype(jnp.float32)
                * attended.reshape(block_rows, key_heads, groups, HD).astype(jnp.float32),
                axis=-1,
            ),
            (1, 2, 0),
        )

        def block_grads(key_owner, allowed, grad_query):
            key_part, value_part = key_block(keys_all, key_owner)
            scores = block_scores(query_four, key_part, allowed)
            probability = jnp.where(allowed, jnp.exp(scores - log_total[..., None]), 0.0)
            grad_value = jnp.einsum(
                "cgqk,qcgd->kcd",
                probability.astype(jnp.bfloat16),
                grad_four,
                preferred_element_type=jnp.float32,
            )
            grad_prob = jnp.einsum(
                "qcgd,kcd->cgqk", grad_four, value_part, preferred_element_type=jnp.float32
            )
            grad_scores = (probability * (grad_prob - row_delta[..., None])).astype(jnp.bfloat16)
            grad_query = grad_query + jnp.einsum(
                "cgqk,kcd->qcgd", grad_scores, key_part, preferred_element_type=jnp.float32
            )
            grad_key = (
                jnp.einsum(
                    "cgqk,qcgd->kcd", grad_scores, query_four, preferred_element_type=jnp.float32
                )
                * score_scale
            )
            stacked = jnp.stack([grad_key, grad_value], axis=2).reshape(
                block_rows, key_heads * 2 * HD
            )
            return (grad_query, stacked)

        query_zero = jnp.zeros((block_rows, key_heads, groups, HD), jnp.float32)

        def visit(step_index, state_now):
            key_owner = (cycle_index - step_index) % cycle_count
            allowed, active = block_mask(key_owner)

            def visit_work(state_in):
                grad_query, key_grads = state_in
                grad_query, stacked = block_grads(key_owner, allowed, grad_query)
                return (grad_query, key_grads + stacked)

            grad_query, key_grads = lax.cond(
                active, visit_work, lambda state_in: state_in, state_now
            )
            key_grads = from_behind(key_grads.astype(jnp.bfloat16), "blk", 1).astype(
                key_grads.dtype
            )
            return (grad_query, key_grads)

        start_state = (query_zero, jnp.zeros((block_rows, key_heads * 2 * HD), jnp.float32))
        grad_query, key_grads = lax.fori_loop(0, cycle_count, visit, start_state)
        return (
            (grad_query * score_scale)
            .astype(jnp.bfloat16)
            .reshape(block_rows, key_heads * groups * HD),
            key_grads.astype(jnp.bfloat16),
        )

    stream = tokens.astype(jnp.float32)
    saved = []
    kept_mats = []
    for layer_index in range(LAYERS):
        attn_mats = gather_attn(layer_index)
        expert_mats = gather_experts(layer_index)
        kept_mats.append((attn_mats, expert_mats))
        scale_first = rms_scale(stream)
        normed_attn = (stream * scale_first * attn_mats[5].astype(jnp.float32)).astype(jnp.bfloat16)
        query_pre = jnp.dot(normed_attn, attn_mats[0], preferred_element_type=jnp.float32).reshape(
            local_tokens, H, HD
        )
        key_pre = jnp.dot(normed_attn, attn_mats[1], preferred_element_type=jnp.float32).reshape(
            local_tokens, KVH, HD
        )
        value_pre = jnp.dot(normed_attn, attn_mats[2], preferred_element_type=jnp.float32).reshape(
            local_tokens, KVH, HD
        )
        query_rot = (
            rotate(query_pre, cosine_table, sine_table)
            .astype(jnp.bfloat16)
            .reshape(local_tokens, H * HD)
        )
        key_rot = rotate(key_pre, cosine_table, sine_table)
        key_value = (
            jnp.stack([key_rot, value_pre], axis=2)
            .astype(jnp.bfloat16)
            .reshape(local_tokens, KVH * 2 * HD)
        )
        queries, key_value_heads = (
            lax.all_to_all(query_rot, "head", split_axis=1, concat_axis=0, tiled=True),
            lax.all_to_all(key_value, "head", split_axis=1, concat_axis=0, tiled=True),
        )
        keys_all = lax.all_gather(key_value_heads, "blk", axis=0, tiled=True)
        attend_query_four = queries.reshape(block_rows, key_heads, groups, HD)

        def attend_visit(key_owner, state_now):
            allowed, active = block_mask(key_owner)

            def attend_work(state_in):
                running_max, running_sum, weighted = state_in
                key_part, value_part = key_block(keys_all, key_owner)
                scores = block_scores(attend_query_four, key_part, allowed)
                new_max = jnp.maximum(running_max, jnp.max(scores, axis=-1))
                exponent = jnp.where(allowed, jnp.exp(scores - new_max[..., None]), 0.0)
                factor = jnp.exp(running_max - new_max)
                running_sum = running_sum * factor + jnp.sum(exponent, axis=-1)
                weighted = weighted * jnp.transpose(factor, (2, 0, 1))[..., None] + jnp.einsum(
                    "cgqk,kcd->qcgd",
                    exponent.astype(jnp.bfloat16),
                    value_part,
                    preferred_element_type=jnp.float32,
                )
                return (new_max, running_sum, weighted)

            return lax.cond(active, attend_work, lambda state_in: state_in, state_now)

        attend_start_state = (
            jnp.full((key_heads, groups, block_rows), MASKED, jnp.float32),
            jnp.zeros((key_heads, groups, block_rows), jnp.float32),
            jnp.zeros((block_rows, key_heads, groups, HD), jnp.float32),
        )
        running_max, running_sum, weighted = lax.fori_loop(
            0, cycle_count, attend_visit, attend_start_state
        )
        attend_attended = (
            (weighted / jnp.transpose(running_sum, (2, 0, 1))[..., None])
            .astype(jnp.bfloat16)
            .reshape(block_rows, key_heads * groups * HD)
        )
        attended = attend_attended
        log_total = running_max + jnp.log(running_sum)
        attended_tok = lax.all_to_all(attended, "head", split_axis=0, concat_axis=1, tiled=True)
        middle = stream + jnp.dot(attended_tok, attn_mats[3], preferred_element_type=jnp.float32)
        scale_second = rms_scale(middle)
        normed_ffn = (middle * scale_second * attn_mats[6].astype(jnp.float32)).astype(jnp.bfloat16)
        logits = jnp.dot(normed_ffn, attn_mats[4], preferred_element_type=jnp.float32)
        chosen = jnp.sum(onehot * logits[:, None, :], axis=-1)
        gate_prob = jax.nn.softmax(chosen, axis=-1)
        outgoing = (
            jnp.zeros((E * CAP, D), jnp.bfloat16)
            .at[buffer_row]
            .set(jnp.repeat(normed_ffn, TOPK, axis=0))
        )
        arrived = lax.all_to_all(outgoing, "head", split_axis=0, concat_axis=0, tiled=True).reshape(
            head_count, local_experts, CAP, D
        )
        gate_pre = jnp.einsum(
            "secd,edf->secf", arrived, expert_mats[0], preferred_element_type=jnp.float32
        )
        up_pre = jnp.einsum(
            "secd,edf->secf", arrived, expert_mats[1], preferred_element_type=jnp.float32
        )
        hidden = (jax.nn.silu(gate_pre) * up_pre).astype(jnp.bfloat16)
        result = jnp.einsum(
            "secf,edf->secd", hidden, expert_mats[2], preferred_element_type=jnp.float32
        ).astype(jnp.bfloat16)
        returned = lax.all_to_all(
            result.reshape(head_count * local_experts * CAP, D),
            "head",
            split_axis=0,
            concat_axis=0,
            tiled=True,
        )
        picked = returned[buffer_row].reshape(local_tokens, TOPK, D)
        saved.append(
            (
                stream,
                scale_first,
                normed_attn,
                queries,
                keys_all,
                attended,
                log_total,
                attended_tok,
                middle,
                scale_second,
                normed_ffn,
                gate_prob,
                picked,
                arrived,
                gate_pre,
                up_pre,
                hidden,
            )
        )
        stream = middle + jnp.sum(gate_prob[..., None] * picked.astype(jnp.float32), axis=1)
    grad_stream = cotangent.astype(jnp.float32)
    layer_grads = [None] * LAYERS
    for layer_index in range(LAYERS - 1, -1, -1):
        (
            stream_in,
            scale_first,
            normed_attn,
            queries,
            keys_all,
            attended,
            log_total,
            attended_tok,
            middle,
            scale_second,
            normed_ffn,
            gate_prob,
            picked,
            arrived,
            gate_pre,
            up_pre,
            hidden,
        ) = saved[layer_index]
        attn_mats = gather_attn(layer_index)
        expert_mats = gather_experts(layer_index)
        grad_choice = jnp.sum(grad_stream[:, None, :] * picked.astype(jnp.float32), axis=-1)
        grad_picked = (
            (gate_prob[..., None] * grad_stream[:, None, :])
            .astype(jnp.bfloat16)
            .reshape(local_tokens * TOPK, D)
        )
        outgoing = jnp.zeros((E * CAP, D), jnp.bfloat16).at[buffer_row].set(grad_picked)
        grad_result = lax.all_to_all(
            outgoing, "head", split_axis=0, concat_axis=0, tiled=True
        ).reshape(head_count, local_experts, CAP, D)
        grad_hidden = jnp.einsum(
            "secd,edf->secf", grad_result, expert_mats[2], preferred_element_type=jnp.float32
        )
        gate_sig = jax.nn.sigmoid(gate_pre)
        grad_gate_pre = (
            grad_hidden * up_pre * gate_sig * (1.0 + gate_pre * (1.0 - gate_sig))
        ).astype(jnp.bfloat16)
        grad_up_pre = (grad_hidden * gate_pre * gate_sig).astype(jnp.bfloat16)
        grad_arrived = (
            jnp.einsum(
                "secf,edf->secd", grad_gate_pre, expert_mats[0], preferred_element_type=jnp.float32
            )
            + jnp.einsum(
                "secf,edf->secd", grad_up_pre, expert_mats[1], preferred_element_type=jnp.float32
            )
        ).astype(jnp.bfloat16)
        returned = lax.all_to_all(
            grad_arrived.reshape(head_count * local_experts * CAP, D),
            "head",
            split_axis=0,
            concat_axis=0,
            tiled=True,
        )
        expert_grads = (
            lax.psum_scatter(
                jnp.einsum(
                    "secd,secf->edf", arrived, grad_gate_pre, preferred_element_type=jnp.float32
                ).astype(jnp.bfloat16),
                "blk",
                scatter_dimension=1,
                tiled=True,
            ).astype(jnp.float32),
            lax.psum_scatter(
                jnp.einsum(
                    "secd,secf->edf", arrived, grad_up_pre, preferred_element_type=jnp.float32
                ).astype(jnp.bfloat16),
                "blk",
                scatter_dimension=1,
                tiled=True,
            ).astype(jnp.float32),
            lax.psum_scatter(
                jnp.einsum(
                    "secd,secf->edf", grad_result, hidden, preferred_element_type=jnp.float32
                ).astype(jnp.bfloat16),
                "blk",
                scatter_dimension=1,
                tiled=True,
            ).astype(jnp.float32),
        )
        grad_normed = jnp.sum(
            returned[buffer_row].reshape(local_tokens, TOPK, D).astype(jnp.float32), axis=1
        )
        grad_chosen = gate_prob * (
            grad_choice - jnp.sum(gate_prob * grad_choice, axis=-1, keepdims=True)
        )
        grad_logits = jnp.sum(onehot * grad_chosen[..., None], axis=1)
        router_full = attn_mats[4].astype(jnp.float32)
        grad_normed = grad_normed + lax.dot_general(
            grad_logits, router_full, (((1,), (1,)), ((), ())), precision=PRECISE
        )
        grad_router = lax.dot_general(
            normed_ffn.astype(jnp.float32), grad_logits, (((0,), (0,)), ((), ())), precision=PRECISE
        )
        grad_middle, grad_gain_second = norm_back(
            middle, scale_second, attn_mats[6].astype(jnp.float32), grad_normed
        )
        grad_stream = grad_stream + grad_middle
        grad_branch = grad_stream.astype(jnp.bfloat16)
        grad_out = contract_rows(attended_tok, grad_branch)
        grad_attended = contract_cols(grad_branch, attn_mats[3]).astype(jnp.bfloat16)
        grad_heads = lax.all_to_all(grad_attended, "head", split_axis=1, concat_axis=0, tiled=True)
        grad_query_h, grad_kv_h = attend_back(queries, keys_all, attended, log_total, grad_heads)
        grad_query_tok, grad_kv_tok = (
            lax.all_to_all(grad_query_h, "head", split_axis=0, concat_axis=1, tiled=True),
            lax.all_to_all(grad_kv_h, "head", split_axis=0, concat_axis=1, tiled=True),
        )
        grad_kv_four = grad_kv_tok.reshape(local_tokens, KVH, 2, HD)
        grad_query_pre = (
            rotate(
                grad_query_tok.reshape(local_tokens, H, HD).astype(jnp.float32),
                cosine_table,
                -sine_table,
            )
            .astype(jnp.bfloat16)
            .reshape(local_tokens, H * HD)
        )
        grad_key_pre = (
            rotate(grad_kv_four[:, :, 0].astype(jnp.float32), cosine_table, -sine_table)
            .astype(jnp.bfloat16)
            .reshape(local_tokens, KVH * HD)
        )
        grad_value_pre = grad_kv_four[:, :, 1].reshape(local_tokens, KVH * HD)
        grad_normed = (
            contract_cols(grad_query_pre, attn_mats[0])
            + contract_cols(grad_key_pre, attn_mats[1])
            + contract_cols(grad_value_pre, attn_mats[2])
        )
        grad_first, grad_gain_first = norm_back(
            stream_in, scale_first, attn_mats[5].astype(jnp.float32), grad_normed
        )
        grad_stream = grad_stream + grad_first
        attn_grads = (
            lax.psum_scatter(
                contract_rows(normed_attn, grad_query_pre),
                ("head", "blk"),
                scatter_dimension=0,
                tiled=True,
            ),
            lax.psum_scatter(
                contract_rows(normed_attn, grad_key_pre),
                ("head", "blk"),
                scatter_dimension=0,
                tiled=True,
            ),
            lax.psum_scatter(
                contract_rows(normed_attn, grad_value_pre),
                ("head", "blk"),
                scatter_dimension=0,
                tiled=True,
            ),
            lax.psum_scatter(grad_out, ("head", "blk"), scatter_dimension=0, tiled=True),
            lax.psum_scatter(grad_router, ("head", "blk"), scatter_dimension=0, tiled=True),
            lax.psum_scatter(grad_gain_first, ("head", "blk"), scatter_dimension=0, tiled=True),
            lax.psum_scatter(grad_gain_second, ("head", "blk"), scatter_dimension=0, tiled=True),
        )
        layer_grads[layer_index] = tuple(attn_grads) + tuple(expert_grads)
    stacked = [
        jnp.stack([layer_grads[layer_index][member] for layer_index in range(LAYERS)])
        for member in range(10)
    ]
    return (
        stream,
        grad_stream,
        stacked[0],
        stacked[1],
        stacked[2],
        stacked[3],
        stacked[4],
        stacked[5],
        stacked[6],
        stacked[7],
        stacked[8],
        stacked[9],
    )


def solution(mesh):
    return jax.shard_map(
        per_device,
        mesh=mesh,
        in_specs=(
            P(("blk", "head"), None),
            P(),
            P(("blk", "head"), None),
            P(None, ("head", "blk"), None),
            P(None, ("head", "blk"), None),
            P(None, ("head", "blk"), None),
            P(None, ("head", "blk"), None),
            P(None, ("head", "blk"), None),
            P(None, ("head", "blk")),
            P(None, ("head", "blk")),
            P(None, "head", "blk", None),
            P(None, "head", "blk", None),
            P(None, "head", "blk", None),
            P(("blk", "head"), None),
        ),
        out_specs=(
            P(("blk", "head"), None),
            P(("blk", "head"), None),
            P(None, ("head", "blk"), None),
            P(None, ("head", "blk"), None),
            P(None, ("head", "blk"), None),
            P(None, ("head", "blk"), None),
            P(None, ("head", "blk"), None),
            P(None, ("head", "blk")),
            P(None, ("head", "blk")),
            P(None, "head", "blk", None),
            P(None, "head", "blk", None),
            P(None, "head", "blk", None),
        ),
        check_vma=False,
    )
```

profile of v0, /device:TPU:0, one launch (start us, length us, event | category | flops | bytes accessed | tf_op | source)
XLA Modules:
  0.0 3142.5 jit_solution(11492627427130764580)
XLA Ops:
  69.8 54.2 %all-gather.41.cloned.1.call-done = bf16[1,1024,512]{2,1,0:T(8,128)(2,1)} async-done(((bf16[1,32,512]{2,1,0:T(8,128)(2,1)}), bf16[1,1024,512]{2,1,0:T(8,128)(2,1)}) %all-gather.41.cloned.1.call-update) | async-done | bytes 1048592 | tf_op jit(solution)/shard_map/all_gather | solution.py:110
  285.9 59.3 %all-to-all-done.3 = bf16[4,320,1024]{2,1,0:T(8,128)(2,1)S(1)} async-done(((bf16[4,320,1024]{2,1,0:T(8,128)(2,1)}), bf16[4,320,1024]{2,1,0:T(8,128)(2,1)S(1)}, u32[]{:S(2)}, u32[]{:S(2)}) %all-to-all-start.3) | async-done | bytes 2621472 | tf_op jit(solution)/shard_map/all_to_all | solution.py:300
  393.6 48.1 %all-gather.53.cloned.1.call-done = bf16[1,8,1024,512]{3,2,1,0:T(8,128)(2,1)} async-done(((bf16[1,8,128,512]{3,2,1,0:T(8,128)(2,1)}), bf16[1,8,1024,512]{3,2,1,0:T(8,128)(2,1)}) %all-gather.53.cloned.1.call-update) | async-done | bytes 8388624 | tf_op jit(solution)/shard_map/all_gather | solution.py:122
  456.3 80.5 %all-gather.6 = bf16[1,1024,32]{2,1,0:T(8,128)(2,1)S(1)} all-gather(bf16[1,32,32]{2,1,0:T(8,128)(2,1)S(1)} %get-tuple-element.1706), channel_id=8, replica_groups=mesh['head'=4,'blk'=8] {'head','blk'}, dimensions={1}, use_global_device_ids=true | all-gather | bytes 67584 | tf_op jit(solution)/shard_map/all_gather | solution.py:113
  744.7 84.3 %all-gather.16 = bf16[1,1024,32]{2,1,0:T(8,128)(2,1)S(1)} all-gather(bf16[1,32,32]{2,1,0:T(8,128)(2,1)S(1)} %get-tuple-element.1705), channel_id=18, replica_groups=mesh['head'=4,'blk'=8] {'head','blk'}, dimensions={1}, use_global_device_ids=true | all-gather | bytes 67584 | tf_op jit(solution)/shard_map/all_gather | solution.py:113
  1070.0 99.6 %while.74 = (s32[]{:T(128)}, f32[512,2,2,64]{0,3,2,1:T(8,128)S(1)}, f32[512,256]{0,1:T(8,128)S(1)}, s32[]{:T(128)}, s32[4096]{0:T(1024)}, /*index=5*/s32[512]{0:...) while((s32[]{:T(128)}, f32[512,2,2,64]{0,3,2,1:T(8,128)S(1)}, ...), condition=%wide.region_39.40_spmd.clone, body=%wide.region_36.39_spmd.clone.sunk | while | flops 685310976 | bytes 30589564 | solution.py:208
  1201.9 65.9 %all_to_all.272 = bf16[4,320,1024]{2,1,0:T(8,128)(2,1)S(1)} all-to-all(bf16[4,320,1024]{2,1,0:T(8,128)(2,1)S(1)} %bitcast.729), channel_id=1, replica_groups=mesh['head'=4,'blk'=8] {'head'}, dimensions={0} | all-to-all | bytes 5242880 | tf_op jit(solution)/shard_map/all_to_all | solution.py:374
  1310.3 46.4 %all-to-all-done.16 = bf16[4,320,1024]{2,1,0:T(8,128)(2,1)S(1)} async-done(((bf16[4,320,1024]{2,1,0:T(8,128)(2,1)}), bf16[4,320,1024]{2,1,0:T(8,128)(2,1)S(1)}, u32[]{:S(2)}, u32[]{:S(2)}) %all-to-all-start.16) | async-done | bytes 2621472 | tf_op jit(solution)/shard_map/all_to_all | solution.py:393
  1381.2 103.5 %while.75 = (s32[]{:T(128)}, f32[512,2,2,64]{0,3,2,1:T(8,128)S(1)}, f32[512,256]{0,1:T(8,128)S(1)}, s32[]{:T(128)}, s32[4096]{0:T(1024)}, /*index=5*/s32[512]{0:...) while((s32[]{:T(128)}, f32[512,2,2,64]{0,3,2,1:T(8,128)S(1)}, ...), condition=%wide.region_51.52_spmd.clone, body=%wide.region_48.51_spmd.clone.sunk | while | flops 685310976 | bytes 30589564 | solution.py:208
  1583.8 51.8 %all-reduce.8 = (f32[1024]{0:T(1024)S(1)}, f32[1024]{0:T(1024)S(1)}, f32[1024]{0:T(1024)S(1)}, f32[1024]{0:T(1024)S(1)}) all-reduce(f32[1024]{0:T(1024)S(1)} %copy-done.89, f32[1024]{0:T(1024)S(1)} %get-tuple-element.1556, f32[1024]{0:T(1024)S(1)} %copy-done.88, ...), channel_id=33, replica_groups=mesh['head'=4,'blk'=8] {'head','blk'}, use_global_device_ids=true, to_apply=%region_66.67.clone | all-reduce | flops 4096 | bytes 32768
  1637.9 73.5 %reduce-scatter.27.cloned.1.call-done = f32[32,512]{1,0:T(8,128)} async-done(((f32[1024,512]{1,0:T(8,128)}), f32[32,512]{1,0:T(8,128)}) %reduce-scatter.27.cloned.1.call-update) | async-done | bytes 65552 | tf_op jit(solution)/shard_map/reduce_scatter | solution.py:491
  1711.4 136.0 %reduce-scatter.25.cloned.1.call-done = f32[32,512]{1,0:T(8,128)} async-done(((f32[1024,512]{1,0:T(8,128)}), f32[32,512]{1,0:T(8,128)}) %reduce-scatter.25.cloned.1.call-update) | async-done | bytes 65552 | tf_op jit(solution)/shard_map/reduce_scatter | solution.py:491
  1848.9 134.8 %reduce-scatter.23.cloned.1.call-done = f32[32,512]{1,0:T(8,128)} async-done(((f32[1024,512]{1,0:T(8,128)}), f32[32,512]{1,0:T(8,128)}) %reduce-scatter.23.cloned.1.call-update) | async-done | bytes 65552 | tf_op jit(solution)/shard_map/reduce_scatter | solution.py:485
  1983.7 136.3 %reduce-scatter.21.cloned.1.call-done = f32[32,512]{1,0:T(8,128)} async-done(((f32[1024,512]{1,0:T(8,128)}), f32[32,512]{1,0:T(8,128)}) %reduce-scatter.21.cloned.1.call-update) | async-done | bytes 65552 | tf_op jit(solution)/shard_map/reduce_scatter | solution.py:485
  2121.5 140.3 %reduce-scatter.31.cloned.1.call-done = f32[32,1024]{1,0:T(8,128)} async-done(((f32[1024,1024]{1,0:T(8,128)}), f32[32,1024]{1,0:T(8,128)}) %reduce-scatter.31.cloned.1.call-update) | async-done | bytes 131088 | tf_op jit(solution)/shard_map/reduce_scatter | solution.py:497
  2261.8 141.4 %reduce-scatter.29.cloned.1.call-done = f32[32,1024]{1,0:T(8,128)} async-done(((f32[1024,1024]{1,0:T(8,128)}), f32[32,1024]{1,0:T(8,128)}) %reduce-scatter.29.cloned.1.call-update) | async-done | bytes 131088 | tf_op jit(solution)/shard_map/reduce_scatter | solution.py:497
  2404.9 69.0 %reduce-scatter.47.cloned.1.call-done = bf16[8,128,512]{2,1,0:T(8,128)(2,1)} async-done(((bf16[8,1024,512]{2,1,0:T(8,128)(2,1)}), bf16[8,128,512]{2,1,0:T(8,128)(2,1)}) %reduce-scatter.47.cloned.1.call-update) | async-done | bytes 1048592 | tf_op jit(solution)/shard_map/reduce_scatter | solution.py:417
  2473.9 74.7 %reduce-scatter.45.cloned.1.call-done = bf16[8,128,512]{2,1,0:T(8,128)(2,1)} async-done(((bf16[8,1024,512]{2,1,0:T(8,128)(2,1)}), bf16[8,128,512]{2,1,0:T(8,128)(2,1)}) %reduce-scatter.45.cloned.1.call-update) | async-done | bytes 1048592 | tf_op jit(solution)/shard_map/reduce_scatter | solution.py:417
  2552.4 70.9 %reduce-scatter.43.cloned.1.call-done = bf16[8,128,512]{2,1,0:T(8,128)(2,1)} async-done(((bf16[8,1024,512]{2,1,0:T(8,128)(2,1)}), bf16[8,128,512]{2,1,0:T(8,128)(2,1)}) %reduce-scatter.43.cloned.1.call-update) | async-done | bytes 1048592 | tf_op jit(solution)/shard_map/reduce_scatter | solution.py:409
  2623.3 74.9 %reduce-scatter.41.cloned.1.call-done = bf16[8,128,512]{2,1,0:T(8,128)(2,1)} async-done(((bf16[8,1024,512]{2,1,0:T(8,128)(2,1)}), bf16[8,128,512]{2,1,0:T(8,128)(2,1)}) %reduce-scatter.41.cloned.1.call-update) | async-done | bytes 1048592 | tf_op jit(solution)/shard_map/reduce_scatter | solution.py:409
  2702.0 71.1 %reduce-scatter.39.cloned.1.call-done = bf16[8,128,512]{2,1,0:T(8,128)(2,1)} async-done(((bf16[8,1024,512]{2,1,0:T(8,128)(2,1)}), bf16[8,128,512]{2,1,0:T(8,128)(2,1)}) %reduce-scatter.39.cloned.1.call-update) | async-done | bytes 1048592 | tf_op jit(solution)/shard_map/reduce_scatter | solution.py:401
  2773.1 74.7 %reduce-scatter.37.cloned.1.call-done = bf16[8,128,512]{2,1,0:T(8,128)(2,1)} async-done(((bf16[8,1024,512]{2,1,0:T(8,128)(2,1)}), bf16[8,128,512]{2,1,0:T(8,128)(2,1)}) %reduce-scatter.37.cloned.1.call-update) | async-done | bytes 1048592 | tf_op jit(solution)/shard_map/reduce_scatter | solution.py:401
  2851.6 141.3 %reduce-scatter.19.cloned.1.call-done = f32[32,1024]{1,0:T(8,128)} async-done(((f32[1024,1024]{1,0:T(8,128)}), f32[32,1024]{1,0:T(8,128)}) %reduce-scatter.19.cloned.1.call-update) | async-done | bytes 131088 | tf_op jit(solution)/shard_map/reduce_scatter | solution.py:479
  2992.9 140.9 %reduce-scatter.17.cloned.1.call-done = f32[32,1024]{1,0:T(8,128)} async-done(((f32[1024,1024]{1,0:T(8,128)}), f32[32,1024]{1,0:T(8,128)}) %reduce-scatter.17.cloned.1.call-update) | async-done | bytes 131088 | tf_op jit(solution)/shard_map/reduce_scatter | solution.py:479
  (862 shorter events, 1191.2 us)
Async XLA Ops:
  140.3 205.0 %all-gather.49.cloned.1.call-start = ((), (), s32[]{:S(2)}) async-start(), calls=%async_computation.58 | async-start | bytes 9437184 | tf_op jit(solution)/shard_map/all_gather | solution.py:120
  141.9 243.6 %all-gather.51.cloned.1.call-start = ((), (), s32[]{:S(2)}) async-start(), calls=%async_computation.59 | async-start | bytes 9437184 | tf_op jit(solution)/shard_map/all_gather | solution.py:121
  145.2 296.5 %all-gather.53.cloned.1.call-start = ((), (), s32[]{:S(2)}) async-start(), calls=%async_computation.60 | async-start | bytes 9437184 | tf_op jit(solution)/shard_map/all_gather | solution.py:122
  285.2 261.3 %all-gather.57.cloned.1.call-start = ((), (), s32[]{:S(2)}) async-start(), calls=%async_computation.62 | async-start | bytes 1081344 | tf_op jit(solution)/shard_map/all_gather | solution.py:111
  456.2 213.3 %all-gather.39.cloned.1.call-start = ((), (), s32[]{:S(2)}) async-start(), calls=%async_computation.37 | async-start | bytes 2359296 | tf_op jit(solution)/shard_map/all_gather | solution.py:249
  598.1 245.6 %all-gather.63.cloned.1.call-start = ((), (), s32[]{:S(2)}) async-start(), calls=%async_computation.65 | async-start | bytes 9437184 | tf_op jit(solution)/shard_map/all_gather | solution.py:120
  598.7 251.6 %all-gather.65.cloned.1.call-start = ((), (), s32[]{:S(2)}) async-start(), calls=%async_computation.66 | async-start | bytes 9437184 | tf_op jit(solution)/shard_map/all_gather | solution.py:121
  599.3 300.1 %all-gather.67.cloned.1.call-start = ((), (), s32[]{:S(2)}) async-start(), calls=%async_computation.67 | async-start | bytes 9437184 | tf_op jit(solution)/shard_map/all_gather | solution.py:122
  1296.8 280.9 %reduce-scatter.35.cloned.1.call-start = ((), (), s32[]{:S(2)}) async-start(), calls=%async_computation.47 | async-start | bytes 540672 | tf_op jit(solution)/shard_map/reduce_scatter | solution.py:498
  1299.2 278.5 %reduce-scatter.33.cloned.1.call-start = ((), (), s32[]{:S(2)}) async-start(), calls=%async_computation.46 | async-start | bytes 540672 | tf_op jit(solution)/shard_map/reduce_scatter | solution.py:498
  1308.5 403.0 %reduce-scatter.27.cloned.1.call-start = ((), (), s32[]{:S(2)}) async-start(), calls=%async_computation.43 | async-start | bytes 2162688 | tf_op jit(solution)/shard_map/reduce_scatter | solution.py:491
  1372.0 475.4 %reduce-scatter.25.cloned.1.call-start = ((), (), s32[]{:S(2)}) async-start(), calls=%async_computation.42 | async-start | bytes 2162688 | tf_op jit(solution)/shard_map/reduce_scatter | solution.py:491
  1498.5 485.3 %reduce-scatter.23.cloned.1.call-start = ((), (), s32[]{:S(2)}) async-start(), calls=%async_computation.41 | async-start | bytes 2162688 | tf_op jit(solution)/shard_map/reduce_scatter | solution.py:485
  1500.4 619.6 %reduce-scatter.21.cloned.1.call-start = ((), (), s32[]{:S(2)}) async-start(), calls=%async_computation.40 | async-start | bytes 2162688 | tf_op jit(solution)/shard_map/reduce_scatter | solution.py:485
  1502.7 759.1 %reduce-scatter.31.cloned.1.call-start = ((), (), s32[]{:S(2)}) async-start(), calls=%async_computation.45 | async-start | bytes 4325376 | tf_op jit(solution)/shard_map/reduce_scatter | solution.py:497
  1506.4 896.7 %reduce-scatter.29.cloned.1.call-start = ((), (), s32[]{:S(2)}) async-start(), calls=%async_computation.44 | async-start | bytes 4325376 | tf_op jit(solution)/shard_map/reduce_scatter | solution.py:497
  1510.1 963.8 %reduce-scatter.47.cloned.1.call-start = ((), (), s32[]{:S(2)}) async-start(), calls=%async_computation.53 | async-start | bytes 9437184 | tf_op jit(solution)/shard_map/reduce_scatter | solution.py:417
  1519.0 1029.7 %reduce-scatter.45.cloned.1.call-start = ((), (), s32[]{:S(2)}) async-start(), calls=%async_computation.52 | async-start | bytes 9437184 | tf_op jit(solution)/shard_map/reduce_scatter | solution.py:417
  1527.8 1095.5 %reduce-scatter.43.cloned.1.call-start = ((), (), s32[]{:S(2)}) async-start(), calls=%async_computation.51 | async-start | bytes 9437184 | tf_op jit(solution)/shard_map/reduce_scatter | solution.py:409
  1536.7 1161.5 %reduce-scatter.41.cloned.1.call-start = ((), (), s32[]{:S(2)}) async-start(), calls=%async_computation.50 | async-start | bytes 9437184 | tf_op jit(solution)/shard_map/reduce_scatter | solution.py:409
  1544.7 1228.4 %reduce-scatter.39.cloned.1.call-start = ((), (), s32[]{:S(2)}) async-start(), calls=%async_computation.49 | async-start | bytes 9437184 | tf_op jit(solution)/shard_map/reduce_scatter | solution.py:401
  1552.0 1295.8 %reduce-scatter.37.cloned.1.call-start = ((), (), s32[]{:S(2)}) async-start(), calls=%async_computation.48 | async-start | bytes 9437184 | tf_op jit(solution)/shard_map/reduce_scatter | solution.py:401
  1560.8 1432.1 %reduce-scatter.19.cloned.1.call-start = ((), (), s32[]{:S(2)}) async-start(), calls=%async_computation.39 | async-start | bytes 4325376 | tf_op jit(solution)/shard_map/reduce_scatter | solution.py:479
  1564.6 1569.2 %reduce-scatter.17.cloned.1.call-start = ((), (), s32[]{:S(2)}) async-start(), calls=%async_computation.38 | async-start | bytes 4325376 | tf_op jit(solution)/shard_map/reduce_scatter | solution.py:479
  (140 other events, 5582.1 us)
Sparse Core Ops, SparseCore 0:
  11.4 56.4 all-gather.42
  127.4 55.1 all-gather.44
  214.9 56.8 all-gather.46
  445.1 81.7 all-gather.56
  585.3 55.1 all-gather.58
  673.0 56.5 all-gather.60
  731.3 55.3 all-gather.62
  788.5 55.1 all-gather.64
  1299.5 140.8 reduce-scatter.34
  1442.6 132.3 reduce-scatter.32
  1577.2 134.1 reduce-scatter.26
  1713.5 133.8 reduce-scatter.24
  1849.7 134.0 reduce-scatter.22
  1986.0 133.9 reduce-scatter.20
  2122.9 138.8 reduce-scatter.30
  2264.5 138.6 reduce-scatter.28
  2406.6 67.2 reduce-scatter.46
  2477.2 71.3 reduce-scatter.44
  2551.9 71.3 reduce-scatter.42
  2626.8 71.3 reduce-scatter.40
  2701.7 71.3 reduce-scatter.38
  2776.4 71.3 reduce-scatter.36
  2850.1 142.8 reduce-scatter.18
  2995.2 138.5 reduce-scatter.16
  (8 shorter events, 374.5 us)
where the time goes:
time: 3160 us; the launch traced here: 3140 us
  waiting for transfers between devices  2130 us (67%)
  blocking collectives  371 us (12%)
  matrix products  195 us (6%)
  local copies, waits for them, and re-layouts  159 us (5%)
  starting transfers between devices  147 us (5%)
  other arithmetic  82.1 us (3%)
  loops' own time  44.6 us (1%)
    reduce_scatter x2, waiting for transfers between devices, per_device(): lax.psum_scatter(contract_rows(normed_attn, grad_query_pre), ('head', 'bl...  282 us
    reduce_scatter x2, waiting for transfers between devices, per_device(): lax.psum_scatter(grad_out, ('head', 'blk'), scatter_dimension=0, tiled=True)  282 us
    reduce_scatter x2, waiting for transfers between devices, per_device(): lax.psum_scatter(contract_rows(normed_attn, grad_key_pre), ('head', 'blk'...  271 us
    reduce_scatter x2, waiting for transfers between devices, per_device(): lax.psum_scatter(contract_rows(normed_attn, grad_value_pre), ('head', 'bl...  209 us
    all_gather x2, blocking collectives, gather_attn(): lax.all_gather(w_router[layer_index], ('head', 'blk'), axis=0, tiled=True)  165 us
    reduce_scatter x2, waiting for transfers between devices, per_device(): lax.psum_scatter(jnp.einsum('secd,secf->edf', arrived, grad_gate_pre, pre...  146 us
    reduce_scatter x2, waiting for transfers between devices, per_device(): lax.psum_scatter(jnp.einsum('secd,secf->edf', arrived, grad_up_pre, prefe...  146 us
    reduce_scatter x2, waiting for transfers between devices, per_device(): lax.psum_scatter(jnp.einsum('secd,secf->edf', grad_result, hidden, prefer...  144 us
  transfers between devices with their start and end apart: 63, of which 52 were waited for; matrix products, arithmetic and copies ran while one was open for 11% of the time, Pallas kernels for 0%

commit v1 on v0

v1 whole, which is shorter than its diff:
```python
import jax
import jax.numpy as jnp
from jax import lax
from jax.sharding import PartitionSpec as P

D = 1024
H = 16
KVH = 8
HD = 64
E = 32
LAYERS = 2
CAP = 40
SIDE = 128


EPSILON = 1e-06
MASKED = -1e30
ROPE_BASE = 10000.0
PRECISE = lax.Precision.HIGHEST
BOTH = ("head", "blk")


def rms_scale(values):
    return lax.rsqrt(jnp.mean(values * values, axis=-1, keepdims=True) + EPSILON)


def rotate(values, cosine_table, sine_table):
    half_dim = values.shape[-1] // 2
    first = values[..., :half_dim]
    second = values[..., half_dim:]
    return jnp.concatenate(
        [first * cosine_table - second * sine_table, second * cosine_table + first * sine_table],
        axis=-1,
    )


def rotary_tables(start, count, head_dim):
    half_dim = head_dim // 2
    frequency = jnp.power(ROPE_BASE, -(jnp.arange(half_dim, dtype=jnp.float32) * 2.0 / head_dim))
    places = start + jnp.arange(count, dtype=jnp.int32)
    angles = places.astype(jnp.float32)[:, None] * frequency[None, :]
    return (jnp.cos(angles)[:, None, :], jnp.sin(angles)[:, None, :])


def dot(left, right):
    return jnp.dot(left, right, preferred_element_type=jnp.float32)


def contract_rows(left, right, precision=None):
    return lax.dot_general(
        left,
        right,
        (((0,), (0,)), ((), ())),
        preferred_element_type=jnp.float32,
        precision=precision,
    )


def contract_cols(left, right, precision=None):
    return lax.dot_general(
        left,
        right,
        (((1,), (1,)), ((), ())),
        preferred_element_type=jnp.float32,
        precision=precision,
    )


def halves(values):
    high = lax.reduce_precision(values, 8, 7)
    return (high.astype(jnp.bfloat16), (values - high).astype(jnp.bfloat16))


def norm_back(stream, scale, gain, grad_normed):
    inner = grad_normed * gain
    grad_gain = jnp.sum(grad_normed * stream * scale, axis=0)
    grad_stream = scale * inner - stream * scale * scale * scale * jnp.mean(
        stream * inner, axis=-1, keepdims=True
    )
    return (grad_stream, grad_gain)


def per_device(
    tokens,
    segments,
    routes,
    w_query,
    w_key,
    w_value,
    w_out,
    w_router,
    gain_attn,
    gain_ffn,
    w_gate,
    w_up,
    w_down,
    cotangent,
):
    head_count = lax.axis_size("head")
    cycle_count = lax.axis_size("blk")
    cycle_index = lax.axis_index("blk")
    local_tokens = tokens.shape[0]
    block_rows = local_tokens * head_count
    query_start = cycle_index * block_rows
    groups = H // KVH
    key_heads = KVH // head_count
    query_cols = H * HD // head_count
    key_cols = KVH * HD // head_count
    qkv_cols = query_cols + 2 * key_cols
    local_experts = E // head_count
    copies = cycle_count // local_experts
    copy_index = cycle_index % copies
    shard_rows = w_query.shape[1]
    slice_rows = w_gate.shape[2]
    hidden_units = w_gate.shape[3]
    score_scale = HD ** (-0.5)
    cosine_table, sine_table = rotary_tables(query_start, block_rows, HD)
    query_segs = lax.dynamic_slice_in_dim(segments, query_start, block_rows)
    query_pos = query_start + jnp.arange(block_rows, dtype=jnp.int32)
    block_last = segments.reshape(cycle_count, block_rows)[:, block_rows - 1]
    first_owner = jnp.sum(
        (block_last < query_segs[0]) & (jnp.arange(cycle_count) < cycle_index)
    ).astype(jnp.int32)

    hot = jnp.any(
        routes.T[None, :, :] == jnp.arange(E, dtype=jnp.int32)[:, None, None], axis=1
    )
    earlier = jnp.triu(jnp.ones((local_tokens, local_tokens), jnp.bfloat16), 1)
    slot = dot(hot.astype(jnp.bfloat16), earlier).astype(jnp.int32)
    picks = hot[:, None, :] & (
        slot[:, None, :] == jnp.arange(CAP, dtype=jnp.int32)[None, :, None]
    )
    picks_mat = picks.astype(jnp.bfloat16).reshape(E * CAP, local_tokens)

    def to_experts(rows):
        if copies > 1:
            mine = jnp.arange(copies)[None, :, None, None] == copy_index
            rows = jnp.where(mine, rows.reshape(E, 1, CAP, D), jnp.zeros((), rows.dtype))
            rows = rows.reshape(E * copies * CAP, D)
        return lax.all_to_all(rows, BOTH, split_axis=0, concat_axis=0, tiled=True)

    def from_experts(rows):
        rows = lax.all_to_all(rows, BOTH, split_axis=0, concat_axis=0, tiled=True)
        if copies > 1:
            rows = lax.dynamic_index_in_dim(
                rows.reshape(E, copies, CAP, D), copy_index, 1, keepdims=False
            ).reshape(E * CAP, D)
        return rows

    def by_head(values, cols):
        return values.reshape(LAYERS, shard_rows, head_count, cols)

    side = jnp.concatenate([w_router, gain_attn[..., None], gain_ffn[..., None]], axis=-1)
    side = jnp.pad(side, ((0, 0), (0, 0), (0, SIDE - side.shape[-1])))
    side = jnp.broadcast_to(side[:, :, None, :], (LAYERS, shard_rows, head_count, SIDE))
    sent = jnp.concatenate(
        [
            by_head(w_query, query_cols),
            by_head(w_key, key_cols),
            by_head(w_value, key_cols),
            side,
        ],
        axis=-1,
    )
    sent = jnp.transpose(sent, (2, 0, 1, 3))
    sent = lax.all_to_all(sent, "head", split_axis=0, concat_axis=0, tiled=True)
    attn_all = lax.all_gather(sent, "blk", axis=0, tiled=False)
    attn_all = jnp.transpose(attn_all, (2, 1, 0, 3, 4)).reshape(LAYERS, D, qkv_cols + SIDE)
    out_all = lax.all_gather(w_out, "blk", axis=1, tiled=True)

    def gather_experts(layer_index):
        mats = jnp.stack([w_gate[layer_index], w_up[layer_index], w_down[layer_index]], axis=1)
        mats = jnp.repeat(mats, copies, axis=0)
        mats = lax.all_to_all(mats, "blk", split_axis=0, concat_axis=0, tiled=True)
        return jnp.transpose(mats, (1, 0, 2, 3)).reshape(3, D, hidden_units)

    def scatter_experts(grads):
        grads = jnp.stack(grads).astype(jnp.bfloat16)
        grads = grads.reshape(3, cycle_count, slice_rows, hidden_units)
        grads = jnp.transpose(grads, (1, 0, 2, 3))
        grads = lax.all_to_all(grads, "blk", split_axis=0, concat_axis=0, tiled=True)
        grads = grads.reshape(local_experts, copies, 3, slice_rows, hidden_units)
        grads = jnp.sum(grads.astype(jnp.float32), axis=1)
        return (grads[:, 0], grads[:, 1], grads[:, 2])

    def sum_over_head(partial):
        parts = lax.all_to_all(
            partial.astype(jnp.bfloat16), "head", split_axis=0, concat_axis=0, tiled=True
        ).reshape(head_count, local_tokens, D)
        return jnp.sum(parts.astype(jnp.float32), axis=0)

    def block_mask(key_owner):
        key_start = key_owner * block_rows
        key_segs = lax.dynamic_slice_in_dim(segments, key_start, block_rows)
        key_pos = key_start + jnp.arange(block_rows, dtype=jnp.int32)
        return (query_segs[:, None] == key_segs[None, :]) & (
            query_pos[:, None] >= key_pos[None, :]
        )

    def key_block(keys_all, key_owner):
        chosen_rows = lax.dynamic_slice_in_dim(keys_all, key_owner * block_rows, block_rows)
        return (
            chosen_rows[:, :key_cols].reshape(block_rows, key_heads, HD),
            chosen_rows[:, key_cols:].reshape(block_rows, key_heads, HD),
        )

    def block_scores(query_four, key_part, allowed):
        scores = (
            jnp.einsum("qcgd,kcd->cgqk", query_four, key_part, preferred_element_type=jnp.float32)
            * score_scale
        )
        return jnp.where(allowed, scores, MASKED)

    def attend(queries, keys_all):
        query_four = queries.reshape(block_rows, key_heads, groups, HD)

        def visit(key_owner, state_in):
            running_max, running_sum, weighted = state_in
            allowed = block_mask(key_owner)
            key_part, value_part = key_block(keys_all, key_owner)
            scores = block_scores(query_four, key_part, allowed)
            new_max = jnp.maximum(running_max, jnp.max(scores, axis=-1))
            exponent = jnp.where(allowed, jnp.exp(scores - new_max[..., None]), 0.0)
            factor = jnp.exp(running_max - new_max)
            running_sum = running_sum * factor + jnp.sum(exponent, axis=-1)
            weighted = weighted * jnp.transpose(factor, (2, 0, 1))[..., None] + jnp.einsum(
                "cgqk,kcd->qcgd",
                exponent.astype(jnp.bfloat16),
                value_part,
                preferred_element_type=jnp.float32,
            )
            return (new_max, running_sum, weighted)

        start_state = (
            jnp.full((key_heads, groups, block_rows), MASKED, jnp.float32),
            jnp.zeros((key_heads, groups, block_rows), jnp.float32),
            jnp.zeros((block_rows, key_heads, groups, HD), jnp.float32),
        )
        running_max, running_sum, weighted = lax.fori_loop(
            first_owner, cycle_index + 1, visit, start_state
        )
        attended = (
            (weighted / jnp.transpose(running_sum, (2, 0, 1))[..., None])
            .astype(jnp.bfloat16)
            .reshape(block_rows, query_cols)
        )
        return (attended, running_max + jnp.log(running_sum))

    def attend_back(queries, keys_all, attended, log_total, grad_attended):
        query_four = queries.reshape(block_rows, key_heads, groups, HD)
        grad_four = grad_attended.reshape(block_rows, key_heads, groups, HD)
        row_delta = jnp.transpose(
            jnp.sum(
                grad_four.astype(jnp.float32)
                * attended.reshape(block_rows, key_heads, groups, HD).astype(jnp.float32),
                axis=-1,
            ),
            (1, 2, 0),
        )

        def visit(key_owner, state_in):
            grad_query, key_grads = state_in
            allowed = block_mask(key_owner)
            key_part, value_part = key_block(keys_all, key_owner)
            scores = block_scores(query_four, key_part, allowed)
            probability = jnp.where(allowed, jnp.exp(scores - log_total[..., None]), 0.0)
            grad_value = jnp.einsum(
                "cgqk,qcgd->kcd",
                probability.astype(jnp.bfloat16),
                grad_four,
                preferred_element_type=jnp.float32,
            )
            grad_prob = jnp.einsum(
                "qcgd,kcd->cgqk", grad_four, value_part, preferred_element_type=jnp.float32
            )
            grad_scores = (probability * (grad_prob - row_delta[..., None])).astype(jnp.bfloat16)
            grad_query = grad_query + jnp.einsum(
                "cgqk,kcd->qcgd", grad_scores, key_part, preferred_element_type=jnp.float32
            )
            grad_key = (
                jnp.einsum(
                    "cgqk,qcgd->kcd", grad_scores, query_four, preferred_element_type=jnp.float32
                )
                * score_scale
            )
            stacked = jnp.concatenate(
                [grad_key.reshape(block_rows, key_cols), grad_value.reshape(block_rows, key_cols)],
                axis=1,
            ).astype(jnp.bfloat16)
            key_grads = lax.dynamic_update_slice_in_dim(
                key_grads, stacked, key_owner * block_rows, 0
            )
            return (grad_query, key_grads)

        start_state = (
            jnp.zeros((block_rows, key_heads, groups, HD), jnp.float32),
            jnp.zeros((cycle_count * block_rows, 2 * key_cols), jnp.bfloat16),
        )
        grad_query, key_grads = lax.fori_loop(first_owner, cycle_index + 1, visit, start_state)
        key_grads = lax.all_to_all(key_grads, "blk", split_axis=0, concat_axis=0, tiled=True)
        key_grads = jnp.sum(
            key_grads.reshape(cycle_count, block_rows, 2 * key_cols).astype(jnp.float32), axis=0
        ).astype(jnp.bfloat16)
        grad_query = (grad_query * score_scale).astype(jnp.bfloat16)
        return (grad_query.reshape(block_rows, query_cols), key_grads)

    stream = tokens.astype(jnp.float32)
    saved = []
    for layer_index in range(LAYERS):
        qkv_mat = attn_all[layer_index, :, :qkv_cols]
        side_all = attn_all[layer_index, :, qkv_cols:]
        router = side_all[:, :E]
        gain_first = side_all[:, E].astype(jnp.float32)
        gain_second = side_all[:, E + 1].astype(jnp.float32)
        out_mat = out_all[layer_index]
        gate_mat, up_mat, down_mat = gather_experts(layer_index)
        scale_first = rms_scale(stream)
        normed_attn = (stream * scale_first * gain_first).astype(jnp.bfloat16)
        normed_block = lax.all_gather(normed_attn, "head", axis=0, tiled=True)
        qkv_pre = dot(normed_block, qkv_mat)
        query_pre = qkv_pre[:, :query_cols].reshape(block_rows, H // head_count, HD)
        key_pre = qkv_pre[:, query_cols : query_cols + key_cols].reshape(block_rows, key_heads, HD)
        queries = (
            rotate(query_pre, cosine_table, sine_table)
            .astype(jnp.bfloat16)
            .reshape(block_rows, query_cols)
        )
        key_rot = rotate(key_pre, cosine_table, sine_table).reshape(block_rows, key_cols)
        key_value = jnp.concatenate(
            [key_rot, qkv_pre[:, query_cols + key_cols :]], axis=1
        ).astype(jnp.bfloat16)
        keys_all = lax.all_gather(key_value, "blk", axis=0, tiled=True)
        attended, log_total = attend(queries, keys_all)
        middle = stream + sum_over_head(dot(attended, out_mat))
        scale_second = rms_scale(middle)
        normed_ffn = (middle * scale_second * gain_second).astype(jnp.bfloat16)
        logits = lax.dot_general(
            router, normed_ffn, (((0,), (1,)), ((), ())), preferred_element_type=jnp.float32
        )
        top = jnp.max(jnp.where(hot, logits, -jnp.inf), axis=0, keepdims=True)
        weight = jnp.where(hot, jnp.exp(jnp.where(hot, logits - top, 0.0)), 0.0)
        gate_prob = weight / jnp.sum(weight, axis=0, keepdims=True)
        arrived = to_experts(dot(picks_mat, normed_ffn).astype(jnp.bfloat16))
        gate_pre = dot(arrived, gate_mat)
        up_pre = dot(arrived, up_mat)
        hidden = (jax.nn.silu(gate_pre) * up_pre).astype(jnp.bfloat16)
        result = contract_cols(hidden, down_mat).astype(jnp.bfloat16)
        returned = from_experts(result)
        gate_rows = jnp.where(picks, gate_prob[:, None, :], 0.0).reshape(E * CAP, local_tokens)
        gate_high, gate_low = halves(gate_rows)
        saved.append(
            (
                stream,
                scale_first,
                normed_block,
                queries,
                keys_all,
                attended,
                log_total,
                middle,
                scale_second,
                normed_ffn,
                gate_prob,
                gate_rows,
                returned,
                arrived,
                gate_pre,
                up_pre,
                hidden,
                (qkv_mat, router, gain_first, gain_second, out_mat, gate_mat, up_mat, down_mat),
            )
        )
        stream = middle + contract_rows(gate_high, returned) + contract_rows(gate_low, returned)
    grad_stream = cotangent.astype(jnp.float32)
    layer_grads = [None] * LAYERS
    for layer_index in range(LAYERS - 1, -1, -1):
        (
            stream_in,
            scale_first,
            normed_block,
            queries,
            keys_all,
            attended,
            log_total,
            middle,
            scale_second,
            normed_ffn,
            gate_prob,
            gate_rows,
            returned,
            arrived,
            gate_pre,
            up_pre,
            hidden,
            (qkv_mat, router, gain_first, gain_second, out_mat, gate_mat, up_mat, down_mat),
        ) = saved[layer_index]
        grad_high, grad_low = halves(grad_stream)
        spread = dot(picks_mat, grad_high) + dot(picks_mat, grad_low)
        row_gate = jnp.sum(gate_rows, axis=1, keepdims=True)
        grad_result = to_experts((spread * row_gate).astype(jnp.bfloat16))
        row_choice = contract_cols(returned, grad_high) + contract_cols(returned, grad_low)
        grad_choice = jnp.sum(
            jnp.where(picks, row_choice.reshape(E, CAP, local_tokens), 0.0), axis=1
        )
        grad_hidden = dot(grad_result, down_mat)
        gate_sig = jax.nn.sigmoid(gate_pre)
        grad_gate_pre = (
            grad_hidden * up_pre * gate_sig * (1.0 + gate_pre * (1.0 - gate_sig))
        ).astype(jnp.bfloat16)
        grad_up_pre = (grad_hidden * gate_pre * gate_sig).astype(jnp.bfloat16)
        grad_arrived = (
            contract_cols(grad_gate_pre, gate_mat) + contract_cols(grad_up_pre, up_mat)
        ).astype(jnp.bfloat16)
        grad_rows = from_experts(grad_arrived)
        expert_grads = scatter_experts(
            [
                contract_rows(arrived, grad_gate_pre),
                contract_rows(arrived, grad_up_pre),
                contract_rows(grad_result, hidden),
            ]
        )
        grad_normed = contract_rows(picks_mat, grad_rows)
        grad_logits = gate_prob * (
            grad_choice - jnp.sum(gate_prob * grad_choice, axis=0, keepdims=True)
        )
        grad_normed = grad_normed + lax.dot_general(
            grad_logits,
            router.astype(jnp.float32),
            (((0,), (1,)), ((), ())),
            precision=PRECISE,
        )
        grad_router = lax.dot_general(
            normed_ffn.astype(jnp.float32),
            grad_logits,
            (((0,), (1,)), ((), ())),
            precision=PRECISE,
        )
        grad_middle, grad_gain_second = norm_back(middle, scale_second, gain_second, grad_normed)
        grad_stream = grad_stream + grad_middle
        branch_block = lax.all_gather(
            grad_stream.astype(jnp.bfloat16), "head", axis=0, tiled=True
        )
        grad_out = contract_rows(attended, branch_block)
        grad_attended = contract_cols(branch_block, out_mat).astype(jnp.bfloat16)
        grad_query, grad_kv = attend_back(queries, keys_all, attended, log_total, grad_attended)
        grad_query_pre = (
            rotate(
                grad_query.reshape(block_rows, H // head_count, HD).astype(jnp.float32),
                cosine_table,
                -sine_table,
            )
            .astype(jnp.bfloat16)
            .reshape(block_rows, query_cols)
        )
        grad_key_pre = (
            rotate(
                grad_kv[:, :key_cols].reshape(block_rows, key_heads, HD).astype(jnp.float32),
                cosine_table,
                -sine_table,
            )
            .astype(jnp.bfloat16)
            .reshape(block_rows, key_cols)
        )
        grad_qkv = jnp.concatenate([grad_query_pre, grad_key_pre, grad_kv[:, key_cols:]], axis=1)
        grad_normed = sum_over_head(contract_cols(grad_qkv, qkv_mat))
        grad_first, grad_gain_first = norm_back(stream_in, scale_first, gain_first, grad_normed)
        grad_stream = grad_stream + grad_first
        grad_side = jnp.concatenate(
            [grad_router, grad_gain_first[:, None], grad_gain_second[:, None]], axis=1
        )
        grad_side = jnp.pad(grad_side, ((0, 0), (0, SIDE - grad_side.shape[1])))
        grad_mats = jnp.concatenate(
            [contract_rows(normed_block, grad_qkv), grad_side], axis=1
        ).astype(jnp.bfloat16)
        grad_mats = jnp.transpose(
            grad_mats.reshape(head_count, cycle_count, shard_rows, qkv_cols + SIDE), (1, 0, 2, 3)
        )
        grad_mats = lax.all_to_all(grad_mats, "blk", split_axis=0, concat_axis=0, tiled=True)
        grad_mats = jnp.sum(grad_mats.astype(jnp.float32), axis=0).astype(jnp.bfloat16)
        grad_mats = lax.all_to_all(grad_mats, "head", split_axis=0, concat_axis=0, tiled=True)
        grad_mats = grad_mats.astype(jnp.float32)
        grad_out = lax.all_to_all(
            grad_out.astype(jnp.bfloat16).reshape(cycle_count, shard_rows, D),
            "blk",
            split_axis=0,
            concat_axis=0,
            tiled=True,
        )
        grad_out = jnp.sum(grad_out.astype(jnp.float32), axis=0)

        def joined(start, stop):
            return jnp.transpose(grad_mats[:, :, start:stop], (1, 0, 2)).reshape(shard_rows, -1)

        grad_side = jnp.sum(grad_mats[:, :, qkv_cols:], axis=0)
        layer_grads[layer_index] = (
            joined(0, query_cols),
            joined(query_cols, query_cols + key_cols),
            joined(query_cols + key_cols, qkv_cols),
            grad_out,
            grad_side[:, :E],
            grad_side[:, E],
            grad_side[:, E + 1],
        ) + expert_grads
    stacked = [
        jnp.stack([layer_grads[layer_index][member] for layer_index in range(LAYERS)])
        for member in range(10)
    ]
    return (stream, grad_stream, *stacked)


def solution(mesh):
    return jax.shard_map(
        per_device,
        mesh=mesh,
        in_specs=(
            P(("blk", "head"), None),
            P(),
            P(("blk", "head"), None),
            P(None, ("head", "blk"), None),
            P(None, ("head", "blk"), None),
            P(None, ("head", "blk"), None),
            P(None, ("head", "blk"), None),
            P(None, ("head", "blk"), None),
            P(None, ("head", "blk")),
            P(None, ("head", "blk")),
            P(None, "head", "blk", None),
            P(None, "head", "blk", None),
            P(None, "head", "blk", None),
            P(("blk", "head"), None),
        ),
        out_specs=(
            P(("blk", "head"), None),
            P(("blk", "head"), None),
            P(None, ("head", "blk"), None),
            P(None, ("head", "blk"), None),
            P(None, ("head", "blk"), None),
            P(None, ("head", "blk"), None),
            P(None, ("head", "blk"), None),
            P(None, ("head", "blk")),
            P(None, ("head", "blk")),
            P(None, "head", "blk", None),
            P(None, "head", "blk", None),
            P(None, "head", "blk", None),
        ),
        check_vma=False,
    )
```

time: 3160 us -> 1410 us (0.45)
  waiting for transfers between devices: 2130 us -> 758 us
  blocking collectives: 371 us -> 173 us
  local copies, waits for them, and re-layouts: 159 us -> 73.9 us
  matrix products: 195 us -> 127 us
  loops' own time: 44.6 us -> 3.77 us
  starting transfers between devices: 147 us -> 186 us
    reduce_scatter x16 -> x0, waiting for transfers between devices: 1480 us -> none  [the longest x2 282 us: per_device(): lax.psum_scatter(contract_rows(normed_attn, grad_query_pre), ('head', 'bl...]
    all_to_all x15 -> x21, waiting for transfers between devices: 238 us -> 575 us  [the longest x4 218 us: from_experts(): rows = lax.all_to_all(rows, BOTH, split_axis=0, concat_axis=0, tiled=True)]
    all_gather x16 -> x8, waiting for transfers between devices: 356 us -> 182 us  [the longest x2 54.7 us: per_device(): normed_block = lax.all_gather(normed_attn, 'head', axis=0, tiled=True)]
    all_gather x2 -> x0, blocking collectives: 165 us -> none  [gather_attn(): lax.all_gather(w_router[layer_index], ('head', 'blk'), axis=0, tiled=True)]
    all_to_all x15 -> x21, starting transfers between devices: 58.9 us -> 186 us  [the longest x2 93.4 us: attend_back(): lax.all_to_all(key_grads, 'blk', split_axis=0, concat_axis=0, tiled=True)]
    dot_general x42 -> x33, matrix products: 163 us -> 65.5 us  [the longest x17 47.8 us: dot(): return jnp.dot(left, right, preferred_element_type=jnp.float32)]
    unnamed x2 -> x0, blocking collectives: 93.9 us -> none
    ppermute x16 -> x0, starting transfers between devices: 86.5 us -> none  [from_behind(): lax.ppermute(value, axis, [(i, (i + by) % count) for i in range(count)])]
  transfers between devices with their start and end apart: 63 -> 29, of which waited for: 52 -> 27; matrix products, arithmetic and copies ran while one was open for 11% -> 10% of each run, Pallas kernels for 0% -> 0%
where the time goes in v1:
time: 1410 us; the launch traced here: 1400 us
  waiting for transfers between devices  758 us (54%)
  starting transfers between devices  186 us (13%)
  blocking collectives  173 us (12%)
  matrix products  127 us (9%)
  local copies, waits for them, and re-layouts  73.9 us (5%)
  other arithmetic  60.9 us (4%)
  between operations  19.1 us (1%)
    all_to_all x4, waiting for transfers between devices, from_experts(): rows = lax.all_to_all(rows, BOTH, split_axis=0, concat_axis=0, tiled=True)  218 us
    all_to_all x2, blocking collectives, to_experts(): return lax.all_to_all(rows, BOTH, split_axis=0, concat_axis=0, tiled=True)  130 us
    all_to_all x2, waiting for transfers between devices, to_experts(): return lax.all_to_all(rows, BOTH, split_axis=0, concat_axis=0, tiled=True)  113 us
    all_to_all x2, starting transfers between devices, attend_back(): lax.all_to_all(key_grads, 'blk', split_axis=0, concat_axis=0, tiled=True)  93.4 us
    all_to_all x2, waiting for transfers between devices, gather_experts(): mats = lax.all_to_all(mats, 'blk', split_axis=0, concat_axis=0, tiled=True)  68.3 us
    all_to_all x2, waiting for transfers between devices, scatter_experts(): lax.all_to_all(grads, 'blk', split_axis=0, concat_axis=0, tiled=True)  54.7 us
    all_gather x2, waiting for transfers between devices, per_device(): normed_block = lax.all_gather(normed_attn, 'head', axis=0, tiled=True)  54.7 us
    all_to_all x3, waiting for transfers between devices, sum_over_head(): lax.all_to_all(partial.astype(jnp.bfloat16), 'head', split_axis=0, concat...  51.4 us
  transfers between devices with their start and end apart: 29, of which 27 were waited for; matrix products, arithmetic and copies ran while one was open for 10% of the time, Pallas kernels for 0%

profile of v1, /device:TPU:0, one launch (start us, length us, event | category | flops | bytes accessed | tf_op | source)
XLA Modules:
  0.0 1401.8 jit_solution(4767294002453905366)
XLA Ops:
  29.3 29.0 %all-gather.24.cloned.1.call-done = bf16[32,2,32,640]{3,2,1,0:T(8,128)(2,1)} async-done(((bf16[4,2,32,640]{3,2,1,0:T(8,128)(2,1)}), bf16[32,2,32,640]{3,2,1,0:T(8,128)(2,1)}) %all-gather.24.cloned.1.call-update) | async-done | bytes 2621456 | tf_op jit(solution)/shard_map/all_gather | solution.py:167
  65.2 27.1 %all-gather.10.cloned.1.call-done = bf16[512,1024]{1,0:T(8,128)(2,1)} async-done(((bf16[128,1024]{1,0:T(8,128)(2,1)}), bf16[512,1024]{1,0:T(8,128)(2,1)}) %all-gather.10.cloned.1.call-update) | async-done | bytes 1048592 | tf_op jit(solution)/shard_map/all_gather | solution.py:319
  98.9 24.2 %all-gather.12.cloned.1.call-done = bf16[4096,256]{0,1:T(8,128)(2,1)} async-done(((bf16[512,256]{0,1:T(8,128)(2,1)}), bf16[4096,256]{0,1:T(8,128)(2,1)}) %all-gather.12.cloned.1.call-update) | async-done | bytes 2097168 | tf_op jit(solution)/shard_map/all_gather | solution.py:332
  190.6 33.2 %all-to-all-done.3 = bf16[8,3,128,512]{3,2,1,0:T(8,128)(2,1)} async-done(((bf16[8,3,128,512]{3,2,1,0:T(8,128)(2,1)}), bf16[8,3,128,512]{3,2,1,0:T(8,128)(2,1)}, u32[]{:S(2)}, u32[]{:S(2)}) %all-to-all-start.3) | async-done | bytes 3145760 | tf_op jit(solution)/shard_map/all_to_all | solution.py:174
  230.6 56.6 %all-to-all-done.2 = bf16[32,40,1024]{2,1,0:T(8,128)(2,1)S(1)} async-done(((bf16[32,40,1024]{2,1,0:T(8,128)(2,1)}), bf16[32,40,1024]{2,1,0:T(8,128)(2,1)S(1)}, u32[]{:S(2)}, u32[]{:S(2)}) %all-to-all-start.2) | async-done | bytes 2621472 | tf_op jit(solution)/shard_map/all_to_all | solution.py:140
  303.9 57.3 %all-to-all-done.4 = bf16[32,40,1024]{2,1,0:T(8,128)(2,1)S(1)} async-done(((bf16[32,40,1024]{2,1,0:T(8,128)(2,1)}), bf16[32,40,1024]{2,1,0:T(8,128)(2,1)S(1)}, u32[]{:S(2)}, u32[]{:S(2)}) %all-to-all-start.4) | async-done | bytes 2621472 | tf_op jit(solution)/shard_map/all_to_all | solution.py:143
  365.0 27.6 %all-gather.16.cloned.1.call-done = bf16[512,1024]{1,0:T(8,128)(2,1)} async-done(((bf16[128,1024]{1,0:T(8,128)(2,1)}), bf16[512,1024]{1,0:T(8,128)(2,1)}) %all-gather.16.cloned.1.call-update) | async-done | bytes 1048592 | tf_op jit(solution)/shard_map/all_gather | solution.py:319
  396.5 26.8 %all-gather.18.cloned.1.call-done = bf16[4096,256]{0,1:T(8,128)(2,1)} async-done(((bf16[512,256]{0,1:T(8,128)(2,1)}), bf16[4096,256]{0,1:T(8,128)(2,1)}) %all-gather.18.cloned.1.call-update) | async-done | bytes 2097168 | tf_op jit(solution)/shard_map/all_gather | solution.py:332
  439.8 21.9 %all-to-all-done.5 = bf16[4,128,1024]{2,1,0:T(8,128)(2,1)S(1)} async-done(((bf16[4,128,1024]{2,1,0:T(8,128)(2,1)}), bf16[4,128,1024]{2,1,0:T(8,128)(2,1)S(1)}, u32[]{:S(2)}, u32[]{:S(2)}) %all-to-all-start.5) | async-done | bytes 1048608 | tf_op jit(solution)/shard_map/all_to_all | solution.py:187
  461.7 20.4 %all-to-all-start.7 = ((bf16[8,3,128,512]{3,2,1,0:T(8,128)(2,1)}), bf16[8,3,128,512]{3,2,1,0:T(8,128)(2,1)}, u32[]{:S(2)}, u32[]{:S(2)}) async-start(bf16[8,3,128,512]{3,2,1,0:T(8,128)(2,1)} %pad_maximum_fusion.6), calls=%async_computation.7 | async-start | bytes 6291456 | tf_op jit(solution)/shard_map/all_to_all | solution.py:174
  485.4 35.1 %all-to-all-done.7 = bf16[8,3,128,512]{3,2,1,0:T(8,128)(2,1)} async-done(((bf16[8,3,128,512]{3,2,1,0:T(8,128)(2,1)}), bf16[8,3,128,512]{3,2,1,0:T(8,128)(2,1)}, u32[]{:S(2)}, u32[]{:S(2)}) %all-to-all-start.7) | async-done | bytes 3145760 | tf_op jit(solution)/shard_map/all_to_all | solution.py:174
  526.9 56.5 %all-to-all-done.6 = bf16[32,40,1024]{2,1,0:T(8,128)(2,1)S(1)} async-done(((bf16[32,40,1024]{2,1,0:T(8,128)(2,1)}), bf16[32,40,1024]{2,1,0:T(8,128)(2,1)S(1)}, u32[]{:S(2)}, u32[]{:S(2)}) %all-to-all-start.6) | async-done | bytes 2621472 | tf_op jit(solution)/shard_map/all_to_all | solution.py:140
  602.0 55.5 %all-to-all-done.8 = bf16[32,40,1024]{2,1,0:T(8,128)(2,1)S(1)} async-done(((bf16[32,40,1024]{2,1,0:T(8,128)(2,1)}), bf16[32,40,1024]{2,1,0:T(8,128)(2,1)S(1)}, u32[]{:S(2)}, u32[]{:S(2)}) %all-to-all-start.8) | async-done | bytes 2621472 | tf_op jit(solution)/shard_map/all_to_all | solution.py:143
  664.5 64.6 %all_to_all.200 = bf16[32,40,1024]{2,1,0:T(8,128)(2,1)S(1)} all-to-all(bf16[32,40,1024]{2,1,0:T(8,128)(2,1)S(1)} %bitcast.618), channel_id=1, replica_groups=mesh['head'=4,'blk'=8] {'head','blk'}, dimensions={0} | all-to-all | bytes 5242880 | tf_op jit(solution)/shard_map/all_to_all | solution.py:140
  739.8 60.0 %all-to-all-done.10 = bf16[32,40,1024]{2,1,0:T(8,128)(2,1)S(1)} async-done(((bf16[32,40,1024]{2,1,0:T(8,128)(2,1)}), bf16[32,40,1024]{2,1,0:T(8,128)(2,1)S(1)}, u32[]{:S(2)}, u32[]{:S(2)}) %all-to-all-start.10) | async-done | bytes 2621472 | tf_op jit(solution)/shard_map/all_to_all | solution.py:143
  803.5 26.9 %all-gather.20.cloned.1.call-done = bf16[512,1024]{1,0:T(8,128)(2,1)} async-done(((bf16[128,1024]{1,0:T(8,128)(2,1)}), bf16[512,1024]{1,0:T(8,128)(2,1)}) %all-gather.20.cloned.1.call-update) | async-done | bytes 1048592 | tf_op jit(solution)/shard_map/all_gather | solution.py:440
  848.3 42.7 %all-to-all-start.11 = ((bf16[8,512,256]{1,2,0:T(8,128)(2,1)}), bf16[8,512,256]{1,2,0:T(8,128)(2,1)S(1)}, u32[]{:S(2)}, u32[]{:S(2)}) async-start(bf16[8,512,256]{1,2,0:T(8,128)(2,1)} %copy.174), calls=%async_computation.11 | async-start | bytes 4194304 | tf_op jit(solution)/shard_map/all_to_all | solution.py:300
  891.3 26.3 %all-to-all-done.11 = bf16[8,512,256]{1,2,0:T(8,128)(2,1)S(1)} async-done(((bf16[8,512,256]{1,2,0:T(8,128)(2,1)}), bf16[8,512,256]{1,2,0:T(8,128)(2,1)S(1)}, u32[]{:S(2)}, u32[]{:S(2)}) %all-to-all-start.11) | async-done | bytes 2097184 | tf_op jit(solution)/shard_map/all_to_all | solution.py:300
  920.3 26.6 %all_to_all.201 = bf16[4,128,1024]{2,1,0:T(8,128)(2,1)S(1)} all-to-all(bf16[4,128,1024]{2,1,0:T(8,128)(2,1)S(1)} %bitcast.672), channel_id=1, replica_groups=mesh['head'=4,'blk'=8] {'head'}, dimensions={0} | all-to-all | bytes 2097152 | tf_op jit(solution)/shard_map/all_to_all | solution.py:187
  956.6 65.0 %all_to_all.202 = bf16[32,40,1024]{2,1,0:T(8,128)(2,1)S(1)} all-to-all(bf16[32,40,1024]{2,1,0:T(8,128)(2,1)S(1)} %bitcast.617), channel_id=1, replica_groups=mesh['head'=4,'blk'=8] {'head','blk'}, dimensions={0} | all-to-all | bytes 5242880 | tf_op jit(solution)/shard_map/all_to_all | solution.py:140
  1048.1 45.2 %all-to-all-done.14 = bf16[32,40,1024]{2,1,0:T(8,128)(2,1)} async-done(((bf16[32,40,1024]{2,1,0:T(8,128)(2,1)}), bf16[32,40,1024]{2,1,0:T(8,128)(2,1)}, u32[]{:S(2)}, u32[]{:S(2)}) %all-to-all-start.14) | async-done | bytes 2621472 | tf_op jit(solution)/shard_map/all_to_all | solution.py:143
  1105.1 30.5 %all-to-all-done.24 = bf16[8,3,128,512]{3,2,1,0:T(8,128)(2,1)} async-done(((bf16[8,3,128,512]{3,2,1,0:T(8,128)(2,1)}), bf16[8,3,128,512]{3,2,1,0:T(8,128)(2,1)}, u32[]{:S(2)}, u32[]{:S(2)}) %all-to-all-start.24) | async-done | bytes 3145760 | tf_op jit(solution)/shard_map/all_to_all | solution.py:181
  1193.1 50.7 %all-to-all-start.15 = ((bf16[8,512,256]{1,2,0:T(8,128)(2,1)}), bf16[8,512,256]{1,2,0:T(8,128)(2,1)}, u32[]{:S(2)}, u32[]{:S(2)}) async-start(bf16[8,512,256]{1,2,0:T(8,128)(2,1)} %copy.176), calls=%async_computation.15 | async-start | bytes 4194304 | tf_op jit(solution)/shard_map/all_to_all | solution.py:300
  1289.3 24.2 %all-to-all-done.23 = bf16[8,3,128,512]{3,2,1,0:T(8,128)(2,1)} async-done(((bf16[8,3,128,512]{3,2,1,0:T(8,128)(2,1)}), bf16[8,3,128,512]{3,2,1,0:T(8,128)(2,1)}, u32[]{:S(2)}, u32[]{:S(2)}) %all-to-all-start.23) | async-done | bytes 3145760 | tf_op jit(solution)/shard_map/all_to_all | solution.py:181
  (642 shorter events, 478.2 us)
Async XLA Ops:
  7.2 51.2 %all-gather.24.cloned.1.call-start = ((), (), s32[]{:S(2)}) async-start(), calls=%async_computation.32 | async-start | bytes 2949120 | tf_op jit(solution)/shard_map/all_gather | solution.py:167
  29.1 63.2 %all-gather.10.cloned.1.call-start = ((), (), s32[]{:S(2)}) async-start(), calls=%async_computation.25 | async-start | bytes 1310720 | tf_op jit(solution)/shard_map/all_gather | solution.py:319
  64.1 58.9 %all-gather.12.cloned.1.call-start = ((), (), s32[]{:S(2)}) async-start(), calls=%async_computation.26 | async-start | bytes 2359296 | tf_op jit(solution)/shard_map/all_gather | solution.py:332
  95.5 52.8 %all-gather.14.cloned.1.call-start = ((), (), s32[]{:S(2)}) async-start(), calls=%async_computation.27 | async-start | bytes 1179648 | tf_op jit(solution)/shard_map/all_gather | solution.py:169
  150.7 30.7 %all-to-all-start.1 = ((bf16[4,128,1024]{2,1,0:T(8,128)(2,1)}), bf16[4,128,1024]{2,1,0:T(8,128)(2,1)S(1)}, u32[]{:S(2)}, u32[]{:S(2)}) async-start(bf16[4,128,1024]{2,1,0:T(8,128)(2,1)} %bitcast.17), calls=%async_computation.1 | async-start | bytes 2097152 | tf_op jit(solution)/shard_map/all_to_all | solution.py:187
  181.5 42.3 %all-to-all-start.3 = ((bf16[8,3,128,512]{3,2,1,0:T(8,128)(2,1)}), bf16[8,3,128,512]{3,2,1,0:T(8,128)(2,1)}, u32[]{:S(2)}, u32[]{:S(2)}) async-start(bf16[8,3,128,512]{3,2,1,0:T(8,128)(2,1)} %pad_maximum_fusion.5), calls=%async_computation.3 | async-start | bytes 6291456 | tf_op jit(solution)/shard_map/all_to_all | solution.py:174
  223.8 63.4 %all-to-all-start.2 = ((bf16[32,40,1024]{2,1,0:T(8,128)(2,1)}), bf16[32,40,1024]{2,1,0:T(8,128)(2,1)S(1)}, u32[]{:S(2)}, u32[]{:S(2)}) async-start(bf16[32,40,1024]{2,1,0:T(8,128)(2,1)} %bitcast.629), calls=%async_computation.2 | async-start | bytes 5242880 | tf_op jit(solution)/shard_map/all_to_all | solution.py:140
  297.3 64.0 %all-to-all-start.4 = ((bf16[32,40,1024]{2,1,0:T(8,128)(2,1)}), bf16[32,40,1024]{2,1,0:T(8,128)(2,1)S(1)}, u32[]{:S(2)}, u32[]{:S(2)}) async-start(bf16[32,40,1024]{2,1,0:T(8,128)(2,1)} %bitcast.652), calls=%async_computation.4 | async-start | bytes 5242880 | tf_op jit(solution)/shard_map/all_to_all | solution.py:143
  301.2 91.3 %all-gather.16.cloned.1.call-start = ((), (), s32[]{:S(2)}) async-start(), calls=%async_computation.28 | async-start | bytes 1310720 | tf_op jit(solution)/shard_map/all_gather | solution.py:319
  364.9 58.4 %all-gather.18.cloned.1.call-start = ((), (), s32[]{:S(2)}) async-start(), calls=%async_computation.29 | async-start | bytes 2359296 | tf_op jit(solution)/shard_map/all_gather | solution.py:332
  431.6 30.1 %all-to-all-start.5 = ((bf16[4,128,1024]{2,1,0:T(8,128)(2,1)}), bf16[4,128,1024]{2,1,0:T(8,128)(2,1)S(1)}, u32[]{:S(2)}, u32[]{:S(2)}) async-start(bf16[4,128,1024]{2,1,0:T(8,128)(2,1)} %bitcast.43), calls=%async_computation.5 | async-start | bytes 2097152 | tf_op jit(solution)/shard_map/all_to_all | solution.py:187
  461.7 58.8 %all-to-all-start.7 = ((bf16[8,3,128,512]{3,2,1,0:T(8,128)(2,1)}), bf16[8,3,128,512]{3,2,1,0:T(8,128)(2,1)}, u32[]{:S(2)}, u32[]{:S(2)}) async-start(bf16[8,3,128,512]{3,2,1,0:T(8,128)(2,1)} %pad_maximum_fusion.6), calls=%async_computation.7 | async-start | bytes 6291456 | tf_op jit(solution)/shard_map/all_to_all | solution.py:174
  520.5 62.9 %all-to-all-start.6 = ((bf16[32,40,1024]{2,1,0:T(8,128)(2,1)}), bf16[32,40,1024]{2,1,0:T(8,128)(2,1)S(1)}, u32[]{:S(2)}, u32[]{:S(2)}) async-start(bf16[32,40,1024]{2,1,0:T(8,128)(2,1)} %bitcast.630), calls=%async_computation.6 | async-start | bytes 5242880 | tf_op jit(solution)/shard_map/all_to_all | solution.py:140
  593.5 64.0 %all-to-all-start.8 = ((bf16[32,40,1024]{2,1,0:T(8,128)(2,1)}), bf16[32,40,1024]{2,1,0:T(8,128)(2,1)S(1)}, u32[]{:S(2)}, u32[]{:S(2)}) async-start(bf16[32,40,1024]{2,1,0:T(8,128)(2,1)} %bitcast.653), calls=%async_computation.8 | async-start | bytes 5242880 | tf_op jit(solution)/shard_map/all_to_all | solution.py:143
  736.7 63.1 %all-to-all-start.10 = ((bf16[32,40,1024]{2,1,0:T(8,128)(2,1)}), bf16[32,40,1024]{2,1,0:T(8,128)(2,1)S(1)}, u32[]{:S(2)}, u32[]{:S(2)}) async-start(bf16[32,40,1024]{2,1,0:T(8,128)(2,1)} %bitcast.58), calls=%async_computation.10 | async-start | bytes 5242880 | tf_op jit(solution)/shard_map/all_to_all | solution.py:143
  739.7 90.7 %all-gather.20.cloned.1.call-start = ((), (), s32[]{:S(2)}) async-start(), calls=%async_computation.30 | async-start | bytes 1310720 | tf_op jit(solution)/shard_map/all_gather | solution.py:440
  848.3 69.3 %all-to-all-start.11 = ((bf16[8,512,256]{1,2,0:T(8,128)(2,1)}), bf16[8,512,256]{1,2,0:T(8,128)(2,1)S(1)}, u32[]{:S(2)}, u32[]{:S(2)}) async-start(bf16[8,512,256]{1,2,0:T(8,128)(2,1)} %copy.174), calls=%async_computation.11 | async-start | bytes 4194304 | tf_op jit(solution)/shard_map/all_to_all | solution.py:300
  1029.3 64.0 %all-to-all-start.14 = ((bf16[32,40,1024]{2,1,0:T(8,128)(2,1)}), bf16[32,40,1024]{2,1,0:T(8,128)(2,1)}, u32[]{:S(2)}, u32[]{:S(2)}) async-start(bf16[32,40,1024]{2,1,0:T(8,128)(2,1)} %bitcast.74), calls=%async_computation.14 | async-start | bytes 5242880 | tf_op jit(solution)/shard_map/all_to_all | solution.py:143
  1093.3 42.3 %all-to-all-start.24 = ((bf16[8,3,128,512]{3,2,1,0:T(8,128)(2,1)}), bf16[8,3,128,512]{3,2,1,0:T(8,128)(2,1)}, u32[]{:S(2)}, u32[]{:S(2)}) async-start(bf16[8,3,128,512]{3,2,1,0:T(8,128)(2,1)} %copy.197), calls=%async_computation.24 | async-start | bytes 6291456 | tf_op jit(solution)/shard_map/all_to_all | solution.py:181
  1097.8 64.0 %all-gather.22.cloned.1.call-start = ((), (), s32[]{:S(2)}) async-start(), calls=%async_computation.31 | async-start | bytes 1310720 | tf_op jit(solution)/shard_map/all_gather | solution.py:440
  1170.5 22.7 %all-to-all-start.20 = ((bf16[4,32,640]{2,1,0:T(8,128)(2,1)}), bf16[4,32,640]{2,1,0:T(8,128)(2,1)}, u32[]{:S(2)}, u32[]{:S(2)}) async-start(bf16[4,32,640]{2,1,0:T(8,128)(2,1)} %reduce_sum.383), calls=%async_computation.20 | async-start | bytes 327680 | tf_op jit(solution)/shard_map/all_to_all | solution.py:480
  1193.1 77.7 %all-to-all-start.15 = ((bf16[8,512,256]{1,2,0:T(8,128)(2,1)}), bf16[8,512,256]{1,2,0:T(8,128)(2,1)}, u32[]{:S(2)}, u32[]{:S(2)}) async-start(bf16[8,512,256]{1,2,0:T(8,128)(2,1)} %copy.176), calls=%async_computation.15 | async-start | bytes 4194304 | tf_op jit(solution)/shard_map/all_to_all | solution.py:300
  1270.9 42.6 %all-to-all-start.23 = ((bf16[8,3,128,512]{3,2,1,0:T(8,128)(2,1)}), bf16[8,3,128,512]{3,2,1,0:T(8,128)(2,1)}, u32[]{:S(2)}, u32[]{:S(2)}) async-start(bf16[8,3,128,512]{3,2,1,0:T(8,128)(2,1)} %copy.193), calls=%async_computation.23 | async-start | bytes 6291456 | tf_op jit(solution)/shard_map/all_to_all | solution.py:181
  1313.5 27.7 %all-to-all-start.16 = ((bf16[4,128,1024]{2,1,0:T(8,128)(2,1)}), bf16[4,128,1024]{2,1,0:T(8,128)(2,1)}, u32[]{:S(2)}, u32[]{:S(2)}) async-start(bf16[4,128,1024]{2,1,0:T(8,128)(2,1)} %bitcast.669), calls=%async_computation.16 | async-start | bytes 2097152 | tf_op jit(solution)/shard_map/all_to_all | solution.py:187
  (165 other events, 4685.1 us)
Sparse Core Ops, SparseCore 0:
  29.2 29.0 all-gather.23
  64.3 27.9 all-gather.9
  95.6 27.4 all-gather.11
  124.8 23.3 all-gather.13
  365.1 27.4 all-gather.15
  395.8 27.4 all-gather.17
  803.0 27.4 all-gather.19
  1103.8 27.5 all-gather.21

commit v2 on v1

--- a/solution.py
+++ b/solution.py
@@ -164,21 +164,29 @@
     )
     sent = jnp.transpose(sent, (2, 0, 1, 3))
     sent = lax.all_to_all(sent, "head", split_axis=0, concat_axis=0, tiled=True)
-    attn_all = lax.all_gather(sent, "blk", axis=0, tiled=False)
-    attn_all = jnp.transpose(attn_all, (2, 1, 0, 3, 4)).reshape(LAYERS, D, qkv_cols + SIDE)
+    attn_all = []
+    for layer_index in range(LAYERS):
+        mats = lax.all_gather(sent[:, layer_index], "blk", axis=0, tiled=False)
+        attn_all.append(jnp.transpose(mats, (1, 0, 2, 3)).reshape(D, qkv_cols + SIDE))
     out_all = lax.all_gather(w_out, "blk", axis=1, tiled=True)
-
-    def gather_experts(layer_index):
+    tokens_block = lax.all_gather(tokens, "head", axis=0, tiled=True).astype(jnp.float32)
+
+    def exchange_experts(layer_index):
         mats = jnp.stack([w_gate[layer_index], w_up[layer_index], w_down[layer_index]], axis=1)
         mats = jnp.repeat(mats, copies, axis=0)
-        mats = lax.all_to_all(mats, "blk", split_axis=0, concat_axis=0, tiled=True)
-        return jnp.transpose(mats, (1, 0, 2, 3)).reshape(3, D, hidden_units)
-
-    def scatter_experts(grads):
+        return lax.all_to_all(mats, "blk", split_axis=0, concat_axis=0, tiled=True)
+
+    def expert_parts(mats):
+        mats = jnp.transpose(mats, (1, 0, 2, 3)).reshape(3, D, hidden_units)
+        return (mats[0], mats[1], mats[2])
+
+    def exchange_grads(grads):
         grads = jnp.stack(grads).astype(jnp.bfloat16)
         grads = grads.reshape(3, cycle_count, slice_rows, hidden_units)
         grads = jnp.transpose(grads, (1, 0, 2, 3))
-        grads = lax.all_to_all(grads, "blk", split_axis=0, concat_axis=0, tiled=True)
+        return lax.all_to_all(grads, "blk", split_axis=0, concat_axis=0, tiled=True)
+
+    def grad_parts(grads):
         grads = grads.reshape(local_experts, copies, 3, slice_rows, hidden_units)
         grads = jnp.sum(grads.astype(jnp.float32), axis=1)
         return (grads[:, 0], grads[:, 1], grads[:, 2])
@@ -246,7 +254,7 @@
         )
         return (attended, running_max + jnp.log(running_sum))
 
-    def attend_back(queries, keys_all, attended, log_total, grad_attended):
+    def attend_back(queries, keys_all, attended, log_total, grad_attended, beside):
         query_four = queries.reshape(block_rows, key_heads, groups, HD)
         grad_four = grad_attended.reshape(block_rows, key_heads, groups, HD)
         row_delta = jnp.transpose(
@@ -297,26 +305,31 @@
             jnp.zeros((cycle_count * block_rows, 2 * key_cols), jnp.bfloat16),
         )
         grad_query, key_grads = lax.fori_loop(first_owner, cycle_index + 1, visit, start_state)
+        grad_query, key_grads, beside = lax.optimization_barrier((grad_query, key_grads, beside))
         key_grads = lax.all_to_all(key_grads, "blk", split_axis=0, concat_axis=0, tiled=True)
         key_grads = jnp.sum(
             key_grads.reshape(cycle_count, block_rows, 2 * key_cols).astype(jnp.float32), axis=0
         ).astype(jnp.bfloat16)
         grad_query = (grad_query * score_scale).astype(jnp.bfloat16)
-        return (grad_query.reshape(block_rows, query_cols), key_grads)
+        return (grad_query.reshape(block_rows, query_cols), key_grads, beside)
 
     stream = tokens.astype(jnp.float32)
     saved = []
     for layer_index in range(LAYERS):
-        qkv_mat = attn_all[layer_index, :, :qkv_cols]
-        side_all = attn_all[layer_index, :, qkv_cols:]
+        qkv_mat = attn_all[layer_index][:, :qkv_cols]
+        side_all = attn_all[layer_index][:, qkv_cols:]
         router = side_all[:, :E]
         gain_first = side_all[:, E].astype(jnp.float32)
         gain_second = side_all[:, E + 1].astype(jnp.float32)
         out_mat = out_all[layer_index]
-        gate_mat, up_mat, down_mat = gather_experts(layer_index)
         scale_first = rms_scale(stream)
-        normed_attn = (stream * scale_first * gain_first).astype(jnp.bfloat16)
-        normed_block = lax.all_gather(normed_attn, "head", axis=0, tiled=True)
+        if layer_index == 0:
+            normed_block = (tokens_block * rms_scale(tokens_block) * gain_first).astype(
+                jnp.bfloat16
+            )
+        else:
+            normed_attn = (stream * scale_first * gain_first).astype(jnp.bfloat16)
+            normed_block = lax.all_gather(normed_attn, "head", axis=0, tiled=True)
         qkv_pre = dot(normed_block, qkv_mat)
         query_pre = qkv_pre[:, :query_cols].reshape(block_rows, H // head_count, HD)
         key_pre = qkv_pre[:, query_cols : query_cols + key_cols].reshape(block_rows, key_heads, HD)
@@ -331,6 +344,10 @@
         ).astype(jnp.bfloat16)
         keys_all = lax.all_gather(key_value, "blk", axis=0, tiled=True)
         attended, log_total = attend(queries, keys_all)
+        attended, expert_mats = lax.optimization_barrier(
+            (attended, exchange_experts(layer_index))
+        )
+        gate_mat, up_mat, down_mat = expert_parts(expert_mats)
         middle = stream + sum_over_head(dot(attended, out_mat))
         scale_second = rms_scale(middle)
         normed_ffn = (middle * scale_second * gain_second).astype(jnp.bfloat16)
@@ -373,6 +390,9 @@
         stream = middle + contract_rows(gate_high, returned) + contract_rows(gate_low, returned)
     grad_stream = cotangent.astype(jnp.float32)
     layer_grads = [None] * LAYERS
+    mats_grads = [None] * LAYERS
+    out_grads = [None] * LAYERS
+    earlier_sums = ()
     for layer_index in range(LAYERS - 1, -1, -1):
         (
             stream_in,
@@ -412,7 +432,7 @@
             contract_cols(grad_gate_pre, gate_mat) + contract_cols(grad_up_pre, up_mat)
         ).astype(jnp.bfloat16)
         grad_rows = from_experts(grad_arrived)
-        expert_grads = scatter_experts(
+        expert_grads = exchange_grads(
             [
                 contract_rows(arrived, grad_gate_pre),
                 contract_rows(arrived, grad_up_pre),
@@ -442,7 +462,11 @@
         )
         grad_out = contract_rows(attended, branch_block)
         grad_attended = contract_cols(branch_block, out_mat).astype(jnp.bfloat16)
-        grad_query, grad_kv = attend_back(queries, keys_all, attended, log_total, grad_attended)
+        grad_query, grad_kv, (expert_grads, earlier_sums) = attend_back(
+            queries, keys_all, attended, log_total, grad_attended, (expert_grads, earlier_sums)
+        )
+        if earlier_sums:
+            mats_grads[layer_index + 1], out_grads[layer_index + 1] = earlier_sums
         grad_query_pre = (
             rotate(
                 grad_query.reshape(block_rows, H // head_count, HD).astype(jnp.float32),
@@ -462,8 +486,12 @@
             .reshape(block_rows, key_cols)
         )
         grad_qkv = jnp.concatenate([grad_query_pre, grad_key_pre, grad_kv[:, key_cols:]], axis=1)
-        grad_normed = sum_over_head(contract_cols(grad_qkv, qkv_mat))
-        grad_first, grad_gain_first = norm_back(stream_in, scale_first, gain_first, grad_normed)
+        grad_partial = contract_cols(grad_qkv, qkv_mat)
+        grad_normed = sum_over_head(grad_partial)
+        grad_gain_first = (
+            jnp.sum(grad_partial * normed_block.astype(jnp.float32), axis=0) / gain_first
+        )
+        grad_first = norm_back(stream_in, scale_first, gain_first, grad_normed)[0]
         grad_stream = grad_stream + grad_first
         grad_side = jnp.concatenate(
             [grad_router, grad_gain_first[:, None], grad_gain_second[:, None]], axis=1
@@ -474,38 +502,45 @@
         ).astype(jnp.bfloat16)
         grad_mats = jnp.transpose(
             grad_mats.reshape(head_count, cycle_count, shard_rows, qkv_cols + SIDE), (1, 0, 2, 3)
-        )
-        grad_mats = lax.all_to_all(grad_mats, "blk", split_axis=0, concat_axis=0, tiled=True)
-        grad_mats = jnp.sum(grad_mats.astype(jnp.float32), axis=0).astype(jnp.bfloat16)
-        grad_mats = lax.all_to_all(grad_mats, "head", split_axis=0, concat_axis=0, tiled=True)
-        grad_mats = grad_mats.astype(jnp.float32)
-        grad_out = lax.all_to_all(
-            grad_out.astype(jnp.bfloat16).reshape(cycle_count, shard_rows, D),
-            "blk",
-            split_axis=0,
-            concat_axis=0,
-            tiled=True,
-        )
-        grad_out = jnp.sum(grad_out.astype(jnp.float32), axis=0)
-
-        def joined(start, stop):
-            return jnp.transpose(grad_mats[:, :, start:stop], (1, 0, 2)).reshape(shard_rows, -1)
-
-        grad_side = jnp.sum(grad_mats[:, :, qkv_cols:], axis=0)
-        layer_grads[layer_index] = (
-            joined(0, query_cols),
-            joined(query_cols, query_cols + key_cols),
-            joined(query_cols + key_cols, qkv_cols),
-            grad_out,
-            grad_side[:, :E],
-            grad_side[:, E],
-            grad_side[:, E + 1],
-        ) + expert_grads
-    stacked = [
+        ).reshape(cycle_count * head_count * shard_rows, qkv_cols + SIDE)
+        grad_mats = lax.psum_scatter(grad_mats, "blk", scatter_dimension=0, tiled=True)
+        grad_out = lax.psum_scatter(
+            grad_out.astype(jnp.bfloat16), "blk", scatter_dimension=0, tiled=True
+        )
+        earlier_sums = (grad_mats, grad_out)
+        layer_grads[layer_index] = grad_parts(expert_grads)
+    mats_grads[0], out_grads[0] = earlier_sums
+    mats_grads = jnp.stack(
+        [sums.reshape(head_count, shard_rows, qkv_cols + SIDE) for sums in mats_grads], axis=1
+    )
+    mats_grads = lax.all_to_all(
+        mats_grads, "head", split_axis=0, concat_axis=0, tiled=True
+    ).astype(jnp.float32)
+
+    def joined(start, stop):
+        return jnp.transpose(mats_grads[..., start:stop], (1, 2, 0, 3)).reshape(
+            LAYERS, shard_rows, -1
+        )
+
+    grad_side = jnp.sum(mats_grads[..., qkv_cols:], axis=0)
+    gate_grads, up_grads, down_grads = [
         jnp.stack([layer_grads[layer_index][member] for layer_index in range(LAYERS)])
-        for member in range(10)
+        for member in range(3)
     ]
-    return (stream, grad_stream, *stacked)
+    return (
+        stream,
+        grad_stream,
+        joined(0, query_cols),
+        joined(query_cols, query_cols + key_cols),
+        joined(query_cols + key_cols, qkv_cols),
+        jnp.stack(out_grads).astype(jnp.float32),
+        grad_side[..., :E],
+        grad_side[..., E],
+        grad_side[..., E + 1],
+        gate_grads,
+        up_grads,
+        down_grads,
+    )
 
 
 def solution(mesh):

time: 1410 us -> 1300 us (0.922)
  starting transfers between devices: 186 us -> 101 us
  waiting for transfers between devices: 758 us -> 703 us
  local copies, waits for them, and re-layouts: 73.9 us -> 89 us
    all_to_all x10 -> x5, waiting for transfers between devices: 159 us -> 40 us  [the longest x2 20.2 us: exchange_grads(): return lax.all_to_all(grads, 'blk', split_axis=0, concat_axis=0, tiled=True)]
    reduce_scatter x0 -> x4, waiting for transfers between devices: none -> 83.1 us  [the longest x2 60.4 us: per_device(): lax.psum_scatter(grad_mats, 'blk', scatter_dimension=0, tiled=True)]
    all_to_all x2, starting transfers between devices: 93.4 us -> 22 us  [attend_back(): lax.all_to_all(key_grads, 'blk', split_axis=0, concat_axis=0, tiled=True)]
    all_gather x1 -> x3, waiting for transfers between devices: 29 us -> 70.6 us  [the longest x2 63.6 us: per_device(): mats = lax.all_gather(sent[:, layer_index], 'blk', axis=0, tiled=False)]
    all_to_all x10 -> x5, starting transfers between devices: 57.8 us -> 23.1 us  [the longest x2 9.35 us: exchange_grads(): return lax.all_to_all(grads, 'blk', split_axis=0, concat_axis=0, tiled=True)]
    all_to_all x4, waiting for transfers between devices: 218 us -> 186 us  [from_experts(): rows = lax.all_to_all(rows, BOTH, split_axis=0, concat_axis=0, tiled=True)]
    all_gather x2 -> x1, waiting for transfers between devices: 54.7 us -> 27.4 us  [per_device(): normed_block = lax.all_gather(normed_attn, 'head', axis=0, tiled=True)]
    all_gather x2, waiting for transfers between devices: 26.9 us -> 4.36 us  [per_device(): lax.all_gather(grad_stream.astype(jnp.bfloat16), 'head', axis=0, tiled=True)]
  transfers between devices with their start and end apart: 29 -> 29, of which waited for: 27 -> 26; matrix products, arithmetic and copies ran while one was open for 10% -> 13% of each run, Pallas kernels for 0% -> 0%
where the time goes in v2:
time: 1300 us; the launch traced here: 1290 us
  waiting for transfers between devices  703 us (54%)
  blocking collectives  181 us (14%)
  matrix products  136 us (10%)
  starting transfers between devices  101 us (8%)
  local copies, waits for them, and re-layouts  89 us (7%)
  other arithmetic  54.9 us (4%)
  between operations  18.8 us (1%)
    all_to_all x4, waiting for transfers between devices, from_experts(): rows = lax.all_to_all(rows, BOTH, split_axis=0, concat_axis=0, tiled=True)  186 us
    all_to_all x2, blocking collectives, to_experts(): return lax.all_to_all(rows, BOTH, split_axis=0, concat_axis=0, tiled=True)  130 us
    all_to_all x2, waiting for transfers between devices, to_experts(): return lax.all_to_all(rows, BOTH, split_axis=0, concat_axis=0, tiled=True)  113 us
    all_gather x2, waiting for transfers between devices, per_device(): mats = lax.all_gather(sent[:, layer_index], 'blk', axis=0, tiled=False)  63.6 us
    all_gather x2, waiting for transfers between devices, per_device(): keys_all = lax.all_gather(key_value, 'blk', axis=0, tiled=True)  63.3 us
    reduce_scatter x2, waiting for transfers between devices, per_device(): lax.psum_scatter(grad_mats, 'blk', scatter_dimension=0, tiled=True)  60.4 us
    all_to_all x3, waiting for transfers between devices, sum_over_head(): lax.all_to_all(partial.astype(jnp.bfloat16), 'head', split_axis=0, concat...  58.8 us
    dot_general x17, matrix products, dot(): return jnp.dot(left, right, preferred_element_type=jnp.float32)  46.4 us
  transfers between devices with their start and end apart: 29, of which 26 were waited for; matrix products, arithmetic and copies ran while one was open for 13% of the time, Pallas kernels for 0%

profile of v2, /device:TPU:0, one launch (start us, length us, event | category | flops | bytes accessed | tf_op | source)
XLA Modules:
  0.0 1288.1 jit_solution(7409067074935295308)
XLA Ops:
  13.3 24.9 %all_to_all.174 = bf16[4,2,32,640]{3,2,1,0:T(8,128)(2,1)S(1)} all-to-all(bf16[4,2,32,640]{3,2,1,0:T(8,128)(2,1)S(1)} %copy.177), channel_id=1, replica_groups=mesh['head'=4,'blk'=8] {'head'}, dimensions={0} | all-to-all | bytes 655360 | tf_op jit(solution)/shard_map/all_to_all | solution.py:166
  48.4 24.5 %all-gather.26.cloned.1.call-done = bf16[32,1,32,640]{3,2,1,0:T(8,128)(2,1)} async-done(((bf16[4,1,32,640]{3,2,1,0:T(8,128)(2,1)}), bf16[32,1,32,640]{3,2,1,0:T(8,128)(2,1)}) %all-gather.26.cloned.1.call-update) | async-done | bytes 1310736 | tf_op jit(solution)/shard_map/all_gather | solution.py:169
  93.4 27.6 %all-gather.14.cloned.1.call-done = bf16[4096,256]{0,1:T(8,128)(2,1)} async-done(((bf16[512,256]{0,1:T(8,128)(2,1)}), bf16[4096,256]{0,1:T(8,128)(2,1)}) %all-gather.14.cloned.1.call-update) | async-done | bytes 2097168 | tf_op jit(solution)/shard_map/all_gather | solution.py:345
  153.7 25.3 %all-to-all-done.2 = bf16[4,128,1024]{2,1,0:T(8,128)(2,1)} async-done(((bf16[4,128,1024]{2,1,0:T(8,128)(2,1)}), bf16[4,128,1024]{2,1,0:T(8,128)(2,1)}, u32[]{:S(2)}, u32[]{:S(2)}) %all-to-all-start.2) | async-done | bytes 1048608 | tf_op jit(solution)/shard_map/all_to_all | solution.py:195
  190.0 56.5 %all-to-all-done.3 = bf16[32,40,1024]{2,1,0:T(8,128)(2,1)S(1)} async-done(((bf16[32,40,1024]{2,1,0:T(8,128)(2,1)}), bf16[32,40,1024]{2,1,0:T(8,128)(2,1)S(1)}, u32[]{:S(2)}, u32[]{:S(2)}) %all-to-all-start.3) | async-done | bytes 2621472 | tf_op jit(solution)/shard_map/all_to_all | solution.py:140
  261.3 39.0 %all-gather.28.cloned.1.call-done = bf16[32,1,32,640]{3,2,1,0:T(8,128)(2,1)} async-done(((bf16[4,1,32,640]{3,2,1,0:T(8,128)(2,1)}), bf16[32,1,32,640]{3,2,1,0:T(8,128)(2,1)}) %all-gather.28.cloned.1.call-update) | async-done | bytes 1310736 | tf_op jit(solution)/shard_map/all_gather | solution.py:169
  324.5 27.4 %all-gather.18.cloned.1.call-done = bf16[512,1024]{1,0:T(8,128)(2,1)} async-done(((bf16[128,1024]{1,0:T(8,128)(2,1)}), bf16[512,1024]{1,0:T(8,128)(2,1)}) %all-gather.18.cloned.1.call-update) | async-done | bytes 1048592 | tf_op jit(solution)/shard_map/all_gather | solution.py:332
  364.7 35.7 %all-gather.20.cloned.1.call-done = bf16[4096,256]{0,1:T(8,128)(2,1)} async-done(((bf16[512,256]{0,1:T(8,128)(2,1)}), bf16[4096,256]{0,1:T(8,128)(2,1)}) %all-gather.20.cloned.1.call-update) | async-done | bytes 2097168 | tf_op jit(solution)/shard_map/all_gather | solution.py:345
  416.1 24.9 %all-to-all-done.6 = bf16[4,128,1024]{2,1,0:T(8,128)(2,1)S(1)} async-done(((bf16[4,128,1024]{2,1,0:T(8,128)(2,1)}), bf16[4,128,1024]{2,1,0:T(8,128)(2,1)S(1)}, u32[]{:S(2)}, u32[]{:S(2)}) %all-to-all-start.6) | async-done | bytes 1048608 | tf_op jit(solution)/shard_map/all_to_all | solution.py:195
  443.9 23.3 %all-to-all-start.7 = ((bf16[32,40,1024]{2,1,0:T(8,128)(2,1)}), bf16[32,40,1024]{2,1,0:T(8,128)(2,1)S(1)}, u32[]{:S(2)}, u32[]{:S(2)}) async-start(bf16[32,40,1024]{2,1,0:T(8,128)(2,1)} %bitcast.631), calls=%async_computation.7 | async-start | bytes 5242880 | tf_op jit(solution)/shard_map/all_to_all | solution.py:140
  470.7 56.5 %all-to-all-done.7 = bf16[32,40,1024]{2,1,0:T(8,128)(2,1)S(1)} async-done(((bf16[32,40,1024]{2,1,0:T(8,128)(2,1)}), bf16[32,40,1024]{2,1,0:T(8,128)(2,1)S(1)}, u32[]{:S(2)}, u32[]{:S(2)}) %all-to-all-start.7) | async-done | bytes 2621472 | tf_op jit(solution)/shard_map/all_to_all | solution.py:140
  546.9 54.6 %all-to-all-done.8 = bf16[32,40,1024]{2,1,0:T(8,128)(2,1)S(1)} async-done(((bf16[32,40,1024]{2,1,0:T(8,128)(2,1)}), bf16[32,40,1024]{2,1,0:T(8,128)(2,1)S(1)}, u32[]{:S(2)}, u32[]{:S(2)}) %all-to-all-start.8) | async-done | bytes 2621472 | tf_op jit(solution)/shard_map/all_to_all | solution.py:143
  609.6 64.6 %all_to_all.175 = bf16[32,40,1024]{2,1,0:T(8,128)(2,1)S(1)} all-to-all(bf16[32,40,1024]{2,1,0:T(8,128)(2,1)S(1)} %bitcast.619), channel_id=1, replica_groups=mesh['head'=4,'blk'=8] {'head','blk'}, dimensions={0} | all-to-all | bytes 5242880 | tf_op jit(solution)/shard_map/all_to_all | solution.py:140
  686.1 59.4 %all-to-all-done.10 = bf16[32,40,1024]{2,1,0:T(8,128)(2,1)} async-done(((bf16[32,40,1024]{2,1,0:T(8,128)(2,1)}), bf16[32,40,1024]{2,1,0:T(8,128)(2,1)}, u32[]{:S(2)}, u32[]{:S(2)}) %all-to-all-start.10) | async-done | bytes 2621472 | tf_op jit(solution)/shard_map/all_to_all | solution.py:143
  792.6 20.2 %all-to-all-done.11 = bf16[8,3,128,512]{3,2,1,0:T(8,128)(2,1)} async-done(((bf16[8,3,128,512]{3,2,1,0:T(8,128)(2,1)}), bf16[8,3,128,512]{3,2,1,0:T(8,128)(2,1)}, u32[]{:S(2)}, u32[]{:S(2)}) %all-to-all-start.11) | async-done | bytes 3145760 | tf_op jit(solution)/shard_map/all_to_all | solution.py:187
  820.7 17.5 %all-to-all-start.12 = ((bf16[8,512,256]{1,2,0:T(8,128)(2,1)}), bf16[8,512,256]{1,2,0:T(8,128)(2,1)}, u32[]{:S(2)}, u32[]{:S(2)}) async-start(bf16[8,512,256]{1,2,0:T(8,128)(2,1)} %copy.186), calls=%async_computation.12 | async-start | bytes 4194304 | tf_op jit(solution)/shard_map/all_to_all | solution.py:309
  838.5 26.8 %all-to-all-done.12 = bf16[8,512,256]{1,2,0:T(8,128)(2,1)} async-done(((bf16[8,512,256]{1,2,0:T(8,128)(2,1)}), bf16[8,512,256]{1,2,0:T(8,128)(2,1)}, u32[]{:S(2)}, u32[]{:S(2)}) %all-to-all-start.12) | async-done | bytes 2097184 | tf_op jit(solution)/shard_map/all_to_all | solution.py:309
  870.5 26.1 %all_to_all.176 = bf16[4,128,1024]{2,1,0:T(8,128)(2,1)S(1)} all-to-all(bf16[4,128,1024]{2,1,0:T(8,128)(2,1)S(1)} %bitcast.686), channel_id=1, replica_groups=mesh['head'=4,'blk'=8] {'head'}, dimensions={0} | all-to-all | bytes 2097152 | tf_op jit(solution)/shard_map/all_to_all | solution.py:195
  906.3 65.4 %all_to_all.177 = bf16[32,40,1024]{2,1,0:T(8,128)(2,1)S(1)} all-to-all(bf16[32,40,1024]{2,1,0:T(8,128)(2,1)S(1)} %bitcast.618), channel_id=1, replica_groups=mesh['head'=4,'blk'=8] {'head','blk'}, dimensions={0} | all-to-all | bytes 5242880 | tf_op jit(solution)/shard_map/all_to_all | solution.py:140
  983.0 60.1 %all-to-all-done.15 = bf16[32,40,1024]{2,1,0:T(8,128)(2,1)} async-done(((bf16[32,40,1024]{2,1,0:T(8,128)(2,1)}), bf16[32,40,1024]{2,1,0:T(8,128)(2,1)}, u32[]{:S(2)}, u32[]{:S(2)}) %all-to-all-start.15) | async-done | bytes 2621472 | tf_op jit(solution)/shard_map/all_to_all | solution.py:143
  1100.8 22.7 %reduce-scatter.7.cloned.1.call-done = bf16[32,1024]{1,0:T(8,128)(2,1)} async-done(((bf16[256,1024]{1,0:T(8,128)(2,1)}), bf16[32,1024]{1,0:T(8,128)(2,1)}) %reduce-scatter.7.cloned.1.call-update) | async-done | bytes 65552 | tf_op jit(solution)/shard_map/reduce_scatter | solution.py:507
  1123.5 39.4 %reduce-scatter.5.cloned.1.call-done = bf16[128,640]{1,0:T(8,128)(2,1)} async-done(((bf16[1024,640]{1,0:T(8,128)(2,1)}), bf16[128,640]{1,0:T(8,128)(2,1)}) %reduce-scatter.5.cloned.1.call-update) | async-done | bytes 163856 | tf_op jit(solution)/shard_map/reduce_scatter | solution.py:506
  1186.0 16.0 %all-to-all-done.17 = bf16[8,512,256]{1,2,0:T(8,128)(2,1)} async-done(((bf16[8,512,256]{1,2,0:T(8,128)(2,1)}), bf16[8,512,256]{1,2,0:T(8,128)(2,1)}, u32[]{:S(2)}, u32[]{:S(2)}) %all-to-all-start.17) | async-done | bytes 2097184 | tf_op jit(solution)/shard_map/all_to_all | solution.py:309
  1240.8 21.0 %reduce-scatter.9.cloned.1.call-done = bf16[128,640]{1,0:T(8,128)(2,1)} async-done(((bf16[1024,640]{1,0:T(8,128)(2,1)}), bf16[128,640]{1,0:T(8,128)(2,1)}) %reduce-scatter.9.cloned.1.call-update) | async-done | bytes 163856 | tf_op jit(solution)/shard_map/reduce_scatter | solution.py:506
  (618 shorter events, 437.9 us)
Async XLA Ops:
  7.2 39.7 %all-gather.12.cloned.1.call-start = ((), (), s32[]{:S(2)}) async-start(), calls=%async_computation.24 | async-start | bytes 1310720 | tf_op jit(solution)/shard_map/all_gather | solution.py:172
  7.9 65.0 %all-gather.26.cloned.1.call-start = ((), (), s32[]{:S(2)}) async-start(), calls=%async_computation.35 | async-start | bytes 1474560 | tf_op jit(solution)/shard_map/all_gather | solution.py:169
  38.9 82.1 %all-gather.14.cloned.1.call-start = ((), (), s32[]{:S(2)}) async-start(), calls=%async_computation.25 | async-start | bytes 2359296 | tf_op jit(solution)/shard_map/all_gather | solution.py:345
  85.3 48.8 %all-to-all-start.1 = ((bf16[8,3,128,512]{3,2,1,0:T(8,128)(2,1)}), bf16[8,3,128,512]{3,2,1,0:T(8,128)(2,1)}, u32[]{:S(2)}, u32[]{:S(2)}) async-start(bf16[8,3,128,512]{3,2,1,0:T(8,128)(2,1)} %pad_maximum_fusion.3), calls=%async_computation.1 | async-start | bytes 6291456 | tf_op jit(solution)/shard_map/all_to_all | solution.py:177
  89.9 55.8 %all-gather.16.cloned.1.call-start = ((), (), s32[]{:S(2)}) async-start(), calls=%async_computation.26 | async-start | bytes 1179648 | tf_op jit(solution)/shard_map/all_gather | solution.py:171
  183.2 63.3 %all-to-all-start.3 = ((bf16[32,40,1024]{2,1,0:T(8,128)(2,1)}), bf16[32,40,1024]{2,1,0:T(8,128)(2,1)S(1)}, u32[]{:S(2)}, u32[]{:S(2)}) async-start(bf16[32,40,1024]{2,1,0:T(8,128)(2,1)} %bitcast.630), calls=%async_computation.3 | async-start | bytes 5242880 | tf_op jit(solution)/shard_map/all_to_all | solution.py:140
  256.6 64.2 %all-to-all-start.4 = ((bf16[32,40,1024]{2,1,0:T(8,128)(2,1)}), bf16[32,40,1024]{2,1,0:T(8,128)(2,1)S(1)}, u32[]{:S(2)}, u32[]{:S(2)}) async-start(bf16[32,40,1024]{2,1,0:T(8,128)(2,1)} %bitcast.665), calls=%async_computation.4 | async-start | bytes 5242880 | tf_op jit(solution)/shard_map/all_to_all | solution.py:143
  260.6 39.7 %all-gather.28.cloned.1.call-start = ((), (), s32[]{:S(2)}) async-start(), calls=%async_computation.36 | async-start | bytes 1474560 | tf_op jit(solution)/shard_map/all_gather | solution.py:169
  261.2 90.7 %all-gather.18.cloned.1.call-start = ((), (), s32[]{:S(2)}) async-start(), calls=%async_computation.27 | async-start | bytes 1310720 | tf_op jit(solution)/shard_map/all_gather | solution.py:332
  324.5 75.9 %all-gather.20.cloned.1.call-start = ((), (), s32[]{:S(2)}) async-start(), calls=%async_computation.28 | async-start | bytes 2359296 | tf_op jit(solution)/shard_map/all_gather | solution.py:345
  359.3 49.5 %all-to-all-start.5 = ((bf16[8,3,128,512]{3,2,1,0:T(8,128)(2,1)}), bf16[8,3,128,512]{3,2,1,0:T(8,128)(2,1)}, u32[]{:S(2)}, u32[]{:S(2)}) async-start(bf16[8,3,128,512]{3,2,1,0:T(8,128)(2,1)} %pad_maximum_fusion.4), calls=%async_computation.5 | async-start | bytes 6291456 | tf_op jit(solution)/shard_map/all_to_all | solution.py:177
  443.9 83.4 %all-to-all-start.7 = ((bf16[32,40,1024]{2,1,0:T(8,128)(2,1)}), bf16[32,40,1024]{2,1,0:T(8,128)(2,1)S(1)}, u32[]{:S(2)}, u32[]{:S(2)}) async-start(bf16[32,40,1024]{2,1,0:T(8,128)(2,1)} %bitcast.631), calls=%async_computation.7 | async-start | bytes 5242880 | tf_op jit(solution)/shard_map/all_to_all | solution.py:140
  537.3 64.1 %all-to-all-start.8 = ((bf16[32,40,1024]{2,1,0:T(8,128)(2,1)}), bf16[32,40,1024]{2,1,0:T(8,128)(2,1)S(1)}, u32[]{:S(2)}, u32[]{:S(2)}) async-start(bf16[32,40,1024]{2,1,0:T(8,128)(2,1)} %bitcast.666), calls=%async_computation.8 | async-start | bytes 5242880 | tf_op jit(solution)/shard_map/all_to_all | solution.py:143
  681.8 63.7 %all-to-all-start.10 = ((bf16[32,40,1024]{2,1,0:T(8,128)(2,1)}), bf16[32,40,1024]{2,1,0:T(8,128)(2,1)}, u32[]{:S(2)}, u32[]{:S(2)}) async-start(bf16[32,40,1024]{2,1,0:T(8,128)(2,1)} %bitcast.616), calls=%async_computation.10 | async-start | bytes 5242880 | tf_op jit(solution)/shard_map/all_to_all | solution.py:143
  685.3 93.9 %all-gather.22.cloned.1.call-start = ((), (), s32[]{:S(2)}) async-start(), calls=%async_computation.29 | async-start | bytes 1310720 | tf_op jit(solution)/shard_map/all_gather | solution.py:460
  770.3 42.4 %all-to-all-start.11 = ((bf16[8,3,128,512]{3,2,1,0:T(8,128)(2,1)}), bf16[8,3,128,512]{3,2,1,0:T(8,128)(2,1)}, u32[]{:S(2)}, u32[]{:S(2)}) async-start(bf16[8,3,128,512]{3,2,1,0:T(8,128)(2,1)} %copy.184), calls=%async_computation.11 | async-start | bytes 6291456 | tf_op jit(solution)/shard_map/all_to_all | solution.py:187
  820.7 44.6 %all-to-all-start.12 = ((bf16[8,512,256]{1,2,0:T(8,128)(2,1)}), bf16[8,512,256]{1,2,0:T(8,128)(2,1)}, u32[]{:S(2)}, u32[]{:S(2)}) async-start(bf16[8,512,256]{1,2,0:T(8,128)(2,1)} %copy.186), calls=%async_computation.12 | async-start | bytes 4194304 | tf_op jit(solution)/shard_map/all_to_all | solution.py:309
  979.4 63.7 %all-to-all-start.15 = ((bf16[32,40,1024]{2,1,0:T(8,128)(2,1)}), bf16[32,40,1024]{2,1,0:T(8,128)(2,1)}, u32[]{:S(2)}, u32[]{:S(2)}) async-start(bf16[32,40,1024]{2,1,0:T(8,128)(2,1)} %bitcast.617), calls=%async_computation.15 | async-start | bytes 5242880 | tf_op jit(solution)/shard_map/all_to_all | solution.py:143
  982.9 100.5 %all-gather.24.cloned.1.call-start = ((), (), s32[]{:S(2)}) async-start(), calls=%async_computation.30 | async-start | bytes 1310720 | tf_op jit(solution)/shard_map/all_gather | solution.py:460
  1048.8 74.7 %reduce-scatter.7.cloned.1.call-start = ((), (), s32[]{:S(2)}) async-start(), calls=%async_computation.32 | async-start | bytes 589824 | tf_op jit(solution)/shard_map/reduce_scatter | solution.py:507
  1056.7 106.2 %reduce-scatter.5.cloned.1.call-start = ((), (), s32[]{:S(2)}) async-start(), calls=%async_computation.31 | async-start | bytes 1474560 | tf_op jit(solution)/shard_map/reduce_scatter | solution.py:506
  1078.6 84.3 %all-to-all-start.16 = ((bf16[8,3,128,512]{3,2,1,0:T(8,128)(2,1)}), bf16[8,3,128,512]{3,2,1,0:T(8,128)(2,1)}, u32[]{:S(2)}, u32[]{:S(2)}) async-start(bf16[8,3,128,512]{3,2,1,0:T(8,128)(2,1)} %copy.189), calls=%async_computation.16 | async-start | bytes 6291456 | tf_op jit(solution)/shard_map/all_to_all | solution.py:187
  1175.4 53.5 %reduce-scatter.11.cloned.1.call-start = ((), (), s32[]{:S(2)}) async-start(), calls=%async_computation.34 | async-start | bytes 589824 | tf_op jit(solution)/shard_map/reduce_scatter | solution.py:507
  1216.3 45.6 %reduce-scatter.9.cloned.1.call-start = ((), (), s32[]{:S(2)}) async-start(), calls=%async_computation.33 | async-start | bytes 1474560 | tf_op jit(solution)/shard_map/reduce_scatter | solution.py:506
  (159 other events, 3634.6 us)
Sparse Core Ops, SparseCore 0:
  9.6 37.2 all-gather.11
  49.3 23.5 all-gather.25
  78.8 42.2 all-gather.13
  122.8 22.9 all-gather.15
  263.6 36.6 all-gather.27
  324.6 27.3 all-gather.17
  356.2 44.1 all-gather.19
  751.9 27.2 all-gather.21
  1048.9 27.3 all-gather.23
  1079.2 44.2 reduce-scatter.6
  1126.8 36.0 reduce-scatter.4
  1185.9 35.4 reduce-scatter.10
  1224.6 37.1 reduce-scatter.8

commit v3 on v2

--- a/solution.py
+++ b/solution.py
@@ -1,6 +1,10 @@
+import functools
+
 import jax
 import jax.numpy as jnp
 from jax import lax
+from jax.experimental import pallas as pl
+from jax.experimental.pallas import tpu as pltpu
 from jax.sharding import PartitionSpec as P
 
 D = 1024
@@ -11,6 +15,8 @@
 LAYERS = 2
 CAP = 40
 SIDE = 128
+LANES = 128
+SUBLANES = 8
 
 
 EPSILON = 1e-06
@@ -69,6 +75,128 @@
 def halves(values):
     high = lax.reduce_precision(values, 8, 7)
     return (high.astype(jnp.bfloat16), (values - high).astype(jnp.bfloat16))
+
+
+def lane_half(shape):
+    return lax.broadcasted_iota(jnp.int32, shape, 1) // HD
+
+
+def head_lanes(values, head, groups):
+    tile = values[:, head // 2 * LANES : (head // 2 + 1) * LANES]
+    wanted = head // groups
+    if head % 2 != wanted:
+        tile = pltpu.roll(tile, HD, 1)
+    return jnp.where(lane_half(tile.shape) == wanted, tile, 0.0)
+
+
+def attend_kernel(heads, groups, bounds, q_ref, kv_ref, start_ref, o_ref, lse_ref, high, total, acc):
+    rows = q_ref.shape[0]
+    scaled = q_ref[...].astype(jnp.float32) * HD ** (-0.5)
+    queries = [head_lanes(scaled, head, groups).astype(jnp.bfloat16) for head in range(heads)]
+    starts = start_ref[...]
+    spots = bounds[2] + lax.broadcasted_iota(jnp.int32, (rows, 1), 0)
+    high[...] = jnp.full(high.shape, MASKED, jnp.float32)
+    total[...] = jnp.zeros(total.shape, jnp.float32)
+    acc[...] = jnp.zeros(acc.shape, jnp.float32)
+
+    @pl.loop(bounds[0], bounds[1])
+    def _(owner):
+        first = pl.multiple_of(owner * rows, rows)
+        keys = kv_ref[pl.ds(first, rows), :LANES]
+        values = kv_ref[pl.ds(first, rows), LANES:]
+        places = first + lax.broadcasted_iota(jnp.int32, (rows, rows), 1)
+        bias = jnp.where((places >= starts) & (places <= spots), 0.0, MASKED)
+        for head in range(heads):
+            scores = contract_cols(queries[head], keys) + bias
+            old = high[head]
+            new = jnp.maximum(old, jnp.max(scores, axis=1, keepdims=True))
+            exponent = jnp.exp(scores - new)
+            factor = jnp.exp(old - new)
+            total[head] = total[head] * factor + jnp.sum(exponent, axis=1, keepdims=True)
+            acc[head] = acc[head] * factor + dot(exponent.astype(jnp.bfloat16), values)
+            high[head] = new
+
+    lanes = lax.broadcasted_iota(jnp.int32, (rows, LANES), 1)
+    logs = jnp.zeros((rows, LANES), jnp.float32)
+    for pair in range(heads // 2):
+        tile = jnp.zeros((rows, LANES), jnp.float32)
+        for head in (2 * pair, 2 * pair + 1):
+            part = acc[head] / total[head]
+            if head % 2 != head // groups:
+                part = pltpu.roll(part, HD, 1)
+            tile = jnp.where(lane_half(part.shape) == head % 2, part, tile)
+            logs = jnp.where(lanes == head, high[head] + jnp.log(total[head]), logs)
+        o_ref[:, pair * LANES : (pair + 1) * LANES] = tile.astype(jnp.bfloat16)
+    lse_ref[...] = logs.T[:SUBLANES]
+
+
+def attend_back_kernel(
+    heads,
+    groups,
+    bounds,
+    q_ref,
+    kv_ref,
+    start_ref,
+    o_ref,
+    lse_ref,
+    g_ref,
+    gq_ref,
+    gkv_ref,
+    q_sc,
+    qt_sc,
+    g_sc,
+    gt_sc,
+    acc,
+):
+    rows = q_ref.shape[0]
+    scaled = q_ref[...].astype(jnp.float32) * HD ** (-0.5)
+    grads = g_ref[...].astype(jnp.float32)
+    outs = o_ref[...].astype(jnp.float32)
+    lanes = lax.broadcasted_iota(jnp.int32, (rows, LANES), 1)
+    deltas = jnp.zeros((rows, LANES), jnp.float32)
+    for head in range(heads):
+        query = head_lanes(scaled, head, groups)
+        q_sc[head] = query.astype(jnp.bfloat16)
+        qt_sc[head] = query.T.astype(jnp.bfloat16)
+        grad = head_lanes(grads, head, groups)
+        g_sc[head] = grad.astype(jnp.bfloat16)
+        gt_sc[head] = grad.T.astype(jnp.bfloat16)
+        delta = jnp.sum(grad * head_lanes(outs, head, groups), axis=1, keepdims=True)
+        deltas = jnp.where(lanes == head, delta, deltas)
+    deltas = deltas.T
+    logs = lse_ref[...]
+    starts = start_ref[...]
+    spots = bounds[2] + lax.broadcasted_iota(jnp.int32, (1, rows), 1)
+    gkv_ref[...] = jnp.zeros(gkv_ref.shape, gkv_ref.dtype)
+    acc[...] = jnp.zeros(acc.shape, jnp.float32)
+
+    @pl.loop(bounds[0], bounds[1])
+    def _(owner):
+        first = pl.multiple_of(owner * rows, rows)
+        keys = kv_ref[pl.ds(first, rows), :LANES]
+        values = kv_ref[pl.ds(first, rows), LANES:]
+        keys_turned = keys.astype(jnp.float32).T.astype(jnp.bfloat16)
+        places = first + lax.broadcasted_iota(jnp.int32, (rows, rows), 0)
+        bias = jnp.where((places >= starts) & (places <= spots), 0.0, MASKED)
+        grad_keys = jnp.zeros((rows, LANES), jnp.float32)
+        grad_values = jnp.zeros((rows, LANES), jnp.float32)
+        for head in range(heads):
+            wanted = head // groups
+            scores = dot(keys, qt_sc[head]) + bias
+            probability = jnp.exp(scores - logs[head : head + 1])
+            grad_values += dot(probability.astype(jnp.bfloat16), g_sc[head])
+            grad_prob = dot(values, gt_sc[head])
+            grad_scores = (probability * (grad_prob - deltas[head : head + 1])).astype(
+                jnp.bfloat16
+            )
+            grad_keys += dot(grad_scores, q_sc[head])
+            acc[head * HD : (head + 1) * HD] += dot(
+                keys_turned[wanted * HD : (wanted + 1) * HD], grad_scores
+            )
+        gkv_ref[pl.ds(first, rows), :LANES] = grad_keys.astype(jnp.bfloat16)
+        gkv_ref[pl.ds(first, rows), LANES:] = grad_values.astype(jnp.bfloat16)
+
+    gq_ref[...] = (acc[...].T * HD ** (-0.5)).astype(jnp.bfloat16)
 
 
 def norm_back(stream, scale, gain, grad_normed):
@@ -116,7 +244,6 @@
     score_scale = HD ** (-0.5)
     cosine_table, sine_table = rotary_tables(query_start, block_rows, HD)
     query_segs = lax.dynamic_slice_in_dim(segments, query_start, block_rows)
-    query_pos = query_start + jnp.arange(block_rows, dtype=jnp.int32)
     block_last = segments.reshape(cycle_count, block_rows)[:, block_rows - 1]
     first_owner = jnp.sum(
         (block_last < query_segs[0]) & (jnp.arange(cycle_count) < cycle_index)
@@ -168,7 +295,6 @@
     for layer_index in range(LAYERS):
         mats = lax.all_gather(sent[:, layer_index], "blk", axis=0, tiled=False)
         attn_all.append(jnp.transpose(mats, (1, 0, 2, 3)).reshape(D, qkv_cols + SIDE))
-    out_all = lax.all_gather(w_out, "blk", axis=1, tiled=True)
     tokens_block = lax.all_gather(tokens, "head", axis=0, tiled=True).astype(jnp.float32)
 
     def exchange_experts(layer_index):
@@ -197,121 +323,74 @@
         ).reshape(head_count, local_tokens, D)
         return jnp.sum(parts.astype(jnp.float32), axis=0)
 
-    def block_mask(key_owner):
-        key_start = key_owner * block_rows
-        key_segs = lax.dynamic_slice_in_dim(segments, key_start, block_rows)
-        key_pos = key_start + jnp.arange(block_rows, dtype=jnp.int32)
-        return (query_segs[:, None] == key_segs[None, :]) & (
-            query_pos[:, None] >= key_pos[None, :]
-        )
-
-    def key_block(keys_all, key_owner):
-        chosen_rows = lax.dynamic_slice_in_dim(keys_all, key_owner * block_rows, block_rows)
-        return (
-            chosen_rows[:, :key_cols].reshape(block_rows, key_heads, HD),
-            chosen_rows[:, key_cols:].reshape(block_rows, key_heads, HD),
-        )
-
-    def block_scores(query_four, key_part, allowed):
-        scores = (
-            jnp.einsum("qcgd,kcd->cgqk", query_four, key_part, preferred_element_type=jnp.float32)
-            * score_scale
-        )
-        return jnp.where(allowed, scores, MASKED)
-
-    def attend(queries, keys_all):
-        query_four = queries.reshape(block_rows, key_heads, groups, HD)
-
-        def visit(key_owner, state_in):
-            running_max, running_sum, weighted = state_in
-            allowed = block_mask(key_owner)
-            key_part, value_part = key_block(keys_all, key_owner)
-            scores = block_scores(query_four, key_part, allowed)
-            new_max = jnp.maximum(running_max, jnp.max(scores, axis=-1))
-            exponent = jnp.where(allowed, jnp.exp(scores - new_max[..., None]), 0.0)
-            factor = jnp.exp(running_max - new_max)
-            running_sum = running_sum * factor + jnp.sum(exponent, axis=-1)
-            weighted = weighted * jnp.transpose(factor, (2, 0, 1))[..., None] + jnp.einsum(
-                "cgqk,kcd->qcgd",
-                exponent.astype(jnp.bfloat16),
-                value_part,
-                preferred_element_type=jnp.float32,
-            )
-            return (new_max, running_sum, weighted)
-
-        start_state = (
-            jnp.full((key_heads, groups, block_rows), MASKED, jnp.float32),
-            jnp.zeros((key_heads, groups, block_rows), jnp.float32),
-            jnp.zeros((block_rows, key_heads, groups, HD), jnp.float32),
-        )
-        running_max, running_sum, weighted = lax.fori_loop(
-            first_owner, cycle_index + 1, visit, start_state
-        )
-        attended = (
-            (weighted / jnp.transpose(running_sum, (2, 0, 1))[..., None])
-            .astype(jnp.bfloat16)
-            .reshape(block_rows, query_cols)
-        )
-        return (attended, running_max + jnp.log(running_sum))
-
-    def attend_back(queries, keys_all, attended, log_total, grad_attended, beside):
-        query_four = queries.reshape(block_rows, key_heads, groups, HD)
-        grad_four = grad_attended.reshape(block_rows, key_heads, groups, HD)
-        row_delta = jnp.transpose(
-            jnp.sum(
-                grad_four.astype(jnp.float32)
-                * attended.reshape(block_rows, key_heads, groups, HD).astype(jnp.float32),
-                axis=-1,
+    local_heads = H // head_count
+    bounds = jnp.stack([first_owner, cycle_index + 1, query_start]).astype(jnp.int32)
+    starts = jnp.sum(
+        (segments[None, :] < query_segs[:, None]).astype(jnp.int32), axis=1, dtype=jnp.int32
+    )
+    in_smem = pl.BlockSpec(memory_space=pltpu.SMEM)
+    in_vmem = pl.BlockSpec(memory_space=pltpu.VMEM)
+
+    def widen(keys_all):
+        parts = keys_all.reshape(-1, 2, key_cols)
+        parts = jnp.pad(parts, ((0, 0), (0, 0), (0, LANES - key_cols)))
+        return parts.reshape(-1, 2 * LANES)
+
+    def narrow(key_grads):
+        return key_grads.reshape(-1, 2, LANES)[:, :, :key_cols].reshape(-1, 2 * key_cols)
+
+    def attend(queries, keys_wide):
+        total_rows = keys_wide.shape[0]
+        return pl.pallas_call(
+            functools.partial(attend_kernel, local_heads, groups),
+            out_shape=(
+                jax.ShapeDtypeStruct((block_rows, query_cols), jnp.bfloat16),
+                jax.ShapeDtypeStruct((SUBLANES, block_rows), jnp.float32),
             ),
-            (1, 2, 0),
-        )
-
-        def visit(key_owner, state_in):
-            grad_query, key_grads = state_in
-            allowed = block_mask(key_owner)
-            key_part, value_part = key_block(keys_all, key_owner)
-            scores = block_scores(query_four, key_part, allowed)
-            probability = jnp.where(allowed, jnp.exp(scores - log_total[..., None]), 0.0)
-            grad_value = jnp.einsum(
-                "cgqk,qcgd->kcd",
-                probability.astype(jnp.bfloat16),
-                grad_four,
-                preferred_element_type=jnp.float32,
-            )
-            grad_prob = jnp.einsum(
-                "qcgd,kcd->cgqk", grad_four, value_part, preferred_element_type=jnp.float32
-            )
-            grad_scores = (probability * (grad_prob - row_delta[..., None])).astype(jnp.bfloat16)
-            grad_query = grad_query + jnp.einsum(
-                "cgqk,kcd->qcgd", grad_scores, key_part, preferred_element_type=jnp.float32
-            )
-            grad_key = (
-                jnp.einsum(
-                    "cgqk,qcgd->kcd", grad_scores, query_four, preferred_element_type=jnp.float32
-                )
-                * score_scale
-            )
-            stacked = jnp.concatenate(
-                [grad_key.reshape(block_rows, key_cols), grad_value.reshape(block_rows, key_cols)],
-                axis=1,
-            ).astype(jnp.bfloat16)
-            key_grads = lax.dynamic_update_slice_in_dim(
-                key_grads, stacked, key_owner * block_rows, 0
-            )
-            return (grad_query, key_grads)
-
-        start_state = (
-            jnp.zeros((block_rows, key_heads, groups, HD), jnp.float32),
-            jnp.zeros((cycle_count * block_rows, 2 * key_cols), jnp.bfloat16),
-        )
-        grad_query, key_grads = lax.fori_loop(first_owner, cycle_index + 1, visit, start_state)
+            in_specs=[in_smem, in_vmem, in_vmem, in_vmem],
+            out_specs=(in_vmem, in_vmem),
+            scratch_shapes=[
+                pltpu.VMEM((local_heads, block_rows, 1), jnp.float32),
+                pltpu.VMEM((local_heads, block_rows, 1), jnp.float32),
+                pltpu.VMEM((local_heads, block_rows, LANES), jnp.float32),
+            ],
+            cost_estimate=pl.CostEstimate(
+                flops=2 * block_rows * total_rows * LANES * local_heads,
+                bytes_accessed=2 * total_rows * 2 * LANES,
+                transcendentals=block_rows * total_rows * local_heads,
+            ),
+            name="attend",
+        )(bounds, queries, keys_wide, starts[:, None])
+
+    def attend_back(queries, keys_wide, attended, log_total, grad_attended, beside):
+        total_rows = keys_wide.shape[0]
+        scratch = [pltpu.VMEM((local_heads, block_rows, LANES), jnp.bfloat16)]
+        turned = [pltpu.VMEM((local_heads, LANES, block_rows), jnp.bfloat16)]
+        grad_query, key_grads = pl.pallas_call(
+            functools.partial(attend_back_kernel, local_heads, groups),
+            out_shape=(
+                jax.ShapeDtypeStruct((block_rows, query_cols), jnp.bfloat16),
+                jax.ShapeDtypeStruct((total_rows, 2 * LANES), jnp.bfloat16),
+            ),
+            in_specs=[in_smem] + [in_vmem] * 6,
+            out_specs=(in_vmem, in_vmem),
+            scratch_shapes=(scratch + turned) * 2
+            + [pltpu.VMEM((query_cols, block_rows), jnp.float32)],
+            cost_estimate=pl.CostEstimate(
+                flops=5 * block_rows * total_rows * LANES * local_heads,
+                bytes_accessed=4 * total_rows * 2 * LANES,
+                transcendentals=block_rows * total_rows * local_heads,
+            ),
+            name="attend_back",
+        )(bounds, queries, keys_wide, starts[None, :], attended, log_total, grad_attended)
         grad_query, key_grads, beside = lax.optimization_barrier((grad_query, key_grads, beside))
-        key_grads = lax.all_to_all(key_grads, "blk", split_axis=0, concat_axis=0, tiled=True)
+        key_grads = lax.all_to_all(
+            narrow(key_grads), "blk", split_axis=0, concat_axis=0, tiled=True
+        )
         key_grads = jnp.sum(
             key_grads.reshape(cycle_count, block_rows, 2 * key_cols).astype(jnp.float32), axis=0
         ).astype(jnp.bfloat16)
-        grad_query = (grad_query * score_scale).astype(jnp.bfloat16)
-        return (grad_query.reshape(block_rows, query_cols), key_grads, beside)
+        return (grad_query, key_grads, beside)
 
     stream = tokens.astype(jnp.float32)
     saved = []
@@ -321,7 +400,7 @@
         router = side_all[:, :E]
         gain_first = side_all[:, E].astype(jnp.float32)
         gain_second = side_all[:, E + 1].astype(jnp.float32)
-        out_mat = out_all[layer_index]
+        out_mat = lax.all_gather(w_out[layer_index], BOTH, axis=0, tiled=True)
         scale_first = rms_scale(stream)
         if layer_index == 0:
             normed_block = (tokens_block * rms_scale(tokens_block) * gain_first).astype(
@@ -342,13 +421,14 @@
         key_value = jnp.concatenate(
             [key_rot, qkv_pre[:, query_cols + key_cols :]], axis=1
         ).astype(jnp.bfloat16)
-        keys_all = lax.all_gather(key_value, "blk", axis=0, tiled=True)
+        keys_all = widen(lax.all_gather(key_value, "blk", axis=0, tiled=True))
         attended, log_total = attend(queries, keys_all)
         attended, expert_mats = lax.optimization_barrier(
             (attended, exchange_experts(layer_index))
         )
         gate_mat, up_mat, down_mat = expert_parts(expert_mats)
-        middle = stream + sum_over_head(dot(attended, out_mat))
+        attended_tok = lax.all_to_all(attended, "head", split_axis=0, concat_axis=1, tiled=True)
+        middle = stream + dot(attended_tok, out_mat)
         scale_second = rms_scale(middle)
         normed_ffn = (middle * scale_second * gain_second).astype(jnp.bfloat16)
         logits = lax.dot_general(
@@ -373,6 +453,7 @@
                 queries,
                 keys_all,
                 attended,
+                attended_tok,
                 log_total,
                 middle,
                 scale_second,
@@ -401,6 +482,7 @@
             queries,
             keys_all,
             attended,
+            attended_tok,
             log_total,
             middle,
             scale_second,
@@ -457,11 +539,12 @@
         )
         grad_middle, grad_gain_second = norm_back(middle, scale_second, gain_second, grad_normed)
         grad_stream = grad_stream + grad_middle
-        branch_block = lax.all_gather(
-            grad_stream.astype(jnp.bfloat16), "head", axis=0, tiled=True
-        )
-        grad_out = contract_rows(attended, branch_block)
-        grad_attended = contract_cols(branch_block, out_mat).astype(jnp.bfloat16)
+        grad_branch = grad_stream.astype(jnp.bfloat16)
+        grad_attended = contract_cols(grad_branch, out_mat).astype(jnp.bfloat16)
+        grad_attended = lax.all_to_all(
+            grad_attended, "head", split_axis=1, concat_axis=0, tiled=True
+        )
+        grad_out = contract_rows(attended_tok, grad_branch)
         grad_query, grad_kv, (expert_grads, earlier_sums) = attend_back(
             queries, keys_all, attended, log_total, grad_attended, (expert_grads, earlier_sums)
         )
@@ -505,7 +588,7 @@
         ).reshape(cycle_count * head_count * shard_rows, qkv_cols + SIDE)
         grad_mats = lax.psum_scatter(grad_mats, "blk", scatter_dimension=0, tiled=True)
         grad_out = lax.psum_scatter(
-            grad_out.astype(jnp.bfloat16), "blk", scatter_dimension=0, tiled=True
+            grad_out.astype(jnp.bfloat16), BOTH, scatter_dimension=0, tiled=True
         )
         earlier_sums = (grad_mats, grad_out)
         layer_grads[layer_index] = grad_parts(expert_grads)

time: 1300 us -> 1400 us (1.077)
  waiting for transfers between devices: 703 us -> 838 us
  Pallas kernels: 0 us -> 30.7 us
  starting transfers between devices: 101 us -> 72.7 us
    reduce_scatter x2, waiting for transfers between devices: 22.7 us -> 228 us  [per_device(): lax.psum_scatter(grad_out.astype(jnp.bfloat16), BOTH, scatter_dimension=0...]
    all_gather x5 -> x4, waiting for transfers between devices: 79.3 us -> 145 us  [the longest x2 89.2 us: per_device(): out_mat = lax.all_gather(w_out[layer_index], BOTH, axis=0, tiled=True)]
    reduce_scatter x2, waiting for transfers between devices: 60.4 us -> 0.02 us  [per_device(): lax.psum_scatter(grad_mats, 'blk', scatter_dimension=0, tiled=True)]
    all_to_all x3 -> x1, waiting for transfers between devices: 58.8 us -> 9.88 us  [sum_over_head(): lax.all_to_all(partial.astype(jnp.bfloat16), 'head', split_axis=0, concat...]
    all_to_all x4, waiting for transfers between devices: 186 us -> 154 us  [from_experts(): rows = lax.all_to_all(rows, BOTH, split_axis=0, concat_axis=0, tiled=True)]
    pallas_call x0 -> x4, Pallas kernels: none -> 30.7 us  [the longest x2 16.3 us: attend(): pl.pallas_call(functools.partial(attend_kernel, local_heads, groups), out...]
    all_to_all x2, starting transfers between devices: 26.6 us -> 7.02 us  [to_experts(): return lax.all_to_all(rows, BOTH, split_axis=0, concat_axis=0, tiled=True)]
    dot_general x14 -> x0, matrix products: 14.8 us -> none  [the longest x2 3.28 us: visit(): jnp.einsum('qcgd,kcd->cgqk', grad_four, value_part, preferred_element_typ...]
  transfers between devices with their start and end apart: 29 -> 30, of which waited for: 26 -> 24; matrix products, arithmetic and copies ran while one was open for 13% -> 10% of each run, Pallas kernels for 0% -> 2%
where the time goes in v3:
time: 1400 us; the launch traced here: 1390 us
  waiting for transfers between devices  838 us (60%)
  blocking collectives  180 us (13%)
  matrix products  128 us (9%)
  local copies, waits for them, and re-layouts  76.8 us (5%)
  starting transfers between devices  72.7 us (5%)
  other arithmetic  45.7 us (3%)
  Pallas kernels  30.7 us (2%)
  between operations  16.6 us (1%)
    reduce_scatter x2, waiting for transfers between devices, per_device(): lax.psum_scatter(grad_out.astype(jnp.bfloat16), BOTH, scatter_dimension=0...  228 us
    all_to_all x4, waiting for transfers between devices, from_experts(): rows = lax.all_to_all(rows, BOTH, split_axis=0, concat_axis=0, tiled=True)  154 us
    all_to_all x2, blocking collectives, to_experts(): return lax.all_to_all(rows, BOTH, split_axis=0, concat_axis=0, tiled=True)  130 us
    all_to_all x2, waiting for transfers between devices, to_experts(): return lax.all_to_all(rows, BOTH, split_axis=0, concat_axis=0, tiled=True)  113 us
    all_gather x2, waiting for transfers between devices, per_device(): out_mat = lax.all_gather(w_out[layer_index], BOTH, axis=0, tiled=True)  89.2 us
    all_gather x2, waiting for transfers between devices, per_device(): mats = lax.all_gather(sent[:, layer_index], 'blk', axis=0, tiled=False)  63.5 us
    all_gather x2, waiting for transfers between devices, per_device(): keys_all = widen(lax.all_gather(key_value, 'blk', axis=0, tiled=True))  55.3 us
    dot_general x17, matrix products, dot(): return jnp.dot(left, right, preferred_element_type=jnp.float32)  48.2 us
  transfers between devices with their start and end apart: 30, of which 24 were waited for; matrix products, arithmetic and copies ran while one was open for 10% of the time, Pallas kernels for 2%

profile of v3, /device:TPU:0, one launch (start us, length us, event | category | flops | bytes accessed | tf_op | source)
XLA Modules:
  0.0 1388.2 jit_solution(1462313000146185463)
XLA Ops:
  13.3 24.9 %all_to_all.232 = bf16[4,2,32,640]{3,2,1,0:T(8,128)(2,1)S(1)} all-to-all(bf16[4,2,32,640]{3,2,1,0:T(8,128)(2,1)S(1)} %copy.163), channel_id=1, replica_groups=mesh['head'=4,'blk'=8] {'head'}, dimensions={0} | all-to-all | bytes 655360 | tf_op jit(solution)/shard_map/all_to_all | solution.py:293
  48.5 24.5 %all-gather.21.cloned.1.call-done = bf16[32,1,32,640]{3,2,1,0:T(8,128)(2,1)} async-done(((bf16[4,1,32,640]{3,2,1,0:T(8,128)(2,1)}), bf16[32,1,32,640]{3,2,1,0:T(8,128)(2,1)}) %all-gather.21.cloned.1.call-update) | async-done | bytes 1310736 | tf_op jit(solution)/shard_map/all_gather | solution.py:296
  97.9 21.9 %all-gather.15.cloned.1.call-done.kv_ref = bf16[4096,256]{1,0:T(8,128)(2,1)} async-done(((bf16[512,256]{1,0:T(8,128)(2,1)}), bf16[4096,256]{1,0:T(8,128)(2,1)}) %all-gather.15.cloned.1.call-update) | async-done | bytes 2097168 | tf_op jit(solution)/shard_map/all_gather | solution.py:424
  141.1 37.8 %all-gather.23.cloned.1.call-done = bf16[1,1024,1024]{2,1,0:T(8,128)(2,1)} async-done(((bf16[1,32,1024]{2,1,0:T(8,128)(2,1)}), bf16[1,1024,1024]{2,1,0:T(8,128)(2,1)}) %all-gather.23.cloned.1.call-update) | async-done | bytes 2097168 | tf_op jit(solution)/shard_map/all_gather | solution.py:403
  191.4 56.5 %all-to-all-done.3 = bf16[32,40,1024]{2,1,0:T(8,128)(2,1)S(1)} async-done(((bf16[32,40,1024]{2,1,0:T(8,128)(2,1)}), bf16[32,40,1024]{2,1,0:T(8,128)(2,1)S(1)}, u32[]{:S(2)}, u32[]{:S(2)}) %all-to-all-start.3) | async-done | bytes 2621472 | tf_op jit(solution)/shard_map/all_to_all | solution.py:267
  262.7 39.0 %all-gather.25.cloned.1.call-done = bf16[32,1,32,640]{3,2,1,0:T(8,128)(2,1)} async-done(((bf16[4,1,32,640]{3,2,1,0:T(8,128)(2,1)}), bf16[32,1,32,640]{3,2,1,0:T(8,128)(2,1)}) %all-gather.25.cloned.1.call-update) | async-done | bytes 1310736 | tf_op jit(solution)/shard_map/all_gather | solution.py:296
  307.5 14.7 %all-to-all-done.4 = bf16[32,40,1024]{2,1,0:T(8,128)(2,1)S(1)} async-done(((bf16[32,40,1024]{2,1,0:T(8,128)(2,1)}), bf16[32,40,1024]{2,1,0:T(8,128)(2,1)S(1)}, u32[]{:S(2)}, u32[]{:S(2)}) %all-to-all-start.4) | async-done | bytes 2621472 | tf_op jit(solution)/shard_map/all_to_all | solution.py:270
  325.2 27.4 %all-gather.17.cloned.1.call-done = bf16[512,1024]{1,0:T(8,128)(2,1)} async-done(((bf16[128,1024]{1,0:T(8,128)(2,1)}), bf16[512,1024]{1,0:T(8,128)(2,1)}) %all-gather.17.cloned.1.call-update) | async-done | bytes 1048592 | tf_op jit(solution)/shard_map/all_gather | solution.py:411
  367.2 33.4 %all-gather.19.cloned.1.call-done.kv_ref = bf16[4096,256]{1,0:T(8,128)(2,1)} async-done(((bf16[512,256]{1,0:T(8,128)(2,1)}), bf16[4096,256]{1,0:T(8,128)(2,1)}) %all-gather.19.cloned.1.call-update) | async-done | bytes 2097168 | tf_op jit(solution)/shard_map/all_gather | solution.py:424
  400.6 8.2 attend.3
  417.4 51.4 %all-gather.27.cloned.1.call-done = bf16[1,1024,1024]{2,1,0:T(8,128)(2,1)} async-done(((bf16[1,32,1024]{2,1,0:T(8,128)(2,1)}), bf16[1,1024,1024]{2,1,0:T(8,128)(2,1)}) %all-gather.27.cloned.1.call-update) | async-done | bytes 2097168 | tf_op jit(solution)/shard_map/all_gather | solution.py:403
  482.2 56.5 %all-to-all-done.7 = bf16[32,40,1024]{2,1,0:T(8,128)(2,1)} async-done(((bf16[32,40,1024]{2,1,0:T(8,128)(2,1)}), bf16[32,40,1024]{2,1,0:T(8,128)(2,1)}, u32[]{:S(2)}, u32[]{:S(2)}) %all-to-all-start.7) | async-done | bytes 2621472 | tf_op jit(solution)/shard_map/all_to_all | solution.py:267
  561.2 54.7 %all-to-all-done.8 = bf16[32,40,1024]{2,1,0:T(8,128)(2,1)} async-done(((bf16[32,40,1024]{2,1,0:T(8,128)(2,1)}), bf16[32,40,1024]{2,1,0:T(8,128)(2,1)}, u32[]{:S(2)}, u32[]{:S(2)}) %all-to-all-start.8) | async-done | bytes 2621472 | tf_op jit(solution)/shard_map/all_to_all | solution.py:270
  625.1 64.4 %all_to_all.233 = bf16[32,40,1024]{2,1,0:T(8,128)(2,1)S(1)} all-to-all(bf16[32,40,1024]{2,1,0:T(8,128)(2,1)S(1)} %bitcast.306), channel_id=1, replica_groups=mesh['head'=4,'blk'=8] {'head','blk'}, dimensions={0} | all-to-all | bytes 5242880 | tf_op jit(solution)/shard_map/all_to_all | solution.py:267
  717.2 44.0 %all-to-all-done.10 = bf16[32,40,1024]{2,1,0:T(8,128)(2,1)} async-done(((bf16[32,40,1024]{2,1,0:T(8,128)(2,1)}), bf16[32,40,1024]{2,1,0:T(8,128)(2,1)}, u32[]{:S(2)}, u32[]{:S(2)}) %all-to-all-start.10) | async-done | bytes 2621472 | tf_op jit(solution)/shard_map/all_to_all | solution.py:270
  792.3 30.7 %all-to-all-done.12 = bf16[8,3,128,512]{3,2,1,0:T(8,128)(2,1)} async-done(((bf16[8,3,128,512]{3,2,1,0:T(8,128)(2,1)}), bf16[8,3,128,512]{3,2,1,0:T(8,128)(2,1)}, u32[]{:S(2)}, u32[]{:S(2)}) %all-to-all-start.12) | async-done | bytes 3145760 | tf_op jit(solution)/shard_map/all_to_all | solution.py:313
  829.3 24.7 %all-to-all-done.13 = bf16[8,512,256]{2,1,0:T(8,128)(2,1)} async-done(((bf16[8,512,256]{2,1,0:T(8,128)(2,1)}), bf16[8,512,256]{2,1,0:T(8,128)(2,1)}, u32[]{:S(2)}, u32[]{:S(2)}) %all-to-all-start.13) | async-done | bytes 2097184 | tf_op jit(solution)/shard_map/all_to_all | solution.py:387
  861.0 25.8 %all_to_all.234 = bf16[4,128,1024]{2,1,0:T(8,128)(2,1)S(1)} all-to-all(bf16[4,128,1024]{2,1,0:T(8,128)(2,1)S(1)} %bitcast.358), channel_id=1, replica_groups=mesh['head'=4,'blk'=8] {'head'}, dimensions={0} | all-to-all | bytes 2097152 | tf_op jit(solution)/shard_map/all_to_all | solution.py:321
  896.0 65.3 %all_to_all.235 = bf16[32,40,1024]{2,1,0:T(8,128)(2,1)S(1)} all-to-all(bf16[32,40,1024]{2,1,0:T(8,128)(2,1)S(1)} %bitcast.305), channel_id=1, replica_groups=mesh['head'=4,'blk'=8] {'head','blk'}, dimensions={0} | all-to-all | bytes 5242880 | tf_op jit(solution)/shard_map/all_to_all | solution.py:267
  992.6 40.2 %all-to-all-done.16 = bf16[32,40,1024]{2,1,0:T(8,128)(2,1)} async-done(((bf16[32,40,1024]{2,1,0:T(8,128)(2,1)}), bf16[32,40,1024]{2,1,0:T(8,128)(2,1)}, u32[]{:S(2)}, u32[]{:S(2)}) %all-to-all-start.16) | async-done | bytes 2621472 | tf_op jit(solution)/shard_map/all_to_all | solution.py:270
  1063.0 101.2 %reduce-scatter.7.cloned.1.call-done = bf16[32,1024]{1,0:T(8,128)(2,1)} async-done(((bf16[1024,1024]{1,0:T(8,128)(2,1)}), bf16[32,1024]{1,0:T(8,128)(2,1)}) %reduce-scatter.7.cloned.1.call-update) | async-done | bytes 65552 | tf_op jit(solution)/shard_map/reduce_scatter | solution.py:590
  1173.8 21.4 %all-to-all-done.19 = bf16[8,512,256]{2,1,0:T(8,128)(2,1)} async-done(((bf16[8,512,256]{2,1,0:T(8,128)(2,1)}), bf16[8,512,256]{2,1,0:T(8,128)(2,1)}, u32[]{:S(2)}, u32[]{:S(2)}) %all-to-all-start.19) | async-done | bytes 2097184 | tf_op jit(solution)/shard_map/all_to_all | solution.py:387
  1233.0 9.9 all-to-all-done.20
  1249.5 126.9 %reduce-scatter.11.cloned.1.call-done = bf16[32,1024]{1,0:T(8,128)(2,1)} async-done(((bf16[1024,1024]{1,0:T(8,128)(2,1)}), bf16[32,1024]{1,0:T(8,128)(2,1)}) %reduce-scatter.11.cloned.1.call-update) | async-done | bytes 65552 | tf_op jit(solution)/shard_map/reduce_scatter | solution.py:590
  (460 shorter events, 366.1 us)
Async XLA Ops:
  7.2 39.7 %all-gather.13.cloned.1.call-start = ((), (), s32[]{:S(2)}) async-start(), calls=%async_computation.26 | async-start | bytes 1310720 | tf_op jit(solution)/shard_map/all_gather | solution.py:298
  7.9 65.0 %all-gather.21.cloned.1.call-start = ((), (), s32[]{:S(2)}) async-start(), calls=%async_computation.34 | async-start | bytes 1474560 | tf_op jit(solution)/shard_map/all_gather | solution.py:296
  38.9 80.9 %all-gather.15.cloned.1.call-start = ((), (), s32[]{:S(2)}) async-start(), calls=%async_computation.27 | async-start | bytes 2359296 | tf_op jit(solution)/shard_map/all_gather | solution.py:424
  77.7 101.2 %all-gather.23.cloned.1.call-start = ((), (), s32[]{:S(2)}) async-start(), calls=%async_computation.35 | async-start | bytes 2162688 | tf_op jit(solution)/shard_map/all_gather | solution.py:403
  85.1 47.1 %all-to-all-start.1 = ((bf16[8,3,128,512]{3,2,1,0:T(8,128)(2,1)}), bf16[8,3,128,512]{3,2,1,0:T(8,128)(2,1)S(1)}, u32[]{:S(2)}, u32[]{:S(2)}) async-start(bf16[8,3,128,512]{3,2,1,0:T(8,128)(2,1)} %pad_maximum_fusion.3), calls=%async_computation.1 | async-start | bytes 6291456 | tf_op jit(solution)/shard_map/all_to_all | solution.py:303
  134.2 44.7 %all-to-all-start.2 = ((bf16[4,128,256]{1,2,0:T(8,128)(2,1)}), bf16[4,128,256]{1,2,0:T(8,128)(2,1)}, u32[]{:S(2)}, u32[]{:S(2)}) async-start(bf16[4,128,256]{1,2,0:T(8,128)(2,1)} %copy.170), calls=%async_computation.2 | async-start | bytes 524288 | tf_op jit(solution)/shard_map/all_to_all | solution.py:430
  184.3 63.5 %all-to-all-start.3 = ((bf16[32,40,1024]{2,1,0:T(8,128)(2,1)}), bf16[32,40,1024]{2,1,0:T(8,128)(2,1)S(1)}, u32[]{:S(2)}, u32[]{:S(2)}) async-start(bf16[32,40,1024]{2,1,0:T(8,128)(2,1)} %bitcast.314), calls=%async_computation.3 | async-start | bytes 5242880 | tf_op jit(solution)/shard_map/all_to_all | solution.py:267
  258.0 64.2 %all-to-all-start.4 = ((bf16[32,40,1024]{2,1,0:T(8,128)(2,1)}), bf16[32,40,1024]{2,1,0:T(8,128)(2,1)S(1)}, u32[]{:S(2)}, u32[]{:S(2)}) async-start(bf16[32,40,1024]{2,1,0:T(8,128)(2,1)} %bitcast.337), calls=%async_computation.4 | async-start | bytes 5242880 | tf_op jit(solution)/shard_map/all_to_all | solution.py:270
  262.6 90.0 %all-gather.17.cloned.1.call-start = ((), (), s32[]{:S(2)}) async-start(), calls=%async_computation.28 | async-start | bytes 1310720 | tf_op jit(solution)/shard_map/all_gather | solution.py:411
  325.1 75.5 %all-gather.19.cloned.1.call-start = ((), (), s32[]{:S(2)}) async-start(), calls=%async_computation.29 | async-start | bytes 2359296 | tf_op jit(solution)/shard_map/all_gather | solution.py:424
  357.0 111.7 %all-gather.27.cloned.1.call-start = ((), (), s32[]{:S(2)}) async-start(), calls=%async_computation.37 | async-start | bytes 2162688 | tf_op jit(solution)/shard_map/all_gather | solution.py:403
  361.6 48.2 %all-to-all-start.5 = ((bf16[8,3,128,512]{3,2,1,0:T(8,128)(2,1)}), bf16[8,3,128,512]{3,2,1,0:T(8,128)(2,1)}, u32[]{:S(2)}, u32[]{:S(2)}) async-start(bf16[8,3,128,512]{3,2,1,0:T(8,128)(2,1)} %pad_maximum_fusion.4), calls=%async_computation.5 | async-start | bytes 6291456 | tf_op jit(solution)/shard_map/all_to_all | solution.py:303
  411.6 57.2 %all-to-all-start.6 = ((bf16[4,128,256]{1,2,0:T(8,128)(2,1)}), bf16[4,128,256]{1,2,0:T(8,128)(2,1)S(1)}, u32[]{:S(2)}, u32[]{:S(2)}) async-start(bf16[4,128,256]{1,2,0:T(8,128)(2,1)} %copy.177), calls=%async_computation.6 | async-start | bytes 524288 | tf_op jit(solution)/shard_map/all_to_all | solution.py:430
  475.0 63.6 %all-to-all-start.7 = ((bf16[32,40,1024]{2,1,0:T(8,128)(2,1)}), bf16[32,40,1024]{2,1,0:T(8,128)(2,1)}, u32[]{:S(2)}, u32[]{:S(2)}) async-start(bf16[32,40,1024]{2,1,0:T(8,128)(2,1)} %bitcast.315), calls=%async_computation.7 | async-start | bytes 5242880 | tf_op jit(solution)/shard_map/all_to_all | solution.py:267
  551.4 64.4 %all-to-all-start.8 = ((bf16[32,40,1024]{2,1,0:T(8,128)(2,1)}), bf16[32,40,1024]{2,1,0:T(8,128)(2,1)}, u32[]{:S(2)}, u32[]{:S(2)}) async-start(bf16[32,40,1024]{2,1,0:T(8,128)(2,1)} %bitcast.341), calls=%async_computation.8 | async-start | bytes 5242880 | tf_op jit(solution)/shard_map/all_to_all | solution.py:270
  697.1 64.1 %all-to-all-start.10 = ((bf16[32,40,1024]{2,1,0:T(8,128)(2,1)}), bf16[32,40,1024]{2,1,0:T(8,128)(2,1)}, u32[]{:S(2)}, u32[]{:S(2)}) async-start(bf16[32,40,1024]{2,1,0:T(8,128)(2,1)} %bitcast.304), calls=%async_computation.10 | async-start | bytes 5242880 | tf_op jit(solution)/shard_map/all_to_all | solution.py:270
  780.7 42.3 %all-to-all-start.12 = ((bf16[8,3,128,512]{3,2,1,0:T(8,128)(2,1)}), bf16[8,3,128,512]{3,2,1,0:T(8,128)(2,1)}, u32[]{:S(2)}, u32[]{:S(2)}) async-start(bf16[8,3,128,512]{3,2,1,0:T(8,128)(2,1)} %copy.182), calls=%async_computation.12 | async-start | bytes 6291456 | tf_op jit(solution)/shard_map/all_to_all | solution.py:313
  968.9 63.9 %all-to-all-start.16 = ((bf16[32,40,1024]{2,1,0:T(8,128)(2,1)}), bf16[32,40,1024]{2,1,0:T(8,128)(2,1)}, u32[]{:S(2)}, u32[]{:S(2)}) async-start(bf16[32,40,1024]{2,1,0:T(8,128)(2,1)} %bitcast.88), calls=%async_computation.16 | async-start | bytes 5242880 | tf_op jit(solution)/shard_map/all_to_all | solution.py:270
  972.6 90.4 %reduce-scatter.5.cloned.1.call-start = ((), (), s32[]{:S(2)}) async-start(), calls=%async_computation.30 | async-start | bytes 1474560 | tf_op jit(solution)/shard_map/reduce_scatter | solution.py:589
  975.4 188.8 %reduce-scatter.7.cloned.1.call-start = ((), (), s32[]{:S(2)}) async-start(), calls=%async_computation.31 | async-start | bytes 2162688 | tf_op jit(solution)/shard_map/reduce_scatter | solution.py:590
  1052.2 112.0 %all-to-all-start.18 = ((bf16[8,3,128,512]{3,2,1,0:T(8,128)(2,1)}), bf16[8,3,128,512]{3,2,1,0:T(8,128)(2,1)S(1)}, u32[]{:S(2)}, u32[]{:S(2)}) async-start(bf16[8,3,128,512]{3,2,1,0:T(8,128)(2,1)} %copy.190), calls=%async_computation.18 | async-start | bytes 6291456 | tf_op jit(solution)/shard_map/all_to_all | solution.py:313
  1168.6 74.8 %reduce-scatter.9.cloned.1.call-start = ((), (), s32[]{:S(2)}) async-start(), calls=%async_computation.32 | async-start | bytes 1474560 | tf_op jit(solution)/shard_map/reduce_scatter | solution.py:589
  1202.2 174.2 %reduce-scatter.11.cloned.1.call-start = ((), (), s32[]{:S(2)}) async-start(), calls=%async_computation.33 | async-start | bytes 2162688 | tf_op jit(solution)/shard_map/reduce_scatter | solution.py:590
  1245.1 132.9 %all-to-all-start.21 = ((bf16[4,2,32,640]{3,2,1,0:T(8,128)(2,1)}), bf16[4,2,32,640]{3,2,1,0:T(8,128)(2,1)S(1)}, u32[]{:S(2)}, u32[]{:S(2)}) async-start(bf16[4,2,32,640]{3,2,1,0:T(8,128)(2,1)} %copy.200), calls=%async_computation.24 | async-start | bytes 655360 | tf_op jit(solution)/shard_map/all_to_all | solution.py:599
  (104 other events, 1850.9 us)
Sparse Core Ops, SparseCore 0:
  9.6 37.2 all-gather.12
  49.3 23.5 all-gather.20
  77.8 41.9 all-gather.14
  123.1 55.7 all-gather.22
  264.4 37.2 all-gather.24
  325.2 27.3 all-gather.16
  357.1 43.4 all-gather.18
  404.1 64.6 all-gather.26
  976.7 45.0 reduce-scatter.4
  1023.9 140.3 reduce-scatter.6
  1202.3 33.5 reduce-scatter.8
  1238.0 138.3 reduce-scatter.10

commit v4 on v3

--- a/solution.py
+++ b/solution.py
@@ -89,45 +89,47 @@
     return jnp.where(lane_half(tile.shape) == wanted, tile, 0.0)
 
 
-def attend_kernel(heads, groups, bounds, q_ref, kv_ref, start_ref, o_ref, lse_ref, high, total, acc):
+def attend_kernel(
+    heads, groups, bounds, q_ref, kv_ref, start_ref, o_ref, lse_ref, qt_sc, high, total, acc
+):
     rows = q_ref.shape[0]
     scaled = q_ref[...].astype(jnp.float32) * HD ** (-0.5)
-    queries = [head_lanes(scaled, head, groups).astype(jnp.bfloat16) for head in range(heads)]
+    for head in range(heads):
+        qt_sc[head] = head_lanes(scaled, head, groups).T.astype(jnp.bfloat16)
     starts = start_ref[...]
-    spots = bounds[2] + lax.broadcasted_iota(jnp.int32, (rows, 1), 0)
+    spots = bounds[2] + lax.broadcasted_iota(jnp.int32, (1, rows), 1)
     high[...] = jnp.full(high.shape, MASKED, jnp.float32)
-    total[...] = jnp.zeros(total.shape, jnp.float32)
+    total[...] = jnp.ones(total.shape, jnp.float32)
     acc[...] = jnp.zeros(acc.shape, jnp.float32)
 
     @pl.loop(bounds[0], bounds[1])
     def _(owner):
         first = pl.multiple_of(owner * rows, rows)
         keys = kv_ref[pl.ds(first, rows), :LANES]
-        values = kv_ref[pl.ds(first, rows), LANES:]
-        places = first + lax.broadcasted_iota(jnp.int32, (rows, rows), 1)
+        values = kv_ref[pl.ds(first, rows), LANES:].astype(jnp.float32).T.astype(jnp.bfloat16)
+        places = first + lax.broadcasted_iota(jnp.int32, (rows, rows), 0)
         bias = jnp.where((places >= starts) & (places <= spots), 0.0, MASKED)
         for head in range(heads):
-            scores = contract_cols(queries[head], keys) + bias
-            old = high[head]
-            new = jnp.maximum(old, jnp.max(scores, axis=1, keepdims=True))
+            wanted = head // groups
+            scores = dot(keys, qt_sc[head]) + bias
+            old = high[head : head + 1]
+            new = jnp.maximum(old, jnp.max(scores, axis=0, keepdims=True))
             exponent = jnp.exp(scores - new)
             factor = jnp.exp(old - new)
-            total[head] = total[head] * factor + jnp.sum(exponent, axis=1, keepdims=True)
-            acc[head] = acc[head] * factor + dot(exponent.astype(jnp.bfloat16), values)
-            high[head] = new
-
-    lanes = lax.broadcasted_iota(jnp.int32, (rows, LANES), 1)
-    logs = jnp.zeros((rows, LANES), jnp.float32)
-    for pair in range(heads // 2):
-        tile = jnp.zeros((rows, LANES), jnp.float32)
-        for head in (2 * pair, 2 * pair + 1):
-            part = acc[head] / total[head]
-            if head % 2 != head // groups:
-                part = pltpu.roll(part, HD, 1)
-            tile = jnp.where(lane_half(part.shape) == head % 2, part, tile)
-            logs = jnp.where(lanes == head, high[head] + jnp.log(total[head]), logs)
-        o_ref[:, pair * LANES : (pair + 1) * LANES] = tile.astype(jnp.bfloat16)
-    lse_ref[...] = logs.T[:SUBLANES]
+            total[head : head + 1] = total[head : head + 1] * factor + jnp.sum(
+                exponent, axis=0, keepdims=True
+            )
+            acc[head * HD : (head + 1) * HD] = acc[head * HD : (head + 1) * HD] * factor + dot(
+                values[wanted * HD : (wanted + 1) * HD], exponent.astype(jnp.bfloat16)
+            )
+            high[head : head + 1] = new
+
+    lse_ref[...] = high[...] + jnp.log(total[...])
+    for head in range(heads):
+        acc[head * HD : (head + 1) * HD] = (
+            acc[head * HD : (head + 1) * HD] / total[head : head + 1]
+        )
+    o_ref[...] = acc[...].T.astype(jnp.bfloat16)
 
 
 def attend_back_kernel(
@@ -286,15 +288,27 @@
             by_head(w_key, key_cols),
             by_head(w_value, key_cols),
             side,
+            jnp.broadcast_to(w_out[:, :, None, :], (LAYERS, shard_rows, head_count, D)),
         ],
         axis=-1,
     )
     sent = jnp.transpose(sent, (2, 0, 1, 3))
     sent = lax.all_to_all(sent, "head", split_axis=0, concat_axis=0, tiled=True)
+
+    def gather_rows(part):
+        mats = lax.all_gather(part, "blk", axis=0, tiled=False)
+        return jnp.transpose(mats, (1, 0, 2, 3)).reshape(D, part.shape[-1])
+
     attn_all = []
+    out_all = []
     for layer_index in range(LAYERS):
-        mats = lax.all_gather(sent[:, layer_index], "blk", axis=0, tiled=False)
-        attn_all.append(jnp.transpose(mats, (1, 0, 2, 3)).reshape(D, qkv_cols + SIDE))
+        if layer_index == 0:
+            attn_all.append(gather_rows(sent[:, layer_index, :, : qkv_cols + SIDE]))
+            out_all.append(gather_rows(sent[:, layer_index, :, qkv_cols + SIDE :]))
+        else:
+            mats = gather_rows(sent[:, layer_index])
+            attn_all.append(mats[:, : qkv_cols + SIDE])
+            out_all.append(mats[:, qkv_cols + SIDE :])
     tokens_block = lax.all_gather(tokens, "head", axis=0, tiled=True).astype(jnp.float32)
 
     def exchange_experts(layer_index):
@@ -350,9 +364,10 @@
             in_specs=[in_smem, in_vmem, in_vmem, in_vmem],
             out_specs=(in_vmem, in_vmem),
             scratch_shapes=[
-                pltpu.VMEM((local_heads, block_rows, 1), jnp.float32),
-                pltpu.VMEM((local_heads, block_rows, 1), jnp.float32),
-                pltpu.VMEM((local_heads, block_rows, LANES), jnp.float32),
+                pltpu.VMEM((local_heads, LANES, block_rows), jnp.bfloat16),
+                pltpu.VMEM((SUBLANES, block_rows), jnp.float32),
+                pltpu.VMEM((SUBLANES, block_rows), jnp.float32),
+                pltpu.VMEM((query_cols, block_rows), jnp.float32),
             ],
             cost_estimate=pl.CostEstimate(
                 flops=2 * block_rows * total_rows * LANES * local_heads,
@@ -360,7 +375,7 @@
                 transcendentals=block_rows * total_rows * local_heads,
             ),
             name="attend",
-        )(bounds, queries, keys_wide, starts[:, None])
+        )(bounds, queries, keys_wide, starts[None, :])
 
     def attend_back(queries, keys_wide, attended, log_total, grad_attended, beside):
         total_rows = keys_wide.shape[0]
@@ -400,7 +415,7 @@
         router = side_all[:, :E]
         gain_first = side_all[:, E].astype(jnp.float32)
         gain_second = side_all[:, E + 1].astype(jnp.float32)
-        out_mat = lax.all_gather(w_out[layer_index], BOTH, axis=0, tiled=True)
+        out_mat = out_all[layer_index]
         scale_first = rms_scale(stream)
         if layer_index == 0:
             normed_block = (tokens_block * rms_scale(tokens_block) * gain_first).astype(
@@ -453,7 +468,6 @@
                 queries,
                 keys_all,
                 attended,
-                attended_tok,
                 log_total,
                 middle,
                 scale_second,
@@ -482,7 +496,6 @@
             queries,
             keys_all,
             attended,
-            attended_tok,
             log_total,
             middle,
             scale_second,
@@ -500,6 +513,10 @@
         spread = dot(picks_mat, grad_high) + dot(picks_mat, grad_low)
         row_gate = jnp.sum(gate_rows, axis=1, keepdims=True)
         grad_result = to_experts((spread * row_gate).astype(jnp.bfloat16))
+        if earlier_sums:
+            grad_result, out_grads[layer_index + 1] = lax.optimization_barrier(
+                (grad_result, earlier_sums[1])
+            )
         row_choice = contract_cols(returned, grad_high) + contract_cols(returned, grad_low)
         grad_choice = jnp.sum(
             jnp.where(picks, row_choice.reshape(E, CAP, local_tokens), 0.0), axis=1
@@ -514,6 +531,10 @@
             contract_cols(grad_gate_pre, gate_mat) + contract_cols(grad_up_pre, up_mat)
         ).astype(jnp.bfloat16)
         grad_rows = from_experts(grad_arrived)
+        if earlier_sums:
+            grad_rows, mats_grads[layer_index + 1] = lax.optimization_barrier(
+                (grad_rows, earlier_sums[0])
+            )
         expert_grads = exchange_grads(
             [
                 contract_rows(arrived, grad_gate_pre),
@@ -544,12 +565,11 @@
         grad_attended = lax.all_to_all(
             grad_attended, "head", split_axis=1, concat_axis=0, tiled=True
         )
-        grad_out = contract_rows(attended_tok, grad_branch)
-        grad_query, grad_kv, (expert_grads, earlier_sums) = attend_back(
-            queries, keys_all, attended, log_total, grad_attended, (expert_grads, earlier_sums)
-        )
-        if earlier_sums:
-            mats_grads[layer_index + 1], out_grads[layer_index + 1] = earlier_sums
+        branch_block = lax.all_gather(grad_branch, "head", axis=0, tiled=True)
+        grad_query, grad_kv, (expert_grads, branch_block) = attend_back(
+            queries, keys_all, attended, log_total, grad_attended, (expert_grads, branch_block)
+        )
+        grad_out = contract_rows(attended, branch_block)
         grad_query_pre = (
             rotate(
                 grad_query.reshape(block_rows, H // head_count, HD).astype(jnp.float32),
@@ -588,7 +608,7 @@
         ).reshape(cycle_count * head_count * shard_rows, qkv_cols + SIDE)
         grad_mats = lax.psum_scatter(grad_mats, "blk", scatter_dimension=0, tiled=True)
         grad_out = lax.psum_scatter(
-            grad_out.astype(jnp.bfloat16), BOTH, scatter_dimension=0, tiled=True
+            grad_out.astype(jnp.bfloat16), "blk", scatter_dimension=0, tiled=True
         )
         earlier_sums = (grad_mats, grad_out)
         layer_grads[layer_index] = grad_parts(expert_grads)

time: 1400 us -> 1200 us (0.86)
  waiting for transfers between devices: 838 us -> 649 us
  blocking collectives: 180 us -> 135 us
  starting transfers between devices: 72.7 us -> 89.6 us
    reduce_scatter x2, waiting for transfers between devices: 228 us -> 38.5 us  [per_device(): lax.psum_scatter(grad_out.astype(jnp.bfloat16), 'blk', scatter_dimension=...]
    all_gather x4 -> x5, waiting for transfers between devices: 153 us -> 29.1 us  [the longest x3 29.1 us: gather_rows(): mats = lax.all_gather(part, 'blk', axis=0, tiled=False)]
    all_to_all x2 -> x1, blocking collectives: 130 us -> 64.6 us  [to_experts(): return lax.all_to_all(rows, BOTH, split_axis=0, concat_axis=0, tiled=True)]
    reduce_scatter x2, waiting for transfers between devices: 0.02 us -> 64.4 us  [per_device(): lax.psum_scatter(grad_mats, 'blk', scatter_dimension=0, tiled=True)]
    all_to_all x2, waiting for transfers between devices: 30.7 us -> 59.7 us  [exchange_grads(): return lax.all_to_all(grads, 'blk', split_axis=0, concat_axis=0, tiled=True)]
    all_to_all x1, blocking collectives: 24.9 us -> 44.5 us  [per_device(): sent = lax.all_to_all(sent, 'head', split_axis=0, concat_axis=0, tiled=True)]
    all_to_all x2 -> x3, waiting for transfers between devices: 113 us -> 131 us  [to_experts(): return lax.all_to_all(rows, BOTH, split_axis=0, concat_axis=0, tiled=True)]
    all_to_all x2 -> x3, starting transfers between devices: 7.02 us -> 21.6 us  [to_experts(): return lax.all_to_all(rows, BOTH, split_axis=0, concat_axis=0, tiled=True)]
  transfers between devices with their start and end apart: 30 -> 32, of which waited for: 24 -> 26; matrix products, arithmetic and copies ran while one was open for 10% -> 13% of each run, Pallas kernels for 2% -> 2%
where the time goes in v4:
time: 1200 us; the launch traced here: 1180 us
  waiting for transfers between devices  649 us (54%)
  matrix products  138 us (12%)
  blocking collectives  135 us (11%)
  starting transfers between devices  89.6 us (7%)
  local copies, waits for them, and re-layouts  81 us (7%)
  other arithmetic  51 us (4%)
  Pallas kernels  24.5 us (2%)
  between operations  16.1 us (1%)
    all_to_all x4, waiting for transfers between devices, from_experts(): rows = lax.all_to_all(rows, BOTH, split_axis=0, concat_axis=0, tiled=True)  162 us
    all_to_all x3, waiting for transfers between devices, to_experts(): return lax.all_to_all(rows, BOTH, split_axis=0, concat_axis=0, tiled=True)  131 us
    all_to_all x1, blocking collectives, to_experts(): return lax.all_to_all(rows, BOTH, split_axis=0, concat_axis=0, tiled=True)  64.6 us
    reduce_scatter x2, waiting for transfers between devices, per_device(): lax.psum_scatter(grad_mats, 'blk', scatter_dimension=0, tiled=True)  64.4 us
    all_to_all x2, waiting for transfers between devices, exchange_grads(): return lax.all_to_all(grads, 'blk', split_axis=0, concat_axis=0, tiled=True)  59.7 us
    dot_general x17, matrix products, dot(): return jnp.dot(left, right, preferred_element_type=jnp.float32)  57.2 us
    all_gather x2, waiting for transfers between devices, per_device(): keys_all = widen(lax.all_gather(key_value, 'blk', axis=0, tiled=True))  54.9 us
    all_to_all x1, blocking collectives, per_device(): sent = lax.all_to_all(sent, 'head', split_axis=0, concat_axis=0, tiled=True)  44.5 us
  transfers between devices with their start and end apart: 32, of which 26 were waited for; matrix products, arithmetic and copies ran while one was open for 13% of the time, Pallas kernels for 2%

profile of v4, /device:TPU:0, one launch (start us, length us, event | category | flops | bytes accessed | tf_op | source)
XLA Modules:
  0.0 1183.3 jit_solution(6310453125477259930)
XLA Ops:
  13.1 44.5 %all_to_all.235 = bf16[4,2,32,1664]{3,2,1,0:T(8,128)(2,1)S(1)} all-to-all(bf16[4,2,32,1664]{3,2,1,0:T(8,128)(2,1)S(1)} %bitcast.345), channel_id=1, replica_groups=mesh['head'=4,'blk'=8] {'head'}, dimensions={0} | all-to-all | bytes 1703936 | tf_op jit(solution)/shard_map/all_to_all | solution.py:296
  60.4 23.2 %all-gather.25.cloned.1.call-done = bf16[32,1,32,640]{3,2,1,0:T(8,128)(2,1)} async-done(((bf16[4,1,32,640]{3,2,1,0:T(8,128)(2,1)}), bf16[32,1,32,640]{3,2,1,0:T(8,128)(2,1)}) %all-gather.25.cloned.1.call-update) | async-done | bytes 1310736 | tf_op jit(solution)/shard_map/all_gather | solution.py:299
  111.6 20.1 %all-gather.15.cloned.1.call-done.kv_ref = bf16[4096,256]{1,0:T(8,128)(2,1)} async-done(((bf16[512,256]{1,0:T(8,128)(2,1)}), bf16[4096,256]{1,0:T(8,128)(2,1)}) %all-gather.15.cloned.1.call-update) | async-done | bytes 2097168 | tf_op jit(solution)/shard_map/all_gather | solution.py:439
  136.8 12.1 %all-to-all-done.1 = bf16[8,3,128,512]{3,2,1,0:T(8,128)(2,1)S(1)} async-done(((bf16[8,3,128,512]{3,2,1,0:T(8,128)(2,1)}), bf16[8,3,128,512]{3,2,1,0:T(8,128)(2,1)S(1)}, u32[]{:S(2)}, u32[]{:S(2)}) %all-to-all-start.1) | async-done | bytes 3145760 | tf_op jit(solution)/shard_map/all_to_all | solution.py:317
  178.4 56.3 %all-to-all-done.3 = bf16[32,40,1024]{2,1,0:T(8,128)(2,1)} async-done(((bf16[32,40,1024]{2,1,0:T(8,128)(2,1)}), bf16[32,40,1024]{2,1,0:T(8,128)(2,1)}, u32[]{:S(2)}, u32[]{:S(2)}) %all-to-all-start.3) | async-done | bytes 2621472 | tf_op jit(solution)/shard_map/all_to_all | solution.py:269
  258.9 52.7 %all-to-all-done.4 = bf16[32,40,1024]{2,1,0:T(8,128)(2,1)S(1)} async-done(((bf16[32,40,1024]{2,1,0:T(8,128)(2,1)}), bf16[32,40,1024]{2,1,0:T(8,128)(2,1)S(1)}, u32[]{:S(2)}, u32[]{:S(2)}) %all-to-all-start.4) | async-done | bytes 2621472 | tf_op jit(solution)/shard_map/all_to_all | solution.py:272
  314.6 27.5 %all-gather.17.cloned.1.call-done = bf16[512,1024]{1,0:T(8,128)(2,1)} async-done(((bf16[128,1024]{1,0:T(8,128)(2,1)}), bf16[512,1024]{1,0:T(8,128)(2,1)}) %all-gather.17.cloned.1.call-update) | async-done | bytes 1048592 | tf_op jit(solution)/shard_map/all_gather | solution.py:426
  356.1 34.7 %all-gather.19.cloned.1.call-done.kv_ref = bf16[4096,256]{1,0:T(8,128)(2,1)} async-done(((bf16[512,256]{1,0:T(8,128)(2,1)}), bf16[4096,256]{1,0:T(8,128)(2,1)}) %all-gather.19.cloned.1.call-update) | async-done | bytes 2097168 | tf_op jit(solution)/shard_map/all_gather | solution.py:439
  420.4 12.0 %all-to-all-start.7 = ((bf16[32,40,1024]{2,1,0:T(8,128)(2,1)}), bf16[32,40,1024]{2,1,0:T(8,128)(2,1)}, u32[]{:S(2)}, u32[]{:S(2)}) async-start(bf16[32,40,1024]{2,1,0:T(8,128)(2,1)} %bitcast.312), calls=%async_computation.7 | async-start | bytes 5242880 | tf_op jit(solution)/shard_map/all_to_all | solution.py:269
  436.0 56.5 %all-to-all-done.7 = bf16[32,40,1024]{2,1,0:T(8,128)(2,1)} async-done(((bf16[32,40,1024]{2,1,0:T(8,128)(2,1)}), bf16[32,40,1024]{2,1,0:T(8,128)(2,1)}, u32[]{:S(2)}, u32[]{:S(2)}) %all-to-all-start.7) | async-done | bytes 2621472 | tf_op jit(solution)/shard_map/all_to_all | solution.py:269
  514.8 54.6 %all-to-all-done.8 = bf16[32,40,1024]{2,1,0:T(8,128)(2,1)} async-done(((bf16[32,40,1024]{2,1,0:T(8,128)(2,1)}), bf16[32,40,1024]{2,1,0:T(8,128)(2,1)}, u32[]{:S(2)}, u32[]{:S(2)}) %all-to-all-start.8) | async-done | bytes 2621472 | tf_op jit(solution)/shard_map/all_to_all | solution.py:272
  578.6 64.6 %all_to_all.236 = bf16[32,40,1024]{2,1,0:T(8,128)(2,1)S(1)} all-to-all(bf16[32,40,1024]{2,1,0:T(8,128)(2,1)S(1)} %bitcast.308), channel_id=1, replica_groups=mesh['head'=4,'blk'=8] {'head','blk'}, dimensions={0} | all-to-all | bytes 5242880 | tf_op jit(solution)/shard_map/all_to_all | solution.py:269
  670.5 44.0 %all-to-all-done.10 = bf16[32,40,1024]{2,1,0:T(8,128)(2,1)} async-done(((bf16[32,40,1024]{2,1,0:T(8,128)(2,1)}), bf16[32,40,1024]{2,1,0:T(8,128)(2,1)}, u32[]{:S(2)}, u32[]{:S(2)}) %all-to-all-start.10) | async-done | bytes 2621472 | tf_op jit(solution)/shard_map/all_to_all | solution.py:272
  749.6 29.8 %all-to-all-done.12 = bf16[8,3,128,512]{3,2,1,0:T(8,128)(2,1)} async-done(((bf16[8,3,128,512]{3,2,1,0:T(8,128)(2,1)}), bf16[8,3,128,512]{3,2,1,0:T(8,128)(2,1)}, u32[]{:S(2)}, u32[]{:S(2)}) %all-to-all-start.12) | async-done | bytes 3145760 | tf_op jit(solution)/shard_map/all_to_all | solution.py:327
  787.5 22.9 %all-to-all-done.13 = bf16[8,512,256]{2,1,0:T(8,128)(2,1)} async-done(((bf16[8,512,256]{2,1,0:T(8,128)(2,1)}), bf16[8,512,256]{2,1,0:T(8,128)(2,1)}, u32[]{:S(2)}, u32[]{:S(2)}) %all-to-all-start.13) | async-done | bytes 2097184 | tf_op jit(solution)/shard_map/all_to_all | solution.py:402
  823.9 25.6 %all_to_all.237 = bf16[4,128,1024]{2,1,0:T(8,128)(2,1)S(1)} all-to-all(bf16[4,128,1024]{2,1,0:T(8,128)(2,1)S(1)} %bitcast.355), channel_id=1, replica_groups=mesh['head'=4,'blk'=8] {'head'}, dimensions={0} | all-to-all | bytes 2097152 | tf_op jit(solution)/shard_map/all_to_all | solution.py:335
  868.6 38.5 %reduce-scatter.5.cloned.1.call-done = bf16[32,1024]{1,0:T(8,128)(2,1)} async-done(((bf16[256,1024]{1,0:T(8,128)(2,1)}), bf16[32,1024]{1,0:T(8,128)(2,1)}) %reduce-scatter.5.cloned.1.call-update) | async-done | bytes 65552 | tf_op jit(solution)/shard_map/reduce_scatter | solution.py:610
  907.1 18.5 %all-to-all-done.15 = bf16[32,40,1024]{2,1,0:T(8,128)(2,1)S(1)} async-done(((bf16[32,40,1024]{2,1,0:T(8,128)(2,1)}), bf16[32,40,1024]{2,1,0:T(8,128)(2,1)S(1)}, u32[]{:S(2)}, u32[]{:S(2)}) %all-to-all-start.15) | async-done | bytes 2621472 | tf_op jit(solution)/shard_map/all_to_all | solution.py:269
  956.3 34.0 %reduce-scatter.7.cloned.1.call-done = bf16[128,640]{1,0:T(8,128)(2,1)} async-done(((bf16[1024,640]{1,0:T(8,128)(2,1)}), bf16[128,640]{1,0:T(8,128)(2,1)}) %reduce-scatter.7.cloned.1.call-update) | async-done | bytes 163856 | tf_op jit(solution)/shard_map/reduce_scatter | solution.py:609
  990.4 10.9 all-to-all-done.16
  1035.3 29.9 %all-to-all-done.18 = bf16[8,3,128,512]{3,2,1,0:T(8,128)(2,1)} async-done(((bf16[8,3,128,512]{3,2,1,0:T(8,128)(2,1)}), bf16[8,3,128,512]{3,2,1,0:T(8,128)(2,1)}, u32[]{:S(2)}, u32[]{:S(2)}) %all-to-all-start.18) | async-done | bytes 3145760 | tf_op jit(solution)/shard_map/all_to_all | solution.py:327
  1083.2 12.2 %all-to-all-done.19 = bf16[8,512,256]{2,1,0:T(8,128)(2,1)S(1)} async-done(((bf16[8,512,256]{2,1,0:T(8,128)(2,1)}), bf16[8,512,256]{2,1,0:T(8,128)(2,1)S(1)}, u32[]{:S(2)}, u32[]{:S(2)}) %all-to-all-start.19) | async-done | bytes 2097184 | tf_op jit(solution)/shard_map/all_to_all | solution.py:402
  1126.9 30.4 %reduce-scatter.9.cloned.1.call-done = bf16[128,640]{1,0:T(8,128)(2,1)} async-done(((bf16[1024,640]{1,0:T(8,128)(2,1)}), bf16[128,640]{1,0:T(8,128)(2,1)}) %reduce-scatter.9.cloned.1.call-update) | async-done | bytes 163856 | tf_op jit(solution)/shard_map/reduce_scatter | solution.py:609
  1164.6 9.0 all-to-all-done.21
  (481 shorter events, 402.6 us)
Async XLA Ops:
  7.2 51.6 %all-gather.13.cloned.1.call-start = ((), (), s32[]{:S(2)}) async-start(), calls=%async_computation.26 | async-start | bytes 1310720 | tf_op jit(solution)/shard_map/all_gather | solution.py:312
  7.9 75.6 %all-gather.25.cloned.1.call-start = ((), (), s32[]{:S(2)}) async-start(), calls=%async_computation.36 | async-start | bytes 1474560 | tf_op jit(solution)/shard_map/all_gather | solution.py:299
  58.4 73.4 %all-gather.15.cloned.1.call-start = ((), (), s32[]{:S(2)}) async-start(), calls=%async_computation.27 | async-start | bytes 2359296 | tf_op jit(solution)/shard_map/all_gather | solution.py:439
  89.7 73.4 %all-gather.27.cloned.1.call-start = ((), (), s32[]{:S(2)}) async-start(), calls=%async_computation.37 | async-start | bytes 2359296 | tf_op jit(solution)/shard_map/all_gather | solution.py:299
  99.1 49.7 %all-to-all-start.1 = ((bf16[8,3,128,512]{3,2,1,0:T(8,128)(2,1)}), bf16[8,3,128,512]{3,2,1,0:T(8,128)(2,1)S(1)}, u32[]{:S(2)}, u32[]{:S(2)}) async-start(bf16[8,3,128,512]{3,2,1,0:T(8,128)(2,1)} %pad_maximum_fusion.3), calls=%async_computation.1 | async-start | bytes 6291456 | tf_op jit(solution)/shard_map/all_to_all | solution.py:317
  169.9 64.9 %all-to-all-start.3 = ((bf16[32,40,1024]{2,1,0:T(8,128)(2,1)}), bf16[32,40,1024]{2,1,0:T(8,128)(2,1)}, u32[]{:S(2)}, u32[]{:S(2)}) async-start(bf16[32,40,1024]{2,1,0:T(8,128)(2,1)} %bitcast.311), calls=%async_computation.3 | async-start | bytes 5242880 | tf_op jit(solution)/shard_map/all_to_all | solution.py:269
  174.6 77.0 %all-gather.29.cloned.1.call-start = ((), (), s32[]{:S(2)}) async-start(), calls=%async_computation.38 | async-start | bytes 3833856 | tf_op jit(solution)/shard_map/all_gather | solution.py:299
  247.5 64.1 %all-to-all-start.4 = ((bf16[32,40,1024]{2,1,0:T(8,128)(2,1)}), bf16[32,40,1024]{2,1,0:T(8,128)(2,1)S(1)}, u32[]{:S(2)}, u32[]{:S(2)}) async-start(bf16[32,40,1024]{2,1,0:T(8,128)(2,1)} %bitcast.333), calls=%async_computation.4 | async-start | bytes 5242880 | tf_op jit(solution)/shard_map/all_to_all | solution.py:272
  251.6 90.6 %all-gather.17.cloned.1.call-start = ((), (), s32[]{:S(2)}) async-start(), calls=%async_computation.28 | async-start | bytes 1310720 | tf_op jit(solution)/shard_map/all_gather | solution.py:426
  314.6 76.2 %all-gather.19.cloned.1.call-start = ((), (), s32[]{:S(2)}) async-start(), calls=%async_computation.29 | async-start | bytes 2359296 | tf_op jit(solution)/shard_map/all_gather | solution.py:439
  350.4 48.9 %all-to-all-start.5 = ((bf16[8,3,128,512]{3,2,1,0:T(8,128)(2,1)}), bf16[8,3,128,512]{3,2,1,0:T(8,128)(2,1)}, u32[]{:S(2)}, u32[]{:S(2)}) async-start(bf16[8,3,128,512]{3,2,1,0:T(8,128)(2,1)} %pad_maximum_fusion.4), calls=%async_computation.5 | async-start | bytes 6291456 | tf_op jit(solution)/shard_map/all_to_all | solution.py:317
  420.4 72.0 %all-to-all-start.7 = ((bf16[32,40,1024]{2,1,0:T(8,128)(2,1)}), bf16[32,40,1024]{2,1,0:T(8,128)(2,1)}, u32[]{:S(2)}, u32[]{:S(2)}) async-start(bf16[32,40,1024]{2,1,0:T(8,128)(2,1)} %bitcast.312), calls=%async_computation.7 | async-start | bytes 5242880 | tf_op jit(solution)/shard_map/all_to_all | solution.py:269
  505.2 64.2 %all-to-all-start.8 = ((bf16[32,40,1024]{2,1,0:T(8,128)(2,1)}), bf16[32,40,1024]{2,1,0:T(8,128)(2,1)}, u32[]{:S(2)}, u32[]{:S(2)}) async-start(bf16[32,40,1024]{2,1,0:T(8,128)(2,1)} %bitcast.334), calls=%async_computation.8 | async-start | bytes 5242880 | tf_op jit(solution)/shard_map/all_to_all | solution.py:272
  650.8 63.7 %all-to-all-start.10 = ((bf16[32,40,1024]{2,1,0:T(8,128)(2,1)}), bf16[32,40,1024]{2,1,0:T(8,128)(2,1)}, u32[]{:S(2)}, u32[]{:S(2)}) async-start(bf16[32,40,1024]{2,1,0:T(8,128)(2,1)} %bitcast.307), calls=%async_computation.10 | async-start | bytes 5242880 | tf_op jit(solution)/shard_map/all_to_all | solution.py:272
  737.0 42.3 %all-to-all-start.12 = ((bf16[8,3,128,512]{3,2,1,0:T(8,128)(2,1)}), bf16[8,3,128,512]{3,2,1,0:T(8,128)(2,1)}, u32[]{:S(2)}, u32[]{:S(2)}) async-start(bf16[8,3,128,512]{3,2,1,0:T(8,128)(2,1)} %copy.224), calls=%async_computation.12 | async-start | bytes 6291456 | tf_op jit(solution)/shard_map/all_to_all | solution.py:327
  741.5 37.9 %all-gather.21.cloned.1.call-start = ((), (), s32[]{:S(2)}) async-start(), calls=%async_computation.30 | async-start | bytes 1310720 | tf_op jit(solution)/shard_map/all_gather | solution.py:568
  860.6 65.0 %all-to-all-start.15 = ((bf16[32,40,1024]{2,1,0:T(8,128)(2,1)}), bf16[32,40,1024]{2,1,0:T(8,128)(2,1)S(1)}, u32[]{:S(2)}, u32[]{:S(2)}) async-start(bf16[32,40,1024]{2,1,0:T(8,128)(2,1)} %bitcast.86), calls=%async_computation.15 | async-start | bytes 5242880 | tf_op jit(solution)/shard_map/all_to_all | solution.py:269
  865.5 41.6 %reduce-scatter.5.cloned.1.call-start = ((), (), s32[]{:S(2)}) async-start(), calls=%async_computation.31 | async-start | bytes 589824 | tf_op jit(solution)/shard_map/reduce_scatter | solution.py:610
  936.9 64.3 %all-to-all-start.16 = ((bf16[32,40,1024]{2,1,0:T(8,128)(2,1)}), bf16[32,40,1024]{2,1,0:T(8,128)(2,1)}, u32[]{:S(2)}, u32[]{:S(2)}) async-start(bf16[32,40,1024]{2,1,0:T(8,128)(2,1)} %bitcast.88), calls=%async_computation.17 | async-start | bytes 5242880 | tf_op jit(solution)/shard_map/all_to_all | solution.py:272
  941.1 49.2 %reduce-scatter.7.cloned.1.call-start = ((), (), s32[]{:S(2)}) async-start(), calls=%async_computation.32 | async-start | bytes 1474560 | tf_op jit(solution)/shard_map/reduce_scatter | solution.py:609
  1022.7 42.5 %all-to-all-start.18 = ((bf16[8,3,128,512]{3,2,1,0:T(8,128)(2,1)}), bf16[8,3,128,512]{3,2,1,0:T(8,128)(2,1)}, u32[]{:S(2)}, u32[]{:S(2)}) async-start(bf16[8,3,128,512]{3,2,1,0:T(8,128)(2,1)} %copy.234), calls=%async_computation.20 | async-start | bytes 6291456 | tf_op jit(solution)/shard_map/all_to_all | solution.py:327
  1027.4 37.9 %all-gather.23.cloned.1.call-start = ((), (), s32[]{:S(2)}) async-start(), calls=%async_computation.33 | async-start | bytes 1310720 | tf_op jit(solution)/shard_map/all_gather | solution.py:568
  1068.8 49.5 %reduce-scatter.11.cloned.1.call-start = ((), (), s32[]{:S(2)}) async-start(), calls=%async_computation.35 | async-start | bytes 589824 | tf_op jit(solution)/shard_map/reduce_scatter | solution.py:610
  1103.4 53.9 %reduce-scatter.9.cloned.1.call-start = ((), (), s32[]{:S(2)}) async-start(), calls=%async_computation.34 | async-start | bytes 1474560 | tf_op jit(solution)/shard_map/reduce_scatter | solution.py:609
  (115 other events, 4191.9 us)
Sparse Core Ops, SparseCore 0:
  9.6 47.9 all-gather.12
  60.1 23.4 all-gather.24
  89.8 41.9 all-gather.14
  134.1 28.8 all-gather.26
  177.6 47.1 all-gather.28
  314.7 27.4 all-gather.16
  346.7 44.0 all-gather.18
  743.9 27.4 all-gather.20
  870.0 37.0 reduce-scatter.4
  945.3 44.9 reduce-scatter.6
  1029.7 27.4 all-gather.22
  1083.2 33.5 reduce-scatter.10
  1120.0 37.2 reduce-scatter.8
